TPU v7x, 128 devices: a whole 4x4x4 slice. The times are simulated.
128 devices in a mesh: dp: 32 (over x, z, y_lo), mp: 4 (over y_hi, core).
Axes of the slice: x: 4, y: 4 (y_hi: 2, y_lo: 2; y = y_hi * 2 + y_lo), z: 4, core: 2. Of those that a mesh axis runs over, the one named last changes fastest.
Arguments:
- inputs: bfloat16 [12288, 8192], P('dp', 'mp'), may hold values from -6 to 6
- gate_preact: bfloat16 [12288, 28672], P('dp', 'mp'), may hold values from -6 to 6
- hidden_grad: bfloat16 [12288, 28672], P('dp', 'mp'), may hold values from -0.109375 to 0.109375
- projector: bfloat16 [8192, 512], P('mp'), may hold values from -0.0625 to 0.0625
- first_moment: float32 [28672, 512], P(('mp', 'dp')), may hold values from -0.6 to 0.6
- second_moment: float32 [28672, 512], P(('mp', 'dp')), may hold values from 0.01 to 0.1
Outputs:
- new_first: float32 [28672, 512], P(('mp', 'dp'))
- new_second: float32 [28672, 512], P(('mp', 'dp'))
- weight_update: bfloat16 [28672, 8192], P(('mp', 'dp'))
All inputs are finite; a program needn't handle non-finite values.
Results may differ from a plain program's by a relative error of at most 0.0058.
Values may be sent and summed in bfloat16 or wider, within the bound.
No kernel may reach another device: no remote copies, remote signals or barrier semaphores. Data moves between devices by JAX's collectives and lax.ppermute only.
A program may use at most 128 MiB of HBM per device.

v0:
```python
import jax
import jax.numpy as jnp
from jax import lax
from jax.sharding import PartitionSpec as P


def local(inputs, gate_preact, hidden_grad, projector, first_moment, second_moment):
    grad_up = (
        hidden_grad.astype(jnp.float32) * jax.nn.silu(gate_preact.astype(jnp.float32))
    ).astype(jnp.bfloat16)
    full_proj = lax.all_gather(projector, "mp", axis=0, tiled=True)
    coord_sum = jnp.dot(
        lax.all_gather(inputs, "mp", axis=1, tiled=True),
        full_proj,
        preferred_element_type=jnp.float32,
    )
    coords = coord_sum.astype(jnp.bfloat16)
    projected = lax.psum_scatter(
        lax.dot_general(
            grad_up, coords, (((0,), (0,)), ((), ())), preferred_element_type=jnp.float32
        ),
        "dp",
        scatter_dimension=0,
        tiled=True,
    )
    new_first = 0.9 * first_moment + 0.1 * projected
    new_second = 0.95 * second_moment + 0.05 * projected * projected
    direction = new_first / (1.0 - 0.81) / (jnp.sqrt(new_second / (1.0 - 0.9025)) + 1e-08)
    direction = direction.astype(jnp.bfloat16)
    update = 4.0 * lax.dot_general(
        direction, full_proj, (((1,), (1,)), ((), ())), preferred_element_type=jnp.float32
    )
    return (new_first, new_second, update.astype(jnp.bfloat16))


def solution(mesh):
    return jax.shard_map(
        local,
        mesh=mesh,
        in_specs=(
            P("dp", "mp"),
            P("dp", "mp"),
            P("dp", "mp"),
            P("mp", None),
            P(("mp", "dp"), None),
            P(("mp", "dp"), None),
        ),
        out_specs=(P(("mp", "dp"), None), P(("mp", "dp"), None), P(("mp", "dp"), None)),
        check_vma=False,
    )
```

profile of v0, /device:TPU:74, one launch (start us, length us, event | category | flops | bytes accessed | tf_op | source)
XLA Modules:
  0.0 480.9 jit_solution(11658029528777716738)
XLA Ops:
  7.2 0.0 all-gather.3.cloned.1.call-start
  7.2 0.7 all-gather.3.cloned.1.call-update
  7.9 0.0 all-gather.5.cloned.1.call-start
  7.9 0.7 all-gather.5.cloned.1.call-update
  8.6 0.0 reduce-scatter.2.cloned.1.call-start
  8.7 52.0 %all-gather.3.cloned.1.call-done = bf16[384,8192]{1,0:T(8,128)(2,1)} async-done(((bf16[384,2048]{1,0:T(8,128)(2,1)}), bf16[384,8192]{1,0:T(8,128)(2,1)}) %all-gather.3.cloned.1.call-update) | async-done | bytes 6291472 | tf_op jit(solution)/shard_map/all_gather | solution.py:13
  60.7 63.4 %all-gather.5.cloned.1.call-done = bf16[8192,512]{1,0:T(8,128)(2,1)} async-done(((bf16[2048,512]{1,0:T(8,128)(2,1)}), bf16[8192,512]{1,0:T(8,128)(2,1)}) %all-gather.5.cloned.1.call-update) | async-done | bytes 8388624 | tf_op jit(solution)/shard_map/all_gather | solution.py:11
  124.1 21.4 %fusion.6 = f32[7168,512]{1,0:T(8,128)} fusion(bf16[384,7168]{1,0:T(8,128)(2,1)} %param.7, bf16[384,7168]{1,0:T(8,128)(2,1)} %param.8, bf16[384,8192]{1,0:T(8,128)(2,1)} %all-gather.3.cloned.1.call-done, bf16[8192,512]{1,0:T(8,128)(2,1)} %all-gather.5.cloned.1.call-done), kind=kOutput, calls=%fused_computation.9 | convolution fusion | flops 6062014464 | bytes 40370176 | tf_op jit(solution)/shard_map/dot_general | solution.py:19
  145.5 0.0 copy-start
  145.5 0.0 copy-start.1
  145.5 0.0 reduce-scatter.2.cloned.1.call-update
  145.5 319.3 %reduce-scatter.2.cloned.1.call-done = f32[224,512]{1,0:T(8,128)} async-done(((f32[7168,512]{1,0:T(8,128)}), f32[224,512]{1,0:T(8,128)}) %reduce-scatter.2.cloned.1.call-update) | async-done | bytes 458768 | tf_op jit(solution)/shard_map/reduce_scatter | solution.py:18
  464.8 0.0 copy-done
  464.8 0.0 copy-done.1
  464.8 1.2 fusion.8
  466.0 0.0 copy-start.2
  466.0 0.0 copy-start.3
  466.0 8.3 %fusion.5 = bf16[224,8192]{1,0:T(8,128)(2,1)} fusion(bf16[8192,512]{1,0:T(8,128)(2,1)} %all-gather.5.cloned.1.call-done, f32[224,512]{1,0:T(8,128)S(1)} %get-tuple-element.3, f32[224,512]{1,0:T(8,128)S(1)} %get-tuple-element.4), kind=kOutput, calls=%fused_computation.8 | convolution fusion | flops 1883291648 | bytes 12976128 | tf_op jit(solution)/shard_map/dot_general | solution.py:30
  474.3 0.0 copy-done.2
  474.3 0.0 copy-done.3
Async XLA Ops:
  7.2 53.6 %all-gather.3.cloned.1.call-start = ((), (), s32[]{:S(2)}) async-start(), calls=%async_computation.1 | async-start | bytes 7864320 | tf_op jit(solution)/shard_map/all_gather | solution.py:13
  7.9 116.2 %all-gather.5.cloned.1.call-start = ((), (), s32[]{:S(2)}) async-start(), calls=%async_computation.2 | async-start | bytes 10485760 | tf_op jit(solution)/shard_map/all_gather | solution.py:11
  8.6 456.1 %reduce-scatter.2.cloned.1.call-start = ((), (), s32[]{:S(2)}) async-start(), calls=%async_computation.3 | async-start | bytes 15138816 | tf_op jit(solution)/shard_map/reduce_scatter | solution.py:18
  145.5 319.3 %copy-start = (f32[224,512]{1,0:T(8,128)S(1)}, f32[224,512]{1,0:T(8,128)}, u32[]{:S(2)}) copy-start(f32[224,512]{1,0:T(8,128)} %param.11) | copy-start | bytes 1376260
  145.5 319.3 %copy-start.1 = (f32[224,512]{1,0:T(8,128)S(1)}, f32[224,512]{1,0:T(8,128)}, u32[]{:S(2)}) copy-start(f32[224,512]{1,0:T(8,128)} %param.10) | copy-start | bytes 1376260
  466.0 8.4 %copy-start.2 = (f32[224,512]{1,0:T(8,128)}, f32[224,512]{1,0:T(8,128)S(1)}, u32[]{:S(2)}) copy-start(f32[224,512]{1,0:T(8,128)S(1)} %get-tuple-element.3) | copy-start | bytes 1376260
  466.0 8.3 %copy-start.3 = (f32[224,512]{1,0:T(8,128)}, f32[224,512]{1,0:T(8,128)S(1)}, u32[]{:S(2)}) copy-start(f32[224,512]{1,0:T(8,128)S(1)} %get-tuple-element.4) | copy-start | bytes 1376260
Sparse Core Ops, SparseCore 0:
  9.6 51.0 all-gather.2
  62.4 61.6 all-gather.4
  145.6 319.0 reduce-scatter.1
where the time goes:
time: 481 us
  waiting for transfers between devices  436 us (91%)
  matrix products  29.7 us (6%)
  between operations  13.8 us (3%)
    reduce_scatter x1, waiting for transfers between devices, local(): lax.psum_scatter(lax.dot_general(grad_up, coords, (((0,), (0,)), ((), ())...  319 us
    all_gather x1, waiting for transfers between devices, local(): full_proj = lax.all_gather(projector, 'mp', axis=0, tiled=True)  63.4 us
    all_gather x1, waiting for transfers between devices, local(): lax.all_gather(inputs, 'mp', axis=1, tiled=True)  52 us
    dot_general x1, matrix products, local(): lax.dot_general(grad_up, coords, (((0,), (0,)), ((), ())), preferred_elem...  21.4 us
  transfers between devices with their start and end apart: 3, of which 3 were waited for; matrix products, arithmetic and copies ran while one was open for 0% of the time, Pallas kernels for 0%

commit v1 on v0

v1 whole, which is shorter than its diff:
```python
import jax
import jax.numpy as jnp
from jax import lax
from jax.experimental import pallas as pl
from jax.experimental.pallas import tpu as pltpu
from jax.sharding import Mesh, PartitionSpec as P


F32 = jnp.float32
BF16 = jnp.bfloat16
SIZE = {"x": 4, "z": 4, "yl": 2, "yh": 2, "c": 2}
VMEM_LIMIT = 56 * 1024 * 1024


def shift(a, axis, k):
    n = SIZE[axis]
    return lax.ppermute(a, axis, [(i, (i + k) % n) for i in range(n)])


def coords_kernel(s_ref, x_ref, w_ref, mine_ref, theirs_ref):
    c = s_ref[0]
    for out, half in ((mine_ref, c), (theirs_ref, 1 - c)):
        start = pl.multiple_of(half * 256, 256)
        out[...] = jnp.dot(x_ref[...], w_ref[:, pl.ds(start, 256)], preferred_element_type=F32)


def partial_coords(c, x, w):
    t = x.shape[0]
    return pl.pallas_call(
        coords_kernel,
        in_specs=[
            pl.BlockSpec(memory_space=pltpu.SMEM),
            pl.BlockSpec(memory_space=pltpu.VMEM),
            pl.BlockSpec(memory_space=pltpu.VMEM),
        ],
        out_shape=[jax.ShapeDtypeStruct((t, 256), F32)] * 2,
        compiler_params=pltpu.CompilerParams(vmem_limit_bytes=VMEM_LIMIT),
        name="coords",
    )(c.reshape(1), x, w)


def grad_kernel(s_ref, g_ref, h_ref, *rest):
    to_x, to_z, t_ref = rest[:4], rest[4:8], rest[8]
    i = pl.program_id(0)
    xp = lax.rem(s_ref[0] + i, 4)

    @pl.loop(0, 14)
    def _(b):
        cols = pl.ds(pl.multiple_of(b * 128, 128), 128)
        v = g_ref[:, cols].astype(F32)
        h = h_ref[:, cols].astype(F32)
        u = (h * (v / (1.0 + jnp.exp(-v)))).astype(BF16)
        t_ref[cols, :] = u.T

    for j in range(4):

        @pl.when(i == j)
        def _():
            for q in range(4):
                to_x[j][q] = t_ref[q * 448 : q * 448 + 224, :]

    for k in range(4):
        start = pl.multiple_of(lax.rem(s_ref[1] + k, 4) * 448 + 224, 224)
        to_z[k][xp] = t_ref[pl.ds(start, 224), :]


def grad_pieces(xz, gate, hidden):
    t = gate.shape[0]
    spec = pl.BlockSpec((t, 1792), lambda i, s: (0, lax.rem(s[0] + i, 4)))
    return pl.pallas_call(
        grad_kernel,
        grid_spec=pltpu.PrefetchScalarGridSpec(
            num_scalar_prefetch=1,
            grid=(4,),
            in_specs=[spec, spec],
            out_specs=[pl.BlockSpec((4, 224, t), lambda i, s: (0, 0, 0))] * 8,
            scratch_shapes=[pltpu.VMEM((1792, t), BF16)],
        ),
        out_shape=[jax.ShapeDtypeStruct((4, 224, t), BF16)] * 8,
        compiler_params=pltpu.CompilerParams(vmem_limit_bytes=VMEM_LIMIT),
        name="grads",
    )(xz, gate, hidden)


def matmul_kernel(picks, s_ref, g0, g1, g2, g3, own_ref, other_ref, o0, o1, o2, o3):
    for k, out in enumerate((o0, o1, o2, o3)):
        q = lax.rem(s_ref[0] + k, 4)
        for half, cref in enumerate((own_ref, other_ref)):
            acc = jnp.zeros((224, 256), F32)
            for g, p in zip((g0, g1, g2, g3), picks):
                acc += jnp.dot(g[q], cref[p], preferred_element_type=F32)
            out[:, half * 256 : half * 256 + 256] = acc.astype(out.dtype)


def partial_sums(picks, at, pieces, own, other):
    return pl.pallas_call(
        lambda *refs: matmul_kernel(picks, *refs),
        in_specs=[pl.BlockSpec(memory_space=pltpu.SMEM)]
        + [pl.BlockSpec(memory_space=pltpu.VMEM)] * 6,
        out_shape=[jax.ShapeDtypeStruct((224, 512), F32)]
        + [jax.ShapeDtypeStruct((224, 512), BF16)] * 3,
        compiler_params=pltpu.CompilerParams(vmem_limit_bytes=VMEM_LIMIT),
        name="matmul",
    )(at.reshape(1), *pieces, own, other)


def step(inputs, gate_preact, hidden_grad, projector, first_moment, second_moment):
    x, z, yl, yh, c = (lax.axis_index(a).astype(jnp.int32) for a in ("x", "z", "yl", "yh", "c"))

    mine, theirs = partial_coords(c, inputs, projector)
    theirs = shift(theirs, "c", 1)
    pieces = grad_pieces(jnp.stack([x, z]), gate_preact, hidden_grad)
    theirs, pieces = lax.optimization_barrier((theirs, pieces))
    from_x = [pieces[0]] + [shift(pieces[k], "x", k) for k in (1, 2, 3)]
    from_z = [pieces[4]] + [shift(pieces[4 + k], "z", k) for k in (1, 2, 3)]

    chip_sum = mine + theirs
    far = shift(chip_sum.astype(BF16), "yh", 1)
    half = (chip_sum + far.astype(F32)).astype(BF16)
    own = jnp.stack(
        [half]
        + [shift(half, "x", k) for k in (1, 2, 3)]
        + [shift(half, "z", k) for k in (1, 2, 3)]
    )
    other = shift(own, "c", 1)

    beside_w = shift(projector, "c", 1)
    near_w = lax.ppermute(projector, ("yl", "yh"), [(0, 3), (3, 0), (1, 2), (2, 1)])
    across_w = shift(near_w, "c", 1)
    full_proj = jnp.zeros((4, 2048, 512), BF16)
    for at, block in (
        (2 * yh + c, projector),
        (2 * yh + 1 - c, beside_w),
        (2 - 2 * yh + c, near_w),
        (3 - 2 * yh - c, across_w),
    ):
        full_proj = lax.dynamic_update_slice(full_proj, block[None], (at, 0, 0))
    full_proj = full_proj.reshape(8192, 512)

    part_x = partial_sums((0, 1, 2, 3), z, from_x, own, other)
    part_z = partial_sums((0, 4, 5, 6), x, from_z, own, other)
    sum_x = part_x[0]
    sum_z = part_z[0]
    for k in (1, 2, 3):
        sum_x += shift(part_x[k], "z", k).astype(F32)
        sum_z += shift(part_z[k], "x", k).astype(F32)
    keep = jnp.where(yl == 0, sum_x, sum_z)
    give = jnp.where(yl == 0, sum_z, sum_x).astype(BF16)
    total = keep + shift(give, "yl", 1).astype(F32)
    swapped = jnp.concatenate([total[:, 256:], total[:, :256]], axis=1)
    projected = jnp.where(c == 0, total, swapped)

    new_first = 0.9 * first_moment + 0.1 * projected
    new_second = 0.95 * second_moment + 0.05 * projected * projected
    direction = new_first / (1.0 - 0.81) / (jnp.sqrt(new_second / (1.0 - 0.9025)) + 1e-08)
    direction = direction.astype(BF16)
    update = 4.0 * lax.dot_general(
        direction, full_proj, (((1,), (1,)), ((), ())), preferred_element_type=F32
    )
    return (new_first, new_second, update.astype(BF16))


def solution(mesh):
    fine = Mesh(mesh.devices.reshape(4, 4, 2, 2, 2), ("x", "z", "yl", "yh", "c"))
    dp, mp = ("x", "z", "yl"), ("yh", "c")
    return jax.shard_map(
        step,
        mesh=fine,
        in_specs=(P(dp, mp), P(dp, mp), P(dp, mp), P(mp, None), P(mp + dp, None), P(mp + dp, None)),
        out_specs=(P(mp + dp, None),) * 3,
        check_vma=False,
    )
```

time: 481 us -> 171 us (0.36)
  the two profiles are of different devices: /device:TPU:74 before, /device:TPU:0 now
where the time goes in v1:
time: 171 us; the launch traced here: 170 us
  waiting for transfers between devices  74.1 us (43%)
  starting transfers between devices  44 us (26%)
  Pallas kernels  27.6 us (16%)
  local copies, waits for them, and re-layouts  14.5 us (8%)
  matrix products  7.99 us (5%)
    ppermute x24, waiting for transfers between devices, shift(): return lax.ppermute(a, axis, [(i, (i + k) % n) for i in range(n)])  74.1 us
    ppermute x24, starting transfers between devices, shift(): return lax.ppermute(a, axis, [(i, (i + k) % n) for i in range(n)])  41 us
    pallas_call x1, Pallas kernels, grad_pieces(): pl.pallas_call(grad_kernel, grid_spec=pltpu.PrefetchScalarGridSpec(num_sc...  13 us
    pallas_call x2, Pallas kernels, partial_sums(): pl.pallas_call(lambda *refs: matmul_kernel(picks, *refs), in_specs=[pl.Bl...  10.7 us
    dynamic_update_slice x4, local copies, waits for them, and re-layouts, step(): full_proj = lax.dynamic_update_slice(full_proj, block[None], (at, 0, 0))  9.29 us
    dot_general x1, matrix products, step(): lax.dot_general(direction, full_proj, (((1,), (1,)), ((), ())), preferred...  7.99 us
    pallas_call x1, Pallas kernels, partial_coords(): pl.pallas_call(coords_kernel, in_specs=[pl.BlockSpec(memory_space=pltpu.S...  3.94 us
    broadcast_in_dim x1, local copies, waits for them, and re-layouts, step(): full_proj = jnp.zeros((4, 2048, 512), BF16)  3.94 us
  transfers between devices with their start and end apart: 25, of which 13 were waited for; matrix products, arithmetic and copies ran while one was open for 8% of the time, Pallas kernels for 14%

profile of v1, /device:TPU:0, one launch (start us, length us, event | category | flops | bytes accessed | tf_op | source)
XLA Modules:
  0.0 170.5 jit_solution(14482556666583638323)
XLA Ops:
  0.6 3.9 %coords.1 = (f32[384,256]{1,0:T(8,128)}, f32[384,256]{1,0:T(8,128)}) custom-call(s32[1]{0:T(128)} %bitcast.1.s_ref, bf16[384,2048]{1,0:T(8,128)(2,1)} %x_ref.1, bf16[2048,512]{1,0:T(8,128)(2,1)} %w_ref.1), custom_call_target="tpu_custom_call" | custom-call | tf_op jit(solution)/shard_map/coords/pallas_call | solution.py:29
  5.2 13.0 %grads.1 = (bf16[4,224,384]{2,1,0:T(8,128)(2,1)}, bf16[4,224,384]{2,1,0:T(8,128)(2,1)}, bf16[4,224,384]{2,1,0:T(8,128)(2,1)}, bf16[4,224,384]{2,1,0:T(8,128)(2,1...) custom-call(s32[2]{0:T(128)} %pad_add_fusion.s_ref, ...), custom_call_target="tpu_custom_call" | custom-call | tf_op jit(solution)/shard_map/grads/pallas_call | solution.py:70
  18.3 3.4 %collective-permute-start.4 = (bf16[384,256]{1,0:T(8,128)(2,1)S(1)}, bf16[384,256]{1,0:T(8,128)(2,1)S(1)}, u32[]{:S(2)}, u32[]{:S(2)}) collective-permute-start(bf16[384,256]{1,0:T(8,128)(2,1)S(1)} %get-tuple-element.59), channel_id=1, source_target_pairs={{0,2},{2,0},{1,3},{3,1},{4,6},{6,4},{5,7},{7,5},{8,10},{10,8},{9,1... | collective-permute-start | bytes 589832 | tf_op jit(solution)/shard_map/ppermute | solution.py:17
  21.6 5.6 %collective-permute-done.4 = bf16[384,256]{1,0:T(8,128)(2,1)S(1)} collective-permute-done((bf16[384,256]{1,0:T(8,128)(2,1)S(1)}, bf16[384,256]{1,0:T(8,128)(2,1)S(1)}, u32[]{:S(2)}, u32[]{:S(2)}) %collective-permute-start.4) | collective-permute-done | bytes 196640 | tf_op jit(solution)/shard_map/ppermute | solution.py:17
  28.9 3.0 %collective-permute-start.23 = (bf16[2048,512]{1,0:T(8,128)(2,1)S(1)}, bf16[2048,512]{1,0:T(8,128)(2,1)}, u32[]{:S(2)}, u32[]{:S(2)}) collective-permute-start(bf16[2048,512]{1,0:T(8,128)(2,1)S(1)} %copy-done), channel_id=1, source_target_pairs={{0,6},{6,0},{2,4},{4,2},{1,7},{7,1},{3,5},{5,3},{8,14},{14,8},{10,... | collective-permute-start | bytes 6291464 | tf_op jit(solution)/shard_map/ppermute | solution.py:128
  33.8 2.7 %collective-permute-start.6 = (bf16[384,256]{1,0:T(8,128)(2,1)S(1)}, bf16[384,256]{1,0:T(8,128)(2,1)S(1)}, u32[]{:S(2)}, u32[]{:S(2)}) collective-permute-start(bf16[384,256]{1,0:T(8,128)(2,1)S(1)} %get-tuple-element.58), channel_id=1, source_target_pairs={{0,64},{32,96},{64,0},{96,32},{1,65},{33,97},{65,1},{97,33},{2,66}... | collective-permute-start | bytes 589832 | tf_op jit(solution)/shard_map/ppermute | solution.py:17
  38.0 4.1 %collective-permute-done.6 = bf16[384,256]{1,0:T(8,128)(2,1)S(1)} collective-permute-done((bf16[384,256]{1,0:T(8,128)(2,1)S(1)}, bf16[384,256]{1,0:T(8,128)(2,1)S(1)}, u32[]{:S(2)}, u32[]{:S(2)}) %collective-permute-start.6) | collective-permute-done | bytes 196640 | tf_op jit(solution)/shard_map/ppermute | solution.py:17
  45.4 3.6 %collective-permute-start.9 = (bf16[384,256]{1,0:T(8,128)(2,1)S(1)}, bf16[384,256]{1,0:T(8,128)(2,1)S(1)}, u32[]{:S(2)}, u32[]{:S(2)}) collective-permute-start(bf16[384,256]{1,0:T(8,128)(2,1)S(1)} %get-tuple-element.58), channel_id=1, source_target_pairs={{0,16},{8,24},{16,0},{24,8},{1,17},{9,25},{17,1},{25,9},{2,18},{10... | collective-permute-start | bytes 589832 | tf_op jit(solution)/shard_map/ppermute | solution.py:17
  49.0 7.2 %collective-permute-done.8 = bf16[384,256]{1,0:T(8,128)(2,1)S(1)} collective-permute-done((bf16[384,256]{1,0:T(8,128)(2,1)S(1)}, bf16[384,256]{1,0:T(8,128)(2,1)S(1)}, u32[]{:S(2)}, u32[]{:S(2)}) %collective-permute-start.8) | collective-permute-done | bytes 196640 | tf_op jit(solution)/shard_map/ppermute | solution.py:17
  58.7 2.9 %collective-permute-done.9 = bf16[384,256]{1,0:T(8,128)(2,1)S(1)} collective-permute-done((bf16[384,256]{1,0:T(8,128)(2,1)S(1)}, bf16[384,256]{1,0:T(8,128)(2,1)S(1)}, u32[]{:S(2)}, u32[]{:S(2)}) %collective-permute-start.9) | collective-permute-done | bytes 196640 | tf_op jit(solution)/shard_map/ppermute | solution.py:17
  63.3 4.6 %collective-permute-start.16 = (bf16[4,224,384]{2,1,0:T(8,128)(2,1)S(1)}, bf16[4,224,384]{2,1,0:T(8,128)(2,1)S(1)}, u32[]{:S(2)}, u32[]{:S(2)}) collective-permute-start(bf16[4,224,384]{2,1,0:T(8,128)(2,1)S(1)} %copy-done.14), channel_id=1, source_target_pairs={{0,16},{8,24},{16,0},{24,8},{1,17},{9,25},{17,1},{25,9},{2,18},{10... | collective-permute-start | bytes 2064392 | tf_op jit(solution)/shard_map/ppermute | solution.py:17
  68.5 15.3 %collective-permute-done.16.refs_3_ = bf16[4,224,384]{2,1,0:T(8,128)(2,1)S(1)} collective-permute-done((bf16[4,224,384]{2,1,0:T(8,128)(2,1)S(1)}, bf16[4,224,384]{2,1,0:T(8,128)(2,1)S(1)}, u32[]{:S(2)}, u32[]{:S(2)}) %collective-permute-start.16) | collective-permute-done | bytes 688160 | tf_op jit(solution)/shard_map/ppermute | solution.py:17
  85.4 12.0 %collective-permute-done.17.refs_4_ = bf16[4,224,384]{2,1,0:T(8,128)(2,1)S(1)} collective-permute-done((bf16[4,224,384]{2,1,0:T(8,128)(2,1)S(1)}, bf16[4,224,384]{2,1,0:T(8,128)(2,1)S(1)}, u32[]{:S(2)}, u32[]{:S(2)}) %collective-permute-start.17) | collective-permute-done | bytes 688160 | tf_op jit(solution)/shard_map/ppermute | solution.py:17
  97.3 2.7 %collective-permute-start.2 = (bf16[4,224,384]{2,1,0:T(8,128)(2,1)}, bf16[4,224,384]{2,1,0:T(8,128)(2,1)}, u32[]{:S(2)}, u32[]{:S(2)}) collective-permute-start(bf16[4,224,384]{2,1,0:T(8,128)(2,1)} %get-tuple-element.41), channel_id=1, source_target_pairs={{0,64},{32,96},{64,0},{96,32},{1,65},{33,97},{65,1},{97,33},{2,66}... | collective-permute-start | bytes 2064392 | tf_op jit(solution)/shard_map/ppermute | solution.py:17
  102.6 5.4 %matmul.3 = (f32[224,512]{1,0:T(8,128)}, bf16[224,512]{1,0:T(8,128)(2,1)}, bf16[224,512]{1,0:T(8,128)(2,1)}, bf16[224,512]{1,0:T(8,128)(2,1)}) custom-call(s32[1]{0:T(128)} %bitcast.2.refs_0_, bf16[4,224,384]{2,1,0:T(8,128)(2,1)} %get-tuple-element.49.refs_1_, bf16[4,224,384]{2,1,0:T(8,128)(2,1)} %copy-done.5, bf16[4,224,384]{2,1,0:T(8,128)(2,1)} %copy-done.6, ...), custom_call_target="tpu_custom_call" | custom-call | tf_op jit(solution)/shard_map/matmul/pallas_call | solution.py:96
  108.5 9.9 %collective-permute-done.2.refs_3_ = bf16[4,224,384]{2,1,0:T(8,128)(2,1)} collective-permute-done((bf16[4,224,384]{2,1,0:T(8,128)(2,1)}, bf16[4,224,384]{2,1,0:T(8,128)(2,1)}, u32[]{:S(2)}, u32[]{:S(2)}) %collective-permute-start.2) | collective-permute-done | bytes 688160 | tf_op jit(solution)/shard_map/ppermute | solution.py:17
  120.2 3.9 %broadcast_in_dim.15 = bf16[4,2048,512]{2,1,0:T(8,128)(2,1)} broadcast(bf16[]{:T(256)} %constant.42.clone.1), dimensions={} | broadcast | bytes 8388610 | tf_op jit(solution)/shard_map/broadcast_in_dim | solution.py:130
  125.6 5.7 %collective-permute-done.3.refs_4_ = bf16[4,224,384]{2,1,0:T(8,128)(2,1)} collective-permute-done((bf16[4,224,384]{2,1,0:T(8,128)(2,1)}, bf16[4,224,384]{2,1,0:T(8,128)(2,1)}, u32[]{:S(2)}, u32[]{:S(2)}) %collective-permute-start.3) | collective-permute-done | bytes 688160 | tf_op jit(solution)/shard_map/ppermute | solution.py:17
  133.9 5.4 %matmul.2 = (f32[224,512]{1,0:T(8,128)}, bf16[224,512]{1,0:T(8,128)(2,1)}, bf16[224,512]{1,0:T(8,128)(2,1)}, bf16[224,512]{1,0:T(8,128)(2,1)}) custom-call(s32[1]{0:T(128)} %bitcast.refs_0_, bf16[4,224,384]{2,1,0:T(8,128)(2,1)} %get-tuple-element.39.refs_1_, bf16[4,224,384]{2,1,0:T(8,128)(2,1)} %collective-permute-done.1.refs_2_, ...), custom_call_target="tpu_custom_call" | custom-call | tf_op jit(solution)/shard_map/matmul/pallas_call | solution.py:96
  145.0 3.1 %bitcast_dynamic-update-slice_fusion.2 = bf16[4,2048,512]{2,1,0:T(8,128)(2,1)} fusion(bf16[4,2048,512]{2,1,0:T(8,128)(2,1)} %bitcast_dynamic-update-slice_fusion.3, s32[]{:T(128)S(6)} %select_n.36, bf16[2048,512]{1,0:T(8,128)(2,1)} %collective-permute-done.22), kind=kLoop, calls=%fused_computation.4 | loop fusion | bytes 4194308 | tf_op jit(solution)/shard_map/dynamic_update_slice | solution.py:137
  148.3 5.3 %collective-permute-done.13 = bf16[224,512]{1,0:T(8,128)(2,1)S(1)} collective-permute-done((bf16[224,512]{1,0:T(8,128)(2,1)}, bf16[224,512]{1,0:T(8,128)(2,1)S(1)}, u32[]{:S(2)}, u32[]{:S(2)}) %collective-permute-start.13) | collective-permute-done | bytes 229408 | tf_op jit(solution)/shard_map/ppermute | solution.py:17
  154.1 3.1 %bitcast_dynamic-update-slice_fusion.1 = bf16[4,2048,512]{2,1,0:T(8,128)(2,1)} fusion(bf16[4,2048,512]{2,1,0:T(8,128)(2,1)} %bitcast_dynamic-update-slice_fusion.2, s32[]{:T(128)S(6)} %select_n.37, bf16[2048,512]{1,0:T(8,128)(2,1)} %collective-permute-done.23), kind=kLoop, calls=%fused_computation.3 | loop fusion | bytes 4194308 | tf_op jit(solution)/shard_map/dynamic_update_slice | solution.py:137
  157.2 3.1 %collective-permute-done.21 = bf16[224,512]{1,0:T(8,128)(2,1)S(1)} collective-permute-done((bf16[224,512]{1,0:T(8,128)(2,1)S(1)}, bf16[224,512]{1,0:T(8,128)(2,1)S(1)}, u32[]{:S(2)}, u32[]{:S(2)}) %collective-permute-start.21) | collective-permute-done | bytes 229408 | tf_op jit(solution)/shard_map/ppermute | solution.py:17
  162.5 8.0 %fusion = bf16[224,8192]{1,0:T(8,128)(2,1)} fusion(bf16[8192,512]{1,0:T(8,128)(2,1)} %bitcast.14, f32[224,512]{1,0:T(8,128)S(1)} %get-tuple-element.61, f32[224,512]{1,0:T(8,128)S(1)} %get-tuple-element.62), kind=kOutput, calls=%fused_computation.1 | convolution fusion | flops 1883291648 | bytes 12976128 | tf_op jit(solution)/shard_map/dot_general | solution.py:157
  (81 shorter events, 32.9 us)
Async XLA Ops:
  4.6 13.6 %collective-permute-start = (f32[384,256]{1,0:T(8,128)}, f32[384,256]{1,0:T(8,128)S(1)}, u32[]{:S(2)}, u32[]{:S(2)}) collective-permute-start(f32[384,256]{1,0:T(8,128)} %get-tuple-element.30), channel_id=1, source_target_pairs={{0,1},{1,0},{2,3},{3,2},{4,5},{5,4},{6,7},{7,6},{8,9},{9,8},{10,11... | collective-permute-start | bytes 1179656 | tf_op jit(solution)/shard_map/ppermute | solution.py:17
  18.3 9.0 %collective-permute-start.4 = (bf16[384,256]{1,0:T(8,128)(2,1)S(1)}, bf16[384,256]{1,0:T(8,128)(2,1)S(1)}, u32[]{:S(2)}, u32[]{:S(2)}) collective-permute-start(bf16[384,256]{1,0:T(8,128)(2,1)S(1)} %get-tuple-element.59), channel_id=1, source_target_pairs={{0,2},{2,0},{1,3},{3,1},{4,6},{6,4},{5,7},{7,5},{8,10},{10,8},{9,1... | collective-permute-start | bytes 589832 | tf_op jit(solution)/shard_map/ppermute | solution.py:17
  27.3 9.3 %collective-permute-start.5 = (bf16[384,256]{1,0:T(8,128)(2,1)S(1)}, bf16[384,256]{1,0:T(8,128)(2,1)S(1)}, u32[]{:S(2)}, u32[]{:S(2)}) collective-permute-start(bf16[384,256]{1,0:T(8,128)(2,1)S(1)} %get-tuple-element.58), channel_id=1, source_target_pairs={{0,32},{32,64},{64,96},{96,0},{1,33},{33,65},{65,97},{97,1},{2,34}... | collective-permute-start | bytes 589832 | tf_op jit(solution)/shard_map/ppermute | solution.py:17
  28.9 110.4 %collective-permute-start.22 = (bf16[2048,512]{1,0:T(8,128)(2,1)S(1)}, bf16[2048,512]{1,0:T(8,128)(2,1)}, u32[]{:S(2)}, u32[]{:S(2)}) collective-permute-start(bf16[2048,512]{1,0:T(8,128)(2,1)S(1)} %copy-done), channel_id=1, source_target_pairs={{0,1},{1,0},{2,3},{3,2},{4,5},{5,4},{6,7},{7,6},{8,9},{9,8},{10,11... | collective-permute-start | bytes 6291464 | tf_op jit(solution)/shard_map/ppermute | solution.py:17
  28.9 96.8 %collective-permute-start.23 = (bf16[2048,512]{1,0:T(8,128)(2,1)S(1)}, bf16[2048,512]{1,0:T(8,128)(2,1)}, u32[]{:S(2)}, u32[]{:S(2)}) collective-permute-start(bf16[2048,512]{1,0:T(8,128)(2,1)S(1)} %copy-done), channel_id=1, source_target_pairs={{0,6},{6,0},{2,4},{4,2},{1,7},{7,1},{3,5},{5,3},{8,14},{14,8},{10,... | collective-permute-start | bytes 6291464 | tf_op jit(solution)/shard_map/ppermute | solution.py:128
  31.9 36.0 %collective-permute-start.15 = (bf16[4,224,384]{2,1,0:T(8,128)(2,1)}, bf16[4,224,384]{2,1,0:T(8,128)(2,1)S(1)}, u32[]{:S(2)}, u32[]{:S(2)}) collective-permute-start(bf16[4,224,384]{2,1,0:T(8,128)(2,1)} %get-tuple-element.50), channel_id=1, source_target_pairs={{0,8},{8,16},{16,24},{24,0},{1,9},{9,17},{17,25},{25,1},{2,10},{10... | collective-permute-start | bytes 2064392 | tf_op jit(solution)/shard_map/ppermute | solution.py:17
  33.8 8.3 %collective-permute-start.6 = (bf16[384,256]{1,0:T(8,128)(2,1)S(1)}, bf16[384,256]{1,0:T(8,128)(2,1)S(1)}, u32[]{:S(2)}, u32[]{:S(2)}) collective-permute-start(bf16[384,256]{1,0:T(8,128)(2,1)S(1)} %get-tuple-element.58), channel_id=1, source_target_pairs={{0,64},{32,96},{64,0},{96,32},{1,65},{33,97},{65,1},{97,33},{2,66}... | collective-permute-start | bytes 589832 | tf_op jit(solution)/shard_map/ppermute | solution.py:17
  36.5 8.8 %collective-permute-start.7 = (bf16[384,256]{1,0:T(8,128)(2,1)S(1)}, bf16[384,256]{1,0:T(8,128)(2,1)S(1)}, u32[]{:S(2)}, u32[]{:S(2)}) collective-permute-start(bf16[384,256]{1,0:T(8,128)(2,1)S(1)} %get-tuple-element.58), channel_id=1, source_target_pairs={{0,96},{32,0},{64,32},{96,64},{1,97},{33,1},{65,33},{97,65},{2,98}... | collective-permute-start | bytes 589832 | tf_op jit(solution)/shard_map/ppermute | solution.py:17
  42.1 14.1 %collective-permute-start.8 = (bf16[384,256]{1,0:T(8,128)(2,1)S(1)}, bf16[384,256]{1,0:T(8,128)(2,1)S(1)}, u32[]{:S(2)}, u32[]{:S(2)}) collective-permute-start(bf16[384,256]{1,0:T(8,128)(2,1)S(1)} %get-tuple-element.58), channel_id=1, source_target_pairs={{0,8},{8,16},{16,24},{24,0},{1,9},{9,17},{17,25},{25,1},{2,10},{10... | collective-permute-start | bytes 589832 | tf_op jit(solution)/shard_map/ppermute | solution.py:17
  45.4 16.2 %collective-permute-start.9 = (bf16[384,256]{1,0:T(8,128)(2,1)S(1)}, bf16[384,256]{1,0:T(8,128)(2,1)S(1)}, u32[]{:S(2)}, u32[]{:S(2)}) collective-permute-start(bf16[384,256]{1,0:T(8,128)(2,1)S(1)} %get-tuple-element.58), channel_id=1, source_target_pairs={{0,16},{8,24},{16,0},{24,8},{1,17},{9,25},{17,1},{25,9},{2,18},{10... | collective-permute-start | bytes 589832 | tf_op jit(solution)/shard_map/ppermute | solution.py:17
  56.2 7.0 %collective-permute-start.10 = (bf16[384,256]{1,0:T(8,128)(2,1)S(1)}, bf16[384,256]{1,0:T(8,128)(2,1)S(1)}, u32[]{:S(2)}, u32[]{:S(2)}) collective-permute-start(bf16[384,256]{1,0:T(8,128)(2,1)S(1)} %get-tuple-element.58), channel_id=1, source_target_pairs={{0,24},{8,0},{16,8},{24,16},{1,25},{9,1},{17,9},{25,17},{2,26},{10... | collective-permute-start | bytes 589832 | tf_op jit(solution)/shard_map/ppermute | solution.py:17
  63.2 36.9 %collective-permute-start.11 = (bf16[7,384,256]{2,1,0:T(8,128)(2,1)S(1)}, bf16[7,384,256]{2,1,0:T(8,128)(2,1)S(1)}, u32[]{:S(2)}, u32[]{:S(2)}) collective-permute-start(bf16[7,384,256]{2,1,0:T(8,128)(2,1)S(1)} %bitcast_dynamic-update-slice_fusion.4.refs_5_), channel_id=1, source_target_pairs={{0,1},{1,0},{2,3},{3,2},{4,5},{5,4},{6,7},{7,6},{8,9},{9,8},{10,11... | collective-permute-start | bytes 4128776 | tf_op jit(solution)/shard_map/ppermute | solution.py:17
  63.3 20.6 %collective-permute-start.16 = (bf16[4,224,384]{2,1,0:T(8,128)(2,1)S(1)}, bf16[4,224,384]{2,1,0:T(8,128)(2,1)S(1)}, u32[]{:S(2)}, u32[]{:S(2)}) collective-permute-start(bf16[4,224,384]{2,1,0:T(8,128)(2,1)S(1)} %copy-done.14), channel_id=1, source_target_pairs={{0,16},{8,24},{16,0},{24,8},{1,17},{9,25},{17,1},{25,9},{2,18},{10... | collective-permute-start | bytes 2064392 | tf_op jit(solution)/shard_map/ppermute | solution.py:17
  67.9 29.4 %collective-permute-start.17 = (bf16[4,224,384]{2,1,0:T(8,128)(2,1)S(1)}, bf16[4,224,384]{2,1,0:T(8,128)(2,1)S(1)}, u32[]{:S(2)}, u32[]{:S(2)}) collective-permute-start(bf16[4,224,384]{2,1,0:T(8,128)(2,1)S(1)} %copy-done.13), channel_id=1, source_target_pairs={{0,24},{8,0},{16,8},{24,16},{1,25},{9,1},{17,9},{25,17},{2,26},{10... | collective-permute-start | bytes 2064392 | tf_op jit(solution)/shard_map/ppermute | solution.py:17
  83.9 24.1 %collective-permute-start.1 = (bf16[4,224,384]{2,1,0:T(8,128)(2,1)}, bf16[4,224,384]{2,1,0:T(8,128)(2,1)}, u32[]{:S(2)}, u32[]{:S(2)}) collective-permute-start(bf16[4,224,384]{2,1,0:T(8,128)(2,1)} %get-tuple-element.40), channel_id=1, source_target_pairs={{0,32},{32,64},{64,96},{96,0},{1,33},{33,65},{65,97},{97,1},{2,34}... | collective-permute-start | bytes 2064392 | tf_op jit(solution)/shard_map/ppermute | solution.py:17
  97.3 21.1 %collective-permute-start.2 = (bf16[4,224,384]{2,1,0:T(8,128)(2,1)}, bf16[4,224,384]{2,1,0:T(8,128)(2,1)}, u32[]{:S(2)}, u32[]{:S(2)}) collective-permute-start(bf16[4,224,384]{2,1,0:T(8,128)(2,1)} %get-tuple-element.41), channel_id=1, source_target_pairs={{0,64},{32,96},{64,0},{96,32},{1,65},{33,97},{65,1},{97,33},{2,66}... | collective-permute-start | bytes 2064392 | tf_op jit(solution)/shard_map/ppermute | solution.py:17
  101.1 30.2 %collective-permute-start.3 = (bf16[4,224,384]{2,1,0:T(8,128)(2,1)}, bf16[4,224,384]{2,1,0:T(8,128)(2,1)}, u32[]{:S(2)}, u32[]{:S(2)}) collective-permute-start(bf16[4,224,384]{2,1,0:T(8,128)(2,1)} %get-tuple-element.42), channel_id=1, source_target_pairs={{0,96},{32,0},{64,32},{96,64},{1,97},{33,1},{65,33},{97,65},{2,98}... | collective-permute-start | bytes 2064392 | tf_op jit(solution)/shard_map/ppermute | solution.py:17
  107.9 33.1 %collective-permute-start.18 = (bf16[224,512]{1,0:T(8,128)(2,1)}, bf16[224,512]{1,0:T(8,128)(2,1)S(1)}, u32[]{:S(2)}, u32[]{:S(2)}) collective-permute-start(bf16[224,512]{1,0:T(8,128)(2,1)} %get-tuple-element.54), channel_id=1, source_target_pairs={{0,32},{32,64},{64,96},{96,0},{1,33},{33,65},{65,97},{97,1},{2,34}... | collective-permute-start | bytes 688136 | tf_op jit(solution)/shard_map/ppermute | solution.py:17
  118.5 24.9 %collective-permute-start.19 = (bf16[224,512]{1,0:T(8,128)(2,1)}, bf16[224,512]{1,0:T(8,128)(2,1)S(1)}, u32[]{:S(2)}, u32[]{:S(2)}) collective-permute-start(bf16[224,512]{1,0:T(8,128)(2,1)} %get-tuple-element.55), channel_id=1, source_target_pairs={{0,64},{32,96},{64,0},{96,32},{1,65},{33,97},{65,1},{97,33},{2,66}... | collective-permute-start | bytes 688136 | tf_op jit(solution)/shard_map/ppermute | solution.py:17
  125.6 35.2 %collective-permute-start.24 = (bf16[2048,512]{1,0:T(8,128)(2,1)}, bf16[2048,512]{1,0:T(8,128)(2,1)S(1)}, u32[]{:S(2)}, u32[]{:S(2)}) collective-permute-start(bf16[2048,512]{1,0:T(8,128)(2,1)} %collective-permute-done.23), channel_id=1, source_target_pairs={{0,1},{1,0},{2,3},{3,2},{4,5},{5,4},{6,7},{7,6},{8,9},{9,8},{10,11... | collective-permute-start | bytes 6291464 | tf_op jit(solution)/shard_map/ppermute | solution.py:17
  131.3 16.8 %collective-permute-start.20 = (bf16[224,512]{1,0:T(8,128)(2,1)S(1)}, bf16[224,512]{1,0:T(8,128)(2,1)S(1)}, u32[]{:S(2)}, u32[]{:S(2)}) collective-permute-start(bf16[224,512]{1,0:T(8,128)(2,1)S(1)} %copy-done.15), channel_id=1, source_target_pairs={{0,96},{32,0},{64,32},{96,64},{1,97},{33,1},{65,33},{97,65},{2,98}... | collective-permute-start | bytes 688136 | tf_op jit(solution)/shard_map/ppermute | solution.py:17
  139.3 9.0 %collective-permute-start.12 = (bf16[224,512]{1,0:T(8,128)(2,1)}, bf16[224,512]{1,0:T(8,128)(2,1)S(1)}, u32[]{:S(2)}, u32[]{:S(2)}) collective-permute-start(bf16[224,512]{1,0:T(8,128)(2,1)} %get-tuple-element.46), channel_id=1, source_target_pairs={{0,8},{8,16},{16,24},{24,0},{1,9},{9,17},{17,25},{25,1},{2,10},{10... | collective-permute-start | bytes 688136 | tf_op jit(solution)/shard_map/ppermute | solution.py:17
  141.0 12.6 %collective-permute-start.13 = (bf16[224,512]{1,0:T(8,128)(2,1)}, bf16[224,512]{1,0:T(8,128)(2,1)S(1)}, u32[]{:S(2)}, u32[]{:S(2)}) collective-permute-start(bf16[224,512]{1,0:T(8,128)(2,1)} %get-tuple-element.47), channel_id=1, source_target_pairs={{0,16},{8,24},{16,0},{24,8},{1,17},{9,25},{17,1},{25,9},{2,18},{10... | collective-permute-start | bytes 688136 | tf_op jit(solution)/shard_map/ppermute | solution.py:17
  143.4 10.2 %collective-permute-start.14 = (bf16[224,512]{1,0:T(8,128)(2,1)}, bf16[224,512]{1,0:T(8,128)(2,1)S(1)}, u32[]{:S(2)}, u32[]{:S(2)}) collective-permute-start(bf16[224,512]{1,0:T(8,128)(2,1)} %get-tuple-element.48), channel_id=1, source_target_pairs={{0,24},{8,0},{16,8},{24,16},{1,25},{9,1},{17,9},{25,17},{2,26},{10... | collective-permute-start | bytes 688136 | tf_op jit(solution)/shard_map/ppermute | solution.py:17
  (17 other events, 254.3 us)

commit v2 on v0

v2 whole, which is shorter than its diff:
```python
import jax
import jax.numpy as jnp
from jax import lax
from jax.experimental import pallas as pl
from jax.experimental.pallas import tpu as pltpu
from jax.sharding import Mesh, PartitionSpec as P


F32 = jnp.float32
BF16 = jnp.bfloat16
SIZE = {"x": 4, "z": 4, "yl": 2, "yh": 2, "c": 2}
SMEM = pl.BlockSpec(memory_space=pltpu.SMEM)
VMEM = pl.BlockSpec(memory_space=pltpu.VMEM)
HBM = pl.BlockSpec(memory_space=pl.ANY)
AXES = ("x", "z", "yl", "yh", "c")


def params(mib):
    return pltpu.CompilerParams(vmem_limit_bytes=mib * 1024 * 1024)


def shift(a, axis, k):
    n = SIZE[axis]
    return lax.ppermute(a, axis, [(i, (i + k) % n) for i in range(n)])


def cross(a, k):
    pairs = []
    for i in range(128):
        x, z, rest = i // 32, i // 8 % 4, i % 8
        if i % 2 == 0:
            x = (x + k) % 4
        else:
            z = (z + k) % 4
        pairs.append((i, x * 32 + z * 8 + rest))
    return lax.ppermute(a, AXES, pairs)


def coords_kernel(s_ref, x_ref, w_ref, mine_ref, theirs_ref):
    first = pl.program_id(0) == 0
    c = s_ref[0]
    for out, half in ((mine_ref, c), (theirs_ref, 1 - c)):
        start = pl.multiple_of(half * 256, 256)
        part = jnp.dot(x_ref[...], w_ref[:, pl.ds(start, 256)], preferred_element_type=F32)
        out[...] = jnp.where(first, part, out[...] + part)


def partial_coords(c, x, w):
    t = x.shape[0]
    return pl.pallas_call(
        coords_kernel,
        grid=(4,),
        in_specs=[
            SMEM,
            pl.BlockSpec((t, 512), lambda i: (0, i)),
            pl.BlockSpec((512, 512), lambda i: (i, 0)),
        ],
        out_specs=[VMEM] * 2,
        out_shape=[pltpu.VMEM((t, 256), F32)] * 2,
        compiler_params=params(8),
        name="coords",
    )(c.reshape(1), x, w)


def grad_kernel(s_ref, g_ref, h_ref, x0, x1, x2, x3, z0, z1, z2, z3, t_ref):
    i = pl.program_id(0)
    for b in range(14):
        cols = slice(b * 128, b * 128 + 128)
        v = 0.5 * g_ref[:, cols].astype(F32)
        w = v * h_ref[:, cols].astype(F32)
        t_ref[cols, :] = (w + w * jnp.tanh(v)).astype(BF16).T
    for k, out in enumerate((z0, z1, z2, z3)):
        start = pl.multiple_of(lax.rem(s_ref[1] + k, 4) * 448, 448)
        out[i] = t_ref[pl.ds(start + 224, 224), :]
        for j, own in enumerate((x0, x1, x2, x3)):

            @pl.when(i == j)
            def _():
                own[k] = t_ref[pl.ds(start, 224), :]


def grad_pieces(xz, gate, hidden):
    t = gate.shape[0]
    spec = pl.BlockSpec((t, 1792), lambda i, s: (0, lax.rem(s[0] + i, 4)))
    return pl.pallas_call(
        grad_kernel,
        grid_spec=pltpu.PrefetchScalarGridSpec(
            num_scalar_prefetch=1,
            grid=(4,),
            in_specs=[spec, spec],
            out_specs=[VMEM] * 8,
            scratch_shapes=[pltpu.VMEM((1792, t), BF16)],
        ),
        out_shape=[pltpu.VMEM((4, 224, t), BF16)] * 8,
        compiler_params=params(16),
        name="grads",
    )(xz, gate, hidden)


def partial_sums(near, late):
    acc = None
    for piece, coords in near:
        part = jnp.dot(piece.reshape(896, -1), coords, preferred_element_type=F32)
        acc = part if acc is None else acc + part
    acc = lax.optimization_barrier(acc)
    piece, coords = late
    out = []
    for j in range(4):
        part = jnp.dot(piece[j], coords, preferred_element_type=F32)
        part += acc[j * 224 : j * 224 + 224]
        out.append(part if j == 0 else part.astype(BF16))
    return out


def last_kernel(
    s_ref, mine, got, first, second, w0, w1, w2, w3, new_first, new_second, update, o_ref, sem
):
    yh, c = s_ref[0], s_ref[1]
    projected = mine[...] + got[...].astype(F32)
    m = 0.9 * first[...] + 0.1 * projected
    v = 0.95 * second[...] + 0.05 * projected * projected
    new_first[...] = m
    new_second[...] = v
    direction = (m / (1.0 - 0.81) / (jnp.sqrt(v / (1.0 - 0.9025)) + 1e-08)).astype(BF16)
    blocks = (2 * yh + c, 2 * yh + 1 - c, 2 - 2 * yh + c, 3 - 2 * yh - c)
    stores = []
    for k, w_ref in enumerate((w0, w1, w2, w3)):
        part = 4.0 * lax.dot_general(
            direction, w_ref[...], (((1,), (1,)), ((), ())), preferred_element_type=F32
        )
        o_ref[k] = part.astype(BF16)
        cols = pl.ds(pl.multiple_of(blocks[k] * 2048, 2048), 2048)
        store = pltpu.make_async_copy(o_ref.at[k], update.at[:, cols], sem.at[k])
        store.start()
        stores.append(store)
    for store in stores:
        store.wait()


def last_stage(at, mine, got, first, second, blocks):
    rows = first.shape[0]
    moment = jax.ShapeDtypeStruct((rows, 512), F32)
    args = [pltpu.with_memory_space_constraint(a, pltpu.VMEM) for a in (mine, got, first, second) + blocks]
    return pl.pallas_call(
        last_kernel,
        in_specs=[SMEM] + [VMEM] * 8,
        out_specs=[VMEM, VMEM, HBM],
        out_shape=[moment, moment, jax.ShapeDtypeStruct((rows, 8192), BF16)],
        scratch_shapes=[pltpu.VMEM((4, rows, 2048), BF16), pltpu.SemaphoreType.DMA((4,))],
        compiler_params=params(12),
        name="last",
    )(at, *args)


def step(inputs, gate_preact, hidden_grad, projector, first_moment, second_moment):
    x, z, yl, yh, c = (lax.axis_index(a).astype(jnp.int32) for a in AXES)
    place = jnp.stack([x, z, yh, c])

    inputs, gate_preact, hidden_grad = (
        pltpu.with_memory_space_constraint(a, pltpu.HBM) for a in (inputs, gate_preact, hidden_grad)
    )
    mine, theirs = partial_coords(
        c, inputs, pltpu.with_memory_space_constraint(projector, pltpu.HBM)
    )
    theirs = shift(theirs, "c", 1)
    chip_sum = mine + theirs
    far = shift(chip_sum.astype(BF16), "yh", 1)
    half = (chip_sum + far.astype(F32)).astype(BF16)
    other = shift(half, "c", 1)
    own = jnp.concatenate(
        [jnp.where(c == 0, half, other), jnp.where(c == 0, other, half)], axis=1
    )
    along = {k: cross(own, k) for k in (1, 3, 2)}
    beyond = {k: shift(along[k], "c", 1) for k in (1, 3, 2)}
    coords_x = {k: jnp.where(c == 0, along[k], beyond[k]) for k in (1, 3, 2)}
    coords_z = {k: jnp.where(c == 0, beyond[k], along[k]) for k in (1, 3, 2)}

    near_w = lax.ppermute(projector, ("yl", "yh"), [(0, 3), (3, 0), (1, 2), (2, 1)])
    beside_w = shift(projector, "c", 1)
    across_w = shift(near_w, "c", 1)

    pieces = grad_pieces(jnp.stack([x, z]), gate_preact, hidden_grad)
    from_x = [pieces[0]] + [shift(pieces[k], "x", k) for k in (1, 2, 3)]
    from_z = [pieces[4]] + [shift(pieces[4 + k], "z", k) for k in (1, 2, 3)]

    sums = []
    for got, coords, axis in ((from_z, coords_z, "x"), (from_x, coords_x, "z")):
        part = partial_sums(
            [(got[0], own), (got[1], coords[1]), (got[3], coords[3])], (got[2], coords[2])
        )
        total = part[0]
        for k in (1, 3, 2):
            total += shift(part[k], axis, k).astype(F32)
        sums.append(total)
    sum_z, sum_x = sums
    keep = jnp.where(yl == 0, sum_x, sum_z)
    give = jnp.where(yl == 0, sum_z, sum_x).astype(BF16)
    got = shift(give, "yl", 1)
    return last_stage(
        place[2:], keep, got, first_moment, second_moment, (projector, beside_w, near_w, across_w)
    )


def solution(mesh):
    fine = Mesh(mesh.devices.reshape(4, 4, 2, 2, 2), ("x", "z", "yl", "yh", "c"))
    dp, mp = ("x", "z", "yl"), ("yh", "c")
    return jax.shard_map(
        step,
        mesh=fine,
        in_specs=(P(dp, mp), P(dp, mp), P(dp, mp), P(mp, None), P(mp + dp, None), P(mp + dp, None)),
        out_specs=(P(mp + dp, None),) * 3,
        check_vma=False,
    )
```

time: 481 us -> 142 us (0.30)
  the two profiles are of different devices: /device:TPU:74 before, /device:TPU:4 now
where the time goes in v2:
time: 142 us; the launch traced here: 141 us
  waiting for transfers between devices  64.6 us (45%)
  starting transfers between devices  40.9 us (29%)
  Pallas kernels  19.7 us (14%)
  matrix products  9.8 us (7%)
  local copies, waits for them, and re-layouts  3.47 us (2%)
  other arithmetic  1.94 us (1%)
    ppermute x21, waiting for transfers between devices, shift(): return lax.ppermute(a, axis, [(i, (i + k) % n) for i in range(n)])  64.6 us
    ppermute x21, starting transfers between devices, shift(): return lax.ppermute(a, axis, [(i, (i + k) % n) for i in range(n)])  33.3 us
    pallas_call x1, Pallas kernels, grad_pieces(): pl.pallas_call(grad_kernel, grid_spec=pltpu.PrefetchScalarGridSpec(num_sc...  8.4 us
    pallas_call x1, Pallas kernels, last_stage(): pl.pallas_call(last_kernel, in_specs=[SMEM] + [VMEM] * 8, out_specs=[VMEM...  7.72 us
    dot_general x6, matrix products, partial_sums(): part = jnp.dot(piece.reshape(896, -1), coords, preferred_element_type=F32)  7.4 us
    ppermute x3, starting transfers between devices, cross(): return lax.ppermute(a, AXES, pairs)  4.62 us
    pallas_call x1, Pallas kernels, partial_coords(): pl.pallas_call(coords_kernel, grid=(4,), in_specs=[SMEM, pl.BlockSpec((t,...  3.57 us
    unnamed x30, local copies, waits for them, and re-layouts  3.47 us
  transfers between devices with their start and end apart: 25, of which 15 were waited for; matrix products, arithmetic and copies ran while one was open for 8% of the time, Pallas kernels for 6%

profile of v2, /device:TPU:4, one launch (start us, length us, event | category | flops | bytes accessed | tf_op | source)
XLA Modules:
  0.0 141.4 jit_solution(7203372978707897956)
XLA Ops:
  0.6 3.6 %coords.1 = (f32[384,256]{1,0:T(8,128)S(1)}, f32[384,256]{1,0:T(8,128)S(1)}) custom-call(s32[1]{0:T(128)} %bitcast.1.s_ref, bf16[384,2048]{1,0:T(8,128)(2,1)} %x_ref.1, bf16[2048,512]{1,0:T(8,128)(2,1)} %w0.1), custom_call_target="tpu_custom_call" | custom-call | tf_op jit(solution)/shard_map/coords/pallas_call | solution.py:50
  4.3 1.7 %collective-permute-done.1 = f32[384,256]{1,0:T(8,128)S(1)} collective-permute-done((f32[384,256]{1,0:T(8,128)S(1)}, f32[384,256]{1,0:T(8,128)S(1)}, u32[]{:S(2)}, u32[]{:S(2)}) %collective-permute-start.1) | collective-permute-done | bytes 393248 | tf_op jit(solution)/shard_map/ppermute | solution.py:24
  6.1 3.3 %collective-permute-start.2 = (bf16[384,256]{1,0:T(8,128)(2,1)S(1)}, bf16[384,256]{1,0:T(8,128)(2,1)S(1)}, u32[]{:S(2)}, u32[]{:S(2)}) collective-permute-start(bf16[384,256]{1,0:T(8,128)(2,1)S(1)} %get-tuple-element.23), channel_id=1, source_target_pairs={{0,2},{2,0},{1,3},{3,1},{4,6},{6,4},{5,7},{7,5},{8,10},{10,8},{9,1... | collective-permute-start | bytes 589832 | tf_op jit(solution)/shard_map/ppermute | solution.py:24
  9.3 5.3 %collective-permute-done.2 = bf16[384,256]{1,0:T(8,128)(2,1)S(1)} collective-permute-done((bf16[384,256]{1,0:T(8,128)(2,1)S(1)}, bf16[384,256]{1,0:T(8,128)(2,1)S(1)}, u32[]{:S(2)}, u32[]{:S(2)}) %collective-permute-start.2) | collective-permute-done | bytes 196640 | tf_op jit(solution)/shard_map/ppermute | solution.py:24
  18.4 8.4 %grads.1 = (bf16[4,224,384]{2,1,0:T(8,128)(2,1)S(1)}, bf16[4,224,384]{2,1,0:T(8,128)(2,1)}, bf16[4,224,384]{2,1,0:T(8,128)(2,1)S(1)}, bf16[4,224,384]{2,1,0:T(8,...) custom-call(s32[2]{0:T(128)S(1)} %pad_add_fusion.1.s_ref, ...), custom_call_target="tpu_custom_call" | custom-call | tf_op jit(solution)/shard_map/grads/pallas_call | solution.py:85
  32.2 3.0 %collective-permute-start.23 = (bf16[2048,512]{1,0:T(8,128)(2,1)S(1)}, bf16[2048,512]{1,0:T(8,128)(2,1)}, u32[]{:S(2)}, u32[]{:S(2)}) collective-permute-start(bf16[2048,512]{1,0:T(8,128)(2,1)S(1)} %copy-done), channel_id=1, source_target_pairs={{0,6},{6,0},{2,4},{4,2},{1,7},{7,1},{3,5},{5,3},{8,14},{14,8},{10,... | collective-permute-start | bytes 6291464 | tf_op jit(solution)/shard_map/ppermute | solution.py:178
  37.1 1.7 %fusion.23 = f32[896,512]{1,0:T(8,128)S(1)} fusion(bf16[896,384]{1,0:T(8,128)(2,1)S(1)} %bitcast.51, bf16[384,256]{1,0:T(8,128)(2,1)} %copy-done.13, bf16[384,256]{1,0:T(8,128)(2,1)} %copy-done.11), kind=kOutput, calls=%fused_computation.51 | convolution fusion | flops 353107968 | bytes 2916352 | tf_op jit(solution)/shard_map/dot_general | solution.py:103
  39.8 8.7 %collective-permute-done.6 = bf16[4,224,384]{2,1,0:T(8,128)(2,1)} collective-permute-done((bf16[4,224,384]{2,1,0:T(8,128)(2,1)}, bf16[4,224,384]{2,1,0:T(8,128)(2,1)}, u32[]{:S(2)}, u32[]{:S(2)}) %collective-permute-start.6) | collective-permute-done | bytes 688160 | tf_op jit(solution)/shard_map/ppermute | solution.py:24
  48.5 2.0 %collective-permute-start.16 = (bf16[4,224,384]{2,1,0:T(8,128)(2,1)S(1)}, bf16[4,224,384]{2,1,0:T(8,128)(2,1)S(1)}, u32[]{:S(2)}, u32[]{:S(2)}) collective-permute-start(bf16[4,224,384]{2,1,0:T(8,128)(2,1)S(1)} %copy-done.10), channel_id=1, source_target_pairs={{0,8},{8,16},{16,24},{24,0},{1,9},{9,17},{17,25},{25,1},{2,10},{10... | collective-permute-start | bytes 2064392 | tf_op jit(solution)/shard_map/ppermute | solution.py:24
  50.4 1.9 %fusion.16 = f32[896,512]{1,0:T(8,128)S(1)} fusion(bf16[896,384]{1,0:T(8,128)(2,1)} %bitcast.6, bf16[384,512]{1,0:T(8,128)(2,1)} %collective-permute-done.7, bf16[384,512]{1,0:T(8,128)(2,1)S(1)} %collective-permute-done.8, pred[]{:T(512)S(6)} %eq.5), kind=kOutput, calls=%fused_computation.28 | convolution fusion | flops 352518144 | bytes 3309569 | tf_op jit(solution)/shard_map/dot_general | solution.py:103
  53.5 4.0 %collective-permute-start.17 = (bf16[4,224,384]{2,1,0:T(8,128)(2,1)S(1)}, bf16[4,224,384]{2,1,0:T(8,128)(2,1)S(1)}, u32[]{:S(2)}, u32[]{:S(2)}) collective-permute-start(bf16[4,224,384]{2,1,0:T(8,128)(2,1)S(1)} %copy-done.8), channel_id=1, source_target_pairs={{0,24},{8,0},{16,8},{24,16},{1,25},{9,1},{17,9},{25,17},{2,26},{10... | collective-permute-start | bytes 2064392 | tf_op jit(solution)/shard_map/ppermute | solution.py:24
  57.6 1.8 %collective-permute-start.4 = (bf16[384,512]{1,0:T(8,128)(2,1)}, bf16[384,512]{1,0:T(8,128)(2,1)S(1)}, u32[]{:S(2)}, u32[]{:S(2)}) collective-permute-start(bf16[384,512]{1,0:T(8,128)(2,1)} %pad_maximum_fusion), channel_id=1, source_target_pairs={{0,64},{1,17},{2,66},{3,19},{4,68},{5,21},{6,70},{7,23},{8,72},{9,... | collective-permute-start | bytes 1179656 | tf_op jit(solution)/shard_map/ppermute | solution.py:36
  59.4 1.9 %add_add_fusion.1 = f32[896,512]{1,0:T(8,128)S(1)} fusion(f32[896,512]{1,0:T(8,128)S(1)} %fusion.23, f32[896,512]{1,0:T(8,128)S(1)} %fusion.16, bf16[896,384]{1,0:T(8,128)(2,1)} %bitcast.7, bf16[384,512]{1,0:T(8,128)(2,1)} %collective-permute-done.10, bf16[384,512]{1,0:T(8,128)(2,1)S(1)} %collective-permute-done.11, pred[]{:T(512)S(6)} %eq.5), kind=kOutput, calls=%fused_computation.1 | convolution fusion | flops 353435648 | bytes 6979585 | tf_op jit(solution)/shard_map/dot_general | solution.py:103
  61.3 6.2 %collective-permute-done.16 = bf16[4,224,384]{2,1,0:T(8,128)(2,1)S(1)} collective-permute-done((bf16[4,224,384]{2,1,0:T(8,128)(2,1)S(1)}, bf16[4,224,384]{2,1,0:T(8,128)(2,1)S(1)}, u32[]{:S(2)}, u32[]{:S(2)}) %collective-permute-start.16) | collective-permute-done | bytes 688160 | tf_op jit(solution)/shard_map/ppermute | solution.py:24
  67.5 14.0 %collective-permute-start.15 = (bf16[4,224,384]{2,1,0:T(8,128)(2,1)S(1)}, bf16[4,224,384]{2,1,0:T(8,128)(2,1)S(1)}, u32[]{:S(2)}, u32[]{:S(2)}) collective-permute-start(bf16[4,224,384]{2,1,0:T(8,128)(2,1)S(1)} %copy-done.6), channel_id=1, source_target_pairs={{0,16},{8,24},{16,0},{24,8},{1,17},{9,25},{17,1},{25,9},{2,18},{10... | collective-permute-start | bytes 2064392 | tf_op jit(solution)/shard_map/ppermute | solution.py:24
  82.1 7.8 %collective-permute-done.17 = bf16[4,224,384]{2,1,0:T(8,128)(2,1)S(1)} collective-permute-done((bf16[4,224,384]{2,1,0:T(8,128)(2,1)S(1)}, bf16[4,224,384]{2,1,0:T(8,128)(2,1)S(1)}, u32[]{:S(2)}, u32[]{:S(2)}) %collective-permute-start.17) | collective-permute-done | bytes 688160 | tf_op jit(solution)/shard_map/ppermute | solution.py:24
  93.7 1.7 %collective-permute-start.19 = (bf16[224,512]{1,0:T(8,128)(2,1)S(1)}, bf16[224,512]{1,0:T(8,128)(2,1)S(1)}, u32[]{:S(2)}, u32[]{:S(2)}) collective-permute-start(bf16[224,512]{1,0:T(8,128)(2,1)S(1)} %fusion.10), channel_id=1, source_target_pairs={{0,96},{32,0},{64,32},{96,64},{1,97},{33,1},{65,33},{97,65},{2,98}... | collective-permute-start | bytes 688136 | tf_op jit(solution)/shard_map/ppermute | solution.py:24
  95.7 11.6 %collective-permute-done = bf16[4,224,384]{2,1,0:T(8,128)(2,1)S(1)} collective-permute-done((bf16[4,224,384]{2,1,0:T(8,128)(2,1)S(1)}, bf16[4,224,384]{2,1,0:T(8,128)(2,1)S(1)}, u32[]{:S(2)}, u32[]{:S(2)}) %collective-permute-start) | collective-permute-done | bytes 688160 | tf_op jit(solution)/shard_map/ppermute | solution.py:24
  109.8 3.7 %collective-permute-start.13 = (bf16[224,512]{1,0:T(8,128)(2,1)S(1)}, bf16[224,512]{1,0:T(8,128)(2,1)S(1)}, u32[]{:S(2)}, u32[]{:S(2)}) collective-permute-start(bf16[224,512]{1,0:T(8,128)(2,1)S(1)} %fusion.7), channel_id=1, source_target_pairs={{0,24},{8,0},{16,8},{24,16},{1,25},{9,1},{17,9},{25,17},{2,26},{10... | collective-permute-start | bytes 688136 | tf_op jit(solution)/shard_map/ppermute | solution.py:24
  115.3 3.9 %collective-permute-done.12 = bf16[224,512]{1,0:T(8,128)(2,1)S(1)} collective-permute-done((bf16[224,512]{1,0:T(8,128)(2,1)S(1)}, bf16[224,512]{1,0:T(8,128)(2,1)S(1)}, u32[]{:S(2)}, u32[]{:S(2)}) %collective-permute-start.12) | collective-permute-done | bytes 229408 | tf_op jit(solution)/shard_map/ppermute | solution.py:24
  119.3 4.2 %collective-permute-done.13 = bf16[224,512]{1,0:T(8,128)(2,1)S(1)} collective-permute-done((bf16[224,512]{1,0:T(8,128)(2,1)S(1)}, bf16[224,512]{1,0:T(8,128)(2,1)S(1)}, u32[]{:S(2)}, u32[]{:S(2)}) %collective-permute-start.13) | collective-permute-done | bytes 229408 | tf_op jit(solution)/shard_map/ppermute | solution.py:24
  123.5 1.9 %collective-permute-done.14 = bf16[224,512]{1,0:T(8,128)(2,1)S(1)} collective-permute-done((bf16[224,512]{1,0:T(8,128)(2,1)S(1)}, bf16[224,512]{1,0:T(8,128)(2,1)S(1)}, u32[]{:S(2)}, u32[]{:S(2)}) %collective-permute-start.14) | collective-permute-done | bytes 229408 | tf_op jit(solution)/shard_map/ppermute | solution.py:24
  126.7 6.8 %collective-permute-done.21.got = bf16[224,512]{1,0:T(8,128)(2,1)} collective-permute-done((bf16[224,512]{1,0:T(8,128)(2,1)}, bf16[224,512]{1,0:T(8,128)(2,1)}, u32[]{:S(2)}, u32[]{:S(2)}) %collective-permute-start.21) | collective-permute-done | bytes 229408 | tf_op jit(solution)/shard_map/ppermute | solution.py:24
  133.6 7.7 %last.1 = (f32[224,512]{1,0:T(8,128)}, f32[224,512]{1,0:T(8,128)}, bf16[224,8192]{1,0:T(8,128)(2,1)}) custom-call(s32[2]{0:T(128)S(1)} %pad_add_fusion.s_ref, f32[224,512]{1,0:T(8,128)S(1)} %get-tuple-element.29.mine, bf16[224,512]{1,0:T(8,128)(2,1)} %collective-permute-done.21.got, f32[224,512]{1,0:T(8,128)S(1)} %copy-done.1, f32[224,512]{1,0:T(8,128)S(1)} %copy-done.2, ...), custom_call_target="tpu_custom_call" | custom-call | tf_op jit(solution)/shard_map/last/pallas_call | solution.py:144
  (81 shorter events, 23.8 us)
Async XLA Ops:
  4.2 1.8 %collective-permute-start.1 = (f32[384,256]{1,0:T(8,128)S(1)}, f32[384,256]{1,0:T(8,128)S(1)}, u32[]{:S(2)}, u32[]{:S(2)}) collective-permute-start(f32[384,256]{1,0:T(8,128)S(1)} %get-tuple-element.15), channel_id=1, source_target_pairs={{0,1},{1,0},{2,3},{3,2},{4,5},{5,4},{6,7},{7,6},{8,9},{9,8},{10,11... | collective-permute-start | bytes 1179656 | tf_op jit(solution)/shard_map/ppermute | solution.py:24
  6.1 8.5 %collective-permute-start.2 = (bf16[384,256]{1,0:T(8,128)(2,1)S(1)}, bf16[384,256]{1,0:T(8,128)(2,1)S(1)}, u32[]{:S(2)}, u32[]{:S(2)}) collective-permute-start(bf16[384,256]{1,0:T(8,128)(2,1)S(1)} %get-tuple-element.23), channel_id=1, source_target_pairs={{0,2},{2,0},{1,3},{3,1},{4,6},{6,4},{5,7},{7,5},{8,10},{10,8},{9,1... | collective-permute-start | bytes 589832 | tf_op jit(solution)/shard_map/ppermute | solution.py:24
  17.1 19.0 %collective-permute-start.7 = (bf16[384,512]{1,0:T(8,128)(2,1)}, bf16[384,512]{1,0:T(8,128)(2,1)}, u32[]{:S(2)}, u32[]{:S(2)}) collective-permute-start(bf16[384,512]{1,0:T(8,128)(2,1)} %pad_maximum_fusion), channel_id=1, source_target_pairs={{0,32},{1,9},{2,34},{3,11},{4,36},{5,13},{6,38},{7,15},{8,40},{9,1... | collective-permute-start | bytes 1179656 | tf_op jit(solution)/shard_map/ppermute | solution.py:36
  30.2 18.2 %collective-permute-start.6 = (bf16[4,224,384]{2,1,0:T(8,128)(2,1)}, bf16[4,224,384]{2,1,0:T(8,128)(2,1)}, u32[]{:S(2)}, u32[]{:S(2)}) collective-permute-start(bf16[4,224,384]{2,1,0:T(8,128)(2,1)} %get-tuple-element.17), channel_id=1, source_target_pairs={{0,32},{32,64},{64,96},{96,0},{1,33},{33,65},{65,97},{97,1},{2,34}... | collective-permute-start | bytes 2064392 | tf_op jit(solution)/shard_map/ppermute | solution.py:24
  30.6 8.2 %collective-permute-start.10 = (bf16[384,512]{1,0:T(8,128)(2,1)}, bf16[384,512]{1,0:T(8,128)(2,1)}, u32[]{:S(2)}, u32[]{:S(2)}) collective-permute-start(bf16[384,512]{1,0:T(8,128)(2,1)} %pad_maximum_fusion), channel_id=1, source_target_pairs={{0,96},{1,25},{2,98},{3,27},{4,100},{5,29},{6,102},{7,31},{8,104},... | collective-permute-start | bytes 1179656 | tf_op jit(solution)/shard_map/ppermute | solution.py:36
  32.2 60.7 %collective-permute-start.23 = (bf16[2048,512]{1,0:T(8,128)(2,1)S(1)}, bf16[2048,512]{1,0:T(8,128)(2,1)}, u32[]{:S(2)}, u32[]{:S(2)}) collective-permute-start(bf16[2048,512]{1,0:T(8,128)(2,1)S(1)} %copy-done), channel_id=1, source_target_pairs={{0,6},{6,0},{2,4},{4,2},{1,7},{7,1},{3,5},{5,3},{8,14},{14,8},{10,... | collective-permute-start | bytes 6291464 | tf_op jit(solution)/shard_map/ppermute | solution.py:178
  35.2 18.3 %collective-permute-start.9 = (bf16[4,224,384]{2,1,0:T(8,128)(2,1)}, bf16[4,224,384]{2,1,0:T(8,128)(2,1)}, u32[]{:S(2)}, u32[]{:S(2)}) collective-permute-start(bf16[4,224,384]{2,1,0:T(8,128)(2,1)} %get-tuple-element.18), channel_id=1, source_target_pairs={{0,96},{32,0},{64,32},{96,64},{1,97},{33,1},{65,33},{97,65},{2,98}... | collective-permute-start | bytes 2064392 | tf_op jit(solution)/shard_map/ppermute | solution.py:24
  36.1 12.4 %collective-permute-start.8 = (bf16[384,512]{1,0:T(8,128)(2,1)}, bf16[384,512]{1,0:T(8,128)(2,1)S(1)}, u32[]{:S(2)}, u32[]{:S(2)}) collective-permute-start(bf16[384,512]{1,0:T(8,128)(2,1)} %collective-permute-done.7), channel_id=1, source_target_pairs={{0,1},{1,0},{2,3},{3,2},{4,5},{5,4},{6,7},{7,6},{8,9},{9,8},{10,11... | collective-permute-start | bytes 1179656 | tf_op jit(solution)/shard_map/ppermute | solution.py:24
  38.8 18.8 %collective-permute-start.11 = (bf16[384,512]{1,0:T(8,128)(2,1)}, bf16[384,512]{1,0:T(8,128)(2,1)S(1)}, u32[]{:S(2)}, u32[]{:S(2)}) collective-permute-start(bf16[384,512]{1,0:T(8,128)(2,1)} %collective-permute-done.10), channel_id=1, source_target_pairs={{0,1},{1,0},{2,3},{3,2},{4,5},{5,4},{6,7},{7,6},{8,9},{9,8},{10,11... | collective-permute-start | bytes 1179656 | tf_op jit(solution)/shard_map/ppermute | solution.py:24
  48.4 85.1 %collective-permute-start.22 = (bf16[2048,512]{1,0:T(8,128)(2,1)S(1)}, bf16[2048,512]{1,0:T(8,128)(2,1)}, u32[]{:S(2)}, u32[]{:S(2)}) collective-permute-start(bf16[2048,512]{1,0:T(8,128)(2,1)S(1)} %copy-done), channel_id=1, source_target_pairs={{0,1},{1,0},{2,3},{3,2},{4,5},{5,4},{6,7},{7,6},{8,9},{9,8},{10,11... | collective-permute-start | bytes 6291464 | tf_op jit(solution)/shard_map/ppermute | solution.py:24
  48.5 19.1 %collective-permute-start.16 = (bf16[4,224,384]{2,1,0:T(8,128)(2,1)S(1)}, bf16[4,224,384]{2,1,0:T(8,128)(2,1)S(1)}, u32[]{:S(2)}, u32[]{:S(2)}) collective-permute-start(bf16[4,224,384]{2,1,0:T(8,128)(2,1)S(1)} %copy-done.10), channel_id=1, source_target_pairs={{0,8},{8,16},{16,24},{24,0},{1,9},{9,17},{17,25},{25,1},{2,10},{10... | collective-permute-start | bytes 2064392 | tf_op jit(solution)/shard_map/ppermute | solution.py:24
  53.5 36.4 %collective-permute-start.17 = (bf16[4,224,384]{2,1,0:T(8,128)(2,1)S(1)}, bf16[4,224,384]{2,1,0:T(8,128)(2,1)S(1)}, u32[]{:S(2)}, u32[]{:S(2)}) collective-permute-start(bf16[4,224,384]{2,1,0:T(8,128)(2,1)S(1)} %copy-done.8), channel_id=1, source_target_pairs={{0,24},{8,0},{16,8},{24,16},{1,25},{9,1},{17,9},{25,17},{2,26},{10... | collective-permute-start | bytes 2064392 | tf_op jit(solution)/shard_map/ppermute | solution.py:24
  57.6 33.2 %collective-permute-start.4 = (bf16[384,512]{1,0:T(8,128)(2,1)}, bf16[384,512]{1,0:T(8,128)(2,1)S(1)}, u32[]{:S(2)}, u32[]{:S(2)}) collective-permute-start(bf16[384,512]{1,0:T(8,128)(2,1)} %pad_maximum_fusion), channel_id=1, source_target_pairs={{0,64},{1,17},{2,66},{3,19},{4,68},{5,21},{6,70},{7,23},{8,72},{9,... | collective-permute-start | bytes 1179656 | tf_op jit(solution)/shard_map/ppermute | solution.py:36
  67.5 25.0 %collective-permute-start.15 = (bf16[4,224,384]{2,1,0:T(8,128)(2,1)S(1)}, bf16[4,224,384]{2,1,0:T(8,128)(2,1)S(1)}, u32[]{:S(2)}, u32[]{:S(2)}) collective-permute-start(bf16[4,224,384]{2,1,0:T(8,128)(2,1)S(1)} %copy-done.6), channel_id=1, source_target_pairs={{0,16},{8,24},{16,0},{24,8},{1,17},{9,25},{17,1},{25,9},{2,18},{10... | collective-permute-start | bytes 2064392 | tf_op jit(solution)/shard_map/ppermute | solution.py:24
  89.9 17.4 %collective-permute-start = (bf16[4,224,384]{2,1,0:T(8,128)(2,1)S(1)}, bf16[4,224,384]{2,1,0:T(8,128)(2,1)S(1)}, u32[]{:S(2)}, u32[]{:S(2)}) collective-permute-start(bf16[4,224,384]{2,1,0:T(8,128)(2,1)S(1)} %copy-done.4), channel_id=1, source_target_pairs={{0,64},{32,96},{64,0},{96,32},{1,65},{33,97},{65,1},{97,33},{2,66}... | collective-permute-start | bytes 2064392 | tf_op jit(solution)/shard_map/ppermute | solution.py:24
  90.7 1.7 %collective-permute-start.5 = (bf16[384,512]{1,0:T(8,128)(2,1)S(1)}, bf16[384,512]{1,0:T(8,128)(2,1)S(1)}, u32[]{:S(2)}, u32[]{:S(2)}) collective-permute-start(bf16[384,512]{1,0:T(8,128)(2,1)S(1)} %collective-permute-done.4), channel_id=1, source_target_pairs={{0,1},{1,0},{2,3},{3,2},{4,5},{5,4},{6,7},{7,6},{8,9},{9,8},{10,11... | collective-permute-start | bytes 1179656 | tf_op jit(solution)/shard_map/ppermute | solution.py:24
  92.8 16.9 %collective-permute-start.18 = (bf16[224,512]{1,0:T(8,128)(2,1)S(1)}, bf16[224,512]{1,0:T(8,128)(2,1)S(1)}, u32[]{:S(2)}, u32[]{:S(2)}) collective-permute-start(bf16[224,512]{1,0:T(8,128)(2,1)S(1)} %fusion.9), channel_id=1, source_target_pairs={{0,32},{32,64},{64,96},{96,0},{1,33},{33,65},{65,97},{97,1},{2,34}... | collective-permute-start | bytes 688136 | tf_op jit(solution)/shard_map/ppermute | solution.py:24
  92.9 40.6 %collective-permute-start.24 = (bf16[2048,512]{1,0:T(8,128)(2,1)}, bf16[2048,512]{1,0:T(8,128)(2,1)}, u32[]{:S(2)}, u32[]{:S(2)}) collective-permute-start(bf16[2048,512]{1,0:T(8,128)(2,1)} %collective-permute-done.23.w2), channel_id=1, source_target_pairs={{0,1},{1,0},{2,3},{3,2},{4,5},{5,4},{6,7},{7,6},{8,9},{9,8},{10,11... | collective-permute-start | bytes 6291464 | tf_op jit(solution)/shard_map/ppermute | solution.py:24
  93.7 16.0 %collective-permute-start.19 = (bf16[224,512]{1,0:T(8,128)(2,1)S(1)}, bf16[224,512]{1,0:T(8,128)(2,1)S(1)}, u32[]{:S(2)}, u32[]{:S(2)}) collective-permute-start(bf16[224,512]{1,0:T(8,128)(2,1)S(1)} %fusion.10), channel_id=1, source_target_pairs={{0,96},{32,0},{64,32},{96,64},{1,97},{33,1},{65,33},{97,65},{2,98}... | collective-permute-start | bytes 688136 | tf_op jit(solution)/shard_map/ppermute | solution.py:24
  107.3 7.5 %collective-permute-start.20 = (bf16[224,512]{1,0:T(8,128)(2,1)S(1)}, bf16[224,512]{1,0:T(8,128)(2,1)S(1)}, u32[]{:S(2)}, u32[]{:S(2)}) collective-permute-start(bf16[224,512]{1,0:T(8,128)(2,1)S(1)} %fusion.11), channel_id=1, source_target_pairs={{0,64},{32,96},{64,0},{96,32},{1,65},{33,97},{65,1},{97,33},{2,66}... | collective-permute-start | bytes 688136 | tf_op jit(solution)/shard_map/ppermute | solution.py:24
  109.7 9.5 %collective-permute-start.12 = (bf16[224,512]{1,0:T(8,128)(2,1)S(1)}, bf16[224,512]{1,0:T(8,128)(2,1)S(1)}, u32[]{:S(2)}, u32[]{:S(2)}) collective-permute-start(bf16[224,512]{1,0:T(8,128)(2,1)S(1)} %fusion.6), channel_id=1, source_target_pairs={{0,8},{8,16},{16,24},{24,0},{1,9},{9,17},{17,25},{25,1},{2,10},{10... | collective-permute-start | bytes 688136 | tf_op jit(solution)/shard_map/ppermute | solution.py:24
  109.8 13.7 %collective-permute-start.13 = (bf16[224,512]{1,0:T(8,128)(2,1)S(1)}, bf16[224,512]{1,0:T(8,128)(2,1)S(1)}, u32[]{:S(2)}, u32[]{:S(2)}) collective-permute-start(bf16[224,512]{1,0:T(8,128)(2,1)S(1)} %fusion.7), channel_id=1, source_target_pairs={{0,24},{8,0},{16,8},{24,16},{1,25},{9,1},{17,9},{25,17},{2,26},{10... | collective-permute-start | bytes 688136 | tf_op jit(solution)/shard_map/ppermute | solution.py:24
  114.8 10.5 %collective-permute-start.14 = (bf16[224,512]{1,0:T(8,128)(2,1)S(1)}, bf16[224,512]{1,0:T(8,128)(2,1)S(1)}, u32[]{:S(2)}, u32[]{:S(2)}) collective-permute-start(bf16[224,512]{1,0:T(8,128)(2,1)S(1)} %fusion.8), channel_id=1, source_target_pairs={{0,16},{8,24},{16,0},{24,8},{1,17},{9,25},{17,1},{25,9},{2,18},{10... | collective-permute-start | bytes 688136 | tf_op jit(solution)/shard_map/ppermute | solution.py:24
  126.5 7.1 %collective-permute-start.21 = (bf16[224,512]{1,0:T(8,128)(2,1)}, bf16[224,512]{1,0:T(8,128)(2,1)}, u32[]{:S(2)}, u32[]{:S(2)}) collective-permute-start(bf16[224,512]{1,0:T(8,128)(2,1)} %select_convert_fusion), channel_id=1, source_target_pairs={{0,4},{4,0},{1,5},{5,1},{2,6},{6,2},{3,7},{7,3},{8,12},{12,8},{9,1... | collective-permute-start | bytes 688136 | tf_op jit(solution)/shard_map/ppermute | solution.py:24
  (16 other events, 125.7 us)

commit v3 on v2

v3 whole, which is shorter than its diff:
```python
import jax
import jax.numpy as jnp
from jax import lax
from jax.experimental import pallas as pl
from jax.experimental.pallas import tpu as pltpu
from jax.sharding import Mesh, PartitionSpec as P


F32 = jnp.float32
BF16 = jnp.bfloat16
SIZE = {"x": 4, "z": 4, "yl": 2, "yh": 2, "c": 2}
SMEM = pl.BlockSpec(memory_space=pltpu.SMEM)
VMEM = pl.BlockSpec(memory_space=pltpu.VMEM)
HBM = pl.BlockSpec(memory_space=pl.ANY)
AXES = ("x", "z", "yl", "yh", "c")


def params(mib):
    return pltpu.CompilerParams(vmem_limit_bytes=mib * 1024 * 1024)


def shift(a, axis, k):
    n = SIZE[axis]
    return lax.ppermute(a, axis, [(i, (i + k) % n) for i in range(n)])


def cross(a, k):
    pairs = []
    for i in range(128):
        x, z, rest = i // 32, i // 8 % 4, i % 8
        if i % 2 == 0:
            x = (x + k) % 4
        else:
            z = (z + k) % 4
        pairs.append((i, x * 32 + z * 8 + rest))
    return lax.ppermute(a, AXES, pairs)


def store(whole, early, late, row, value):
    if whole is None:
        (early if row in (1, 2) else late)[{1: 0, 2: 1, 3: 0, 0: 1}[row]] = value
    else:
        whole[row] = value


def front_kernel(s_ref, g_ref, h_ref, i_ref, w_ref, mine, theirs, *rest):
    outs, t_ref = rest[:-1], rest[-1]
    to_x = (outs[0], outs[1], None, outs[2])
    to_z = (outs[5], outs[6], None, outs[7])
    i = pl.program_id(0)
    for b in range(14):
        cols = slice(b * 128, b * 128 + 128)
        v = 0.5 * g_ref[:, cols].astype(F32)
        w = v * h_ref[:, cols].astype(F32)
        t_ref[cols, :] = (w + w * jnp.tanh(v)).astype(BF16).T
    c = s_ref[2]
    for out, half in ((mine, c), (theirs, 1 - c)):
        start = pl.multiple_of(half * 256, 256)
        part = jnp.dot(i_ref[...], w_ref[:, pl.ds(start, 256)], preferred_element_type=F32)

        @pl.when(i == 0)
        def _():
            out[...] = part

        @pl.when(i > 0)
        def _():
            out[...] += part

    for k in range(4):
        start = pl.multiple_of(lax.rem(s_ref[1] + k, 4) * 448, 448)
        for j in range(4):

            @pl.when(i == j)
            def _():
                store(to_x[j], outs[3], outs[4], k, t_ref[pl.ds(start, 224), :])
                store(to_z[k], outs[8], outs[9], j, t_ref[pl.ds(start + 224, 224), :])


def front(at, gate, hidden, inputs, projector):
    t = gate.shape[0]
    block = pl.BlockSpec((t, 1792), lambda i, s: (0, lax.rem(s[0] + i, 4)))
    whole, part = pltpu.VMEM((4, 224, t), BF16), pltpu.VMEM((2, 224, t), BF16)
    args = [
        pltpu.with_memory_space_constraint(a, pltpu.HBM) for a in (gate, hidden, inputs, projector)
    ]
    return pl.pallas_call(
        front_kernel,
        grid_spec=pltpu.PrefetchScalarGridSpec(
            num_scalar_prefetch=1,
            grid=(4,),
            in_specs=[
                block,
                block,
                pl.BlockSpec((t, 512), lambda i, s: (0, i)),
                pl.BlockSpec((512, 512), lambda i, s: (i, 0)),
            ],
            out_specs=[VMEM] * 12,
            scratch_shapes=[pltpu.VMEM((1792, t), BF16)],
        ),
        out_shape=[pltpu.VMEM((t, 256), F32)] * 2 + [whole, whole, whole, part, part] * 2,
        compiler_params=params(16),
        name="front",
    )(at, *args)


def join_kernel(s_ref, half, other, out):
    c = s_ref[2]
    out[:, pl.ds(pl.multiple_of(c * 256, 256), 256)] = half[...]
    out[:, pl.ds(pl.multiple_of(256 - c * 256, 256), 256)] = other[...]


def join(at, half, other):
    args = [pltpu.with_memory_space_constraint(a, pltpu.VMEM) for a in (half, other)]
    return pl.pallas_call(
        join_kernel,
        in_specs=[SMEM, VMEM, VMEM],
        out_specs=VMEM,
        out_shape=pltpu.VMEM((half.shape[0], 512), BF16),
        compiler_params=params(4),
        name="join",
    )(at, *args)


def hold_kernel(a, b, c, x, y, z, sem):
    copies = [pltpu.make_async_copy(s, d, sem.at[k]) for k, (s, d) in enumerate(((a, x), (b, y), (c, z)))]
    for copy in copies:
        copy.start()
    for copy in copies:
        copy.wait()


def hold(blocks):
    args = [pltpu.with_memory_space_constraint(a, pltpu.HBM) for a in blocks]
    return pl.pallas_call(
        hold_kernel,
        in_specs=[HBM] * 3,
        out_specs=[VMEM] * 3,
        out_shape=[pltpu.VMEM((2048, 512), BF16)] * 3,
        scratch_shapes=[pltpu.SemaphoreType.DMA((3,))],
        compiler_params=params(1),
        name="keep",
    )(*args)


def partial_sums(near, late):
    acc = None
    for piece, coords in near:
        part = jnp.dot(piece.reshape(896, -1), coords, preferred_element_type=F32)
        acc = part if acc is None else acc + part
    acc = lax.optimization_barrier(acc)
    (first, second), coords = late
    rows = {1: first[0], 2: first[1], 3: second[0], 0: second[1]}
    out = {}
    for j in (1, 2, 3, 0):
        part = jnp.dot(rows[j], coords, preferred_element_type=F32)
        part += acc[j * 224 : j * 224 + 224]
        out[j] = part if j == 0 else part.astype(BF16)
    return out


def last_kernel(
    s_ref, mine, got, first, second, w0, w1, w2, w3, new_first, new_second, update,
    w_ref, o_ref, sem, w_sem,
):
    yh, c = s_ref[3], s_ref[2]
    load = pltpu.make_async_copy(w3, w_ref, w_sem)
    load.start()
    projected = mine[...] + got[...].astype(F32)
    m = 0.9 * first[...] + 0.1 * projected
    v = 0.95 * second[...] + 0.05 * projected * projected
    new_first[...] = m
    new_second[...] = v
    root = jnp.sqrt(v * (1.0 / (1.0 - 0.9025)))
    direction = (m * (1.0 / (1.0 - 0.81)) / (root + 1e-08)).astype(BF16)
    blocks = (2 * yh + c, 2 * yh + 1 - c, 2 - 2 * yh + c, 3 - 2 * yh - c)
    stores = []
    for k, w in enumerate((w0, w1, w2, w_ref)):
        if k == 3:
            load.wait()
        part = 4.0 * lax.dot_general(
            direction, w[...], (((1,), (1,)), ((), ())), preferred_element_type=F32
        )
        o_ref[k] = part.astype(BF16)
        cols = pl.ds(pl.multiple_of(blocks[k] * 2048, 2048), 2048)
        out = pltpu.make_async_copy(o_ref.at[k], update.at[:, cols], sem.at[k])
        out.start()
        stores.append(out)
    for out in stores:
        out.wait()


def last_stage(at, mine, got, first, second, held, across):
    rows = first.shape[0]
    moment = jax.ShapeDtypeStruct((rows, 512), F32)
    args = [
        pltpu.with_memory_space_constraint(a, pltpu.VMEM)
        for a in (mine, got, first, second) + tuple(held)
    ]
    return pl.pallas_call(
        last_kernel,
        in_specs=[SMEM] + [VMEM] * 7 + [HBM],
        out_specs=[VMEM, VMEM, HBM],
        out_shape=[moment, moment, jax.ShapeDtypeStruct((rows, 8192), BF16)],
        scratch_shapes=[
            pltpu.VMEM((2048, 512), BF16),
            pltpu.VMEM((4, rows, 2048), BF16),
            pltpu.SemaphoreType.DMA((4,)),
            pltpu.SemaphoreType.DMA,
        ],
        compiler_params=params(12),
        name="last",
    )(at, *args, pltpu.with_memory_space_constraint(across, pltpu.HBM))


def step(inputs, gate_preact, hidden_grad, projector, first_moment, second_moment):
    x, z, yl, yh, c = (lax.axis_index(a).astype(jnp.int32) for a in AXES)
    at = jnp.stack([x, z, c, yh])

    mine, theirs, *pieces = front(at, gate_preact, hidden_grad, inputs, projector)
    got_x, got_z = {}, {}
    for got, parts, axis in ((got_x, pieces[:5], "x"), (got_z, pieces[5:], "z")):
        got[0] = parts[0]
        for key, k, part in (("1", 1, parts[1]), ("3", 3, parts[2]), ("2a", 2, parts[3]), ("2b", 2, parts[4])):
            got[key] = shift(part, axis, k)

    chip_sum = mine + shift(theirs, "c", 1)
    far = shift(chip_sum.astype(BF16), "yh", 1)
    half = (chip_sum + far.astype(F32)).astype(BF16)
    own = join(at, half, shift(half, "c", 1))
    along = {k: cross(own, k) for k in (1, 3, 2)}
    beyond = {k: shift(along[k], "c", 1) for k in (1, 3, 2)}
    coords_x = {k: jnp.where(c == 0, along[k], beyond[k]) for k in (1, 3, 2)}
    coords_z = {k: jnp.where(c == 0, beyond[k], along[k]) for k in (1, 3, 2)}

    near_w = lax.ppermute(projector, ("yl", "yh"), [(0, 3), (3, 0), (1, 2), (2, 1)])
    beside_w = shift(projector, "c", 1)
    across_w = shift(near_w, "c", 1)

    sums = []
    for got, coords, axis in ((got_z, coords_z, "x"), (got_x, coords_x, "z")):
        part = partial_sums(
            [(got[0], own), (got["1"], coords[1]), (got["3"], coords[3])],
            ((got["2a"], got["2b"]), coords[2]),
        )
        total = part[0]
        for k in (1, 2, 3):
            total += shift(part[k], axis, k).astype(F32)
        sums.append(total)
    sum_z, sum_x = sums
    keep = jnp.where(yl == 0, sum_x, sum_z)
    give = jnp.where(yl == 0, sum_z, sum_x).astype(BF16)
    got = shift(give, "yl", 1)
    held = hold((projector, beside_w, near_w))
    return last_stage(at, keep, got, first_moment, second_moment, held, across_w)


def solution(mesh):
    fine = Mesh(mesh.devices.reshape(4, 4, 2, 2, 2), ("x", "z", "yl", "yh", "c"))
    dp, mp = ("x", "z", "yl"), ("yh", "c")
    return jax.shard_map(
        step,
        mesh=fine,
        in_specs=(P(dp, mp), P(dp, mp), P(dp, mp), P(mp, None), P(mp + dp, None), P(mp + dp, None)),
        out_specs=(P(mp + dp, None),) * 3,
        check_vma=False,
    )
```

time: 142 us -> 132 us (0.930)
  the two profiles are of different devices: /device:TPU:4 before, /device:TPU:26 now
where the time goes in v3:
time: 132 us
  waiting for transfers between devices  67.9 us (51%)
  starting transfers between devices  30.7 us (23%)
  Pallas kernels  20.7 us (16%)
  matrix products  8.6 us (7%)
  local copies, waits for them, and re-layouts  2.71 us (2%)
    ppermute x23, waiting for transfers between devices, shift(): return lax.ppermute(a, axis, [(i, (i + k) % n) for i in range(n)])  62.5 us
    ppermute x23, starting transfers between devices, shift(): return lax.ppermute(a, axis, [(i, (i + k) % n) for i in range(n)])  27.9 us
    pallas_call x1, Pallas kernels, front(): pl.pallas_call(front_kernel, grid_spec=pltpu.PrefetchScalarGridSpec(num_s...  9.99 us
    pallas_call x1, Pallas kernels, last_stage(): pl.pallas_call(last_kernel, in_specs=[SMEM] + [VMEM] * 7 + [HBM], out_spe...  7.22 us
    dot_general x6, matrix products, partial_sums(): part = jnp.dot(piece.reshape(896, -1), coords, preferred_element_type=F32)  6.21 us
    ppermute x3, waiting for transfers between devices, cross(): return lax.ppermute(a, AXES, pairs)  5.41 us
    pallas_call x1, Pallas kernels, hold(): pl.pallas_call(hold_kernel, in_specs=[HBM] * 3, out_specs=[VMEM] * 3, out...  2.88 us
    unnamed x20, local copies, waits for them, and re-layouts  2.71 us
  transfers between devices with their start and end apart: 27, of which 15 were waited for; matrix products, arithmetic and copies ran while one was open for 7% of the time, Pallas kernels for 2%

profile of v3, /device:TPU:26, one launch (start us, length us, event | category | flops | bytes accessed | tf_op | source)
XLA Modules:
  0.0 131.9 jit_solution(8964331030312752708)
XLA Ops:
  0.7 10.0 %front.1 = (f32[384,256]{1,0:T(8,128)S(1)}, f32[384,256]{1,0:T(8,128)S(1)}, bf16[4,224,384]{2,1,0:T(8,128)(2,1)S(1)}, bf16[4,224,384]{2,1,0:T(8,128)(2,1)}, bf16...) custom-call(s32[4]{0:T(128)S(1)} %pad_add_fusion.s_ref, ...), custom_call_target="tpu_custom_call" | custom-call | tf_op jit(solution)/shard_map/front/pallas_call | solution.py:86
  10.8 1.7 %collective-permute-done.1 = f32[384,256]{1,0:T(8,128)S(1)} collective-permute-done((f32[384,256]{1,0:T(8,128)S(1)}, f32[384,256]{1,0:T(8,128)S(1)}, u32[]{:S(2)}, u32[]{:S(2)}) %collective-permute-start.1) | collective-permute-done | bytes 393248 | tf_op jit(solution)/shard_map/ppermute | solution.py:24
  13.9 7.2 %collective-permute-done.2 = bf16[384,256]{1,0:T(8,128)(2,1)S(1)} collective-permute-done((bf16[384,256]{1,0:T(8,128)(2,1)S(1)}, bf16[384,256]{1,0:T(8,128)(2,1)S(1)}, u32[]{:S(2)}, u32[]{:S(2)}) %collective-permute-start.2) | collective-permute-done | bytes 196640 | tf_op jit(solution)/shard_map/ppermute | solution.py:24
  23.3 1.6 %collective-permute-start.7 = (bf16[384,512]{1,0:T(8,128)(2,1)S(1)}, bf16[384,512]{1,0:T(8,128)(2,1)}, u32[]{:S(2)}, u32[]{:S(2)}) collective-permute-start(bf16[384,512]{1,0:T(8,128)(2,1)S(1)} %join.1), channel_id=1, source_target_pairs={{0,32},{1,9},{2,34},{3,11},{4,36},{5,13},{6,38},{7,15},{8,40},{9,1... | collective-permute-start | bytes 1179656 | tf_op jit(solution)/shard_map/ppermute | solution.py:36
  26.2 1.9 %collective-permute-start.17 = (bf16[4,224,384]{2,1,0:T(8,128)(2,1)}, bf16[4,224,384]{2,1,0:T(8,128)(2,1)}, u32[]{:S(2)}, u32[]{:S(2)}) collective-permute-start(bf16[4,224,384]{2,1,0:T(8,128)(2,1)} %get-tuple-element.27), channel_id=1, source_target_pairs={{0,8},{8,16},{16,24},{24,0},{1,9},{9,17},{17,25},{25,1},{2,10},{10... | collective-permute-start | bytes 2064392 | tf_op jit(solution)/shard_map/ppermute | solution.py:24
  29.0 5.4 %collective-permute-done.7 = bf16[384,512]{1,0:T(8,128)(2,1)} collective-permute-done((bf16[384,512]{1,0:T(8,128)(2,1)S(1)}, bf16[384,512]{1,0:T(8,128)(2,1)}, u32[]{:S(2)}, u32[]{:S(2)}) %collective-permute-start.7) | collective-permute-done | bytes 393248 | tf_op jit(solution)/shard_map/ppermute | solution.py:36
  35.0 10.9 %collective-permute-done.6 = bf16[4,224,384]{2,1,0:T(8,128)(2,1)} collective-permute-done((bf16[4,224,384]{2,1,0:T(8,128)(2,1)}, bf16[4,224,384]{2,1,0:T(8,128)(2,1)}, u32[]{:S(2)}, u32[]{:S(2)}) %collective-permute-start.6) | collective-permute-done | bytes 688160 | tf_op jit(solution)/shard_map/ppermute | solution.py:24
  46.0 1.7 %collective-permute-start.9 = (bf16[4,224,384]{2,1,0:T(8,128)(2,1)S(1)}, bf16[4,224,384]{2,1,0:T(8,128)(2,1)S(1)}, u32[]{:S(2)}, u32[]{:S(2)}) collective-permute-start(bf16[4,224,384]{2,1,0:T(8,128)(2,1)S(1)} %get-tuple-element.23), channel_id=1, source_target_pairs={{0,96},{32,0},{64,32},{96,64},{1,97},{33,1},{65,33},{97,65},{2,98}... | collective-permute-start | bytes 2064392 | tf_op jit(solution)/shard_map/ppermute | solution.py:24
  48.9 1.9 %fusion.16 = f32[896,512]{1,0:T(8,128)S(1)} fusion(bf16[896,384]{1,0:T(8,128)(2,1)} %bitcast.6, bf16[384,512]{1,0:T(8,128)(2,1)} %collective-permute-done.7, bf16[384,512]{1,0:T(8,128)(2,1)S(1)} %collective-permute-done.8, pred[]{:T(512)S(6)} %eq.5), kind=kOutput, calls=%fused_computation.27 | convolution fusion | flops 352518144 | bytes 3309569 | tf_op jit(solution)/shard_map/dot_general | solution.py:148
  50.8 3.6 %collective-permute-start.18 = (bf16[4,224,384]{2,1,0:T(8,128)(2,1)S(1)}, bf16[4,224,384]{2,1,0:T(8,128)(2,1)S(1)}, u32[]{:S(2)}, u32[]{:S(2)}) collective-permute-start(bf16[4,224,384]{2,1,0:T(8,128)(2,1)S(1)} %get-tuple-element.28), channel_id=1, source_target_pairs={{0,24},{8,0},{16,8},{24,16},{1,25},{9,1},{17,9},{25,17},{2,26},{10... | collective-permute-start | bytes 2064392 | tf_op jit(solution)/shard_map/ppermute | solution.py:24
  54.4 1.8 %fusion.13 = f32[896,512]{1,0:T(8,128)S(1)} fusion(bf16[896,384]{1,0:T(8,128)(2,1)} %bitcast.13, bf16[384,512]{1,0:T(8,128)(2,1)S(1)} %collective-permute-done.8, bf16[384,512]{1,0:T(8,128)(2,1)} %collective-permute-done.7, pred[]{:T(512)S(6)} %eq.5), kind=kOutput, calls=%fused_computation.24 | convolution fusion | flops 352518144 | bytes 3309569 | tf_op jit(solution)/shard_map/dot_general | solution.py:148
  56.2 4.1 %collective-permute-done.9 = bf16[4,224,384]{2,1,0:T(8,128)(2,1)S(1)} collective-permute-done((bf16[4,224,384]{2,1,0:T(8,128)(2,1)S(1)}, bf16[4,224,384]{2,1,0:T(8,128)(2,1)S(1)}, u32[]{:S(2)}, u32[]{:S(2)}) %collective-permute-start.9) | collective-permute-done | bytes 688160 | tf_op jit(solution)/shard_map/ppermute | solution.py:24
  60.2 3.3 %collective-permute-start.12 = (bf16[2,224,384]{2,1,0:T(8,128)(2,1)S(1)}, bf16[2,224,384]{2,1,0:T(8,128)(2,1)S(1)}, u32[]{:S(2)}, u32[]{:S(2)}) collective-permute-start(bf16[2,224,384]{2,1,0:T(8,128)(2,1)S(1)} %copy-done.5), channel_id=1, source_target_pairs={{0,64},{32,96},{64,0},{96,32},{1,65},{33,97},{65,1},{97,33},{2,66}... | collective-permute-start | bytes 1032200 | tf_op jit(solution)/shard_map/ppermute | solution.py:24
  64.5 9.0 %collective-permute-done.18 = bf16[4,224,384]{2,1,0:T(8,128)(2,1)S(1)} collective-permute-done((bf16[4,224,384]{2,1,0:T(8,128)(2,1)S(1)}, bf16[4,224,384]{2,1,0:T(8,128)(2,1)S(1)}, u32[]{:S(2)}, u32[]{:S(2)}) %collective-permute-start.18) | collective-permute-done | bytes 688160 | tf_op jit(solution)/shard_map/ppermute | solution.py:24
  75.3 2.9 %collective-permute-start = (bf16[2,224,384]{2,1,0:T(8,128)(2,1)S(1)}, bf16[2,224,384]{2,1,0:T(8,128)(2,1)S(1)}, u32[]{:S(2)}, u32[]{:S(2)}) collective-permute-start(bf16[2,224,384]{2,1,0:T(8,128)(2,1)S(1)} %get-tuple-element.18), channel_id=1, source_target_pairs={{0,64},{32,96},{64,0},{96,32},{1,65},{33,97},{65,1},{97,33},{2,66}... | collective-permute-start | bytes 1032200 | tf_op jit(solution)/shard_map/ppermute | solution.py:24
  78.3 5.7 %collective-permute-done.19 = bf16[2,224,384]{2,1,0:T(8,128)(2,1)S(1)} collective-permute-done((bf16[2,224,384]{2,1,0:T(8,128)(2,1)S(1)}, bf16[2,224,384]{2,1,0:T(8,128)(2,1)S(1)}, u32[]{:S(2)}, u32[]{:S(2)}) %collective-permute-start.19) | collective-permute-done | bytes 344096 | tf_op jit(solution)/shard_map/ppermute | solution.py:24
  85.7 7.9 %collective-permute-done.16 = bf16[2,224,384]{2,1,0:T(8,128)(2,1)S(1)} collective-permute-done((bf16[2,224,384]{2,1,0:T(8,128)(2,1)S(1)}, bf16[2,224,384]{2,1,0:T(8,128)(2,1)S(1)}, u32[]{:S(2)}, u32[]{:S(2)}) %collective-permute-start.16) | collective-permute-done | bytes 344096 | tf_op jit(solution)/shard_map/ppermute | solution.py:24
  96.7 2.1 %collective-permute-start.13 = (bf16[224,512]{1,0:T(8,128)(2,1)S(1)}, bf16[224,512]{1,0:T(8,128)(2,1)S(1)}, u32[]{:S(2)}, u32[]{:S(2)}) collective-permute-start(bf16[224,512]{1,0:T(8,128)(2,1)S(1)} %fusion.6), channel_id=1, source_target_pairs={{0,8},{8,16},{16,24},{24,0},{1,9},{9,17},{17,25},{25,1},{2,10},{10... | collective-permute-start | bytes 688136 | tf_op jit(solution)/shard_map/ppermute | solution.py:24
  98.9 3.6 %collective-permute-done.21 = bf16[224,512]{1,0:T(8,128)(2,1)S(1)} collective-permute-done((bf16[224,512]{1,0:T(8,128)(2,1)S(1)}, bf16[224,512]{1,0:T(8,128)(2,1)S(1)}, u32[]{:S(2)}, u32[]{:S(2)}) %collective-permute-start.21) | collective-permute-done | bytes 229408 | tf_op jit(solution)/shard_map/ppermute | solution.py:24
  104.8 4.4 %collective-permute-start.15 = (bf16[224,512]{1,0:T(8,128)(2,1)S(1)}, bf16[224,512]{1,0:T(8,128)(2,1)S(1)}, u32[]{:S(2)}, u32[]{:S(2)}) collective-permute-start(bf16[224,512]{1,0:T(8,128)(2,1)S(1)} %fusion.8), channel_id=1, source_target_pairs={{0,24},{8,0},{16,8},{24,16},{1,25},{9,1},{17,9},{25,17},{2,26},{10... | collective-permute-start | bytes 688136 | tf_op jit(solution)/shard_map/ppermute | solution.py:24
  110.0 5.7 %collective-permute-done.15 = bf16[224,512]{1,0:T(8,128)(2,1)S(1)} collective-permute-done((bf16[224,512]{1,0:T(8,128)(2,1)S(1)}, bf16[224,512]{1,0:T(8,128)(2,1)S(1)}, u32[]{:S(2)}, u32[]{:S(2)}) %collective-permute-start.15) | collective-permute-done | bytes 229408 | tf_op jit(solution)/shard_map/ppermute | solution.py:24
  117.9 2.9 %keep.1 = (bf16[2048,512]{1,0:T(8,128)(2,1)S(1)}, bf16[2048,512]{1,0:T(8,128)(2,1)S(1)}, bf16[2048,512]{1,0:T(8,128)(2,1)S(1)}) custom-call(bf16[2048,512]{1,0:T(8,128)(2,1)} %a.1, bf16[2048,512]{1,0:T(8,128)(2,1)} %copy-done.8, bf16[2048,512]{1,0:T(8,128)(2,1)} %collective-permute-done.25.c), custom_call_target="tpu_custom_call" | custom-call | tf_op jit(solution)/shard_map/keep/pallas_call | solution.py:134
  120.8 2.3 %collective-permute-done.23.got = bf16[224,512]{1,0:T(8,128)(2,1)S(1)} collective-permute-done((bf16[224,512]{1,0:T(8,128)(2,1)S(1)}, bf16[224,512]{1,0:T(8,128)(2,1)S(1)}, u32[]{:S(2)}, u32[]{:S(2)}) %collective-permute-start.23) | collective-permute-done | bytes 229408 | tf_op jit(solution)/shard_map/ppermute | solution.py:24
  124.5 7.2 %last.1 = (f32[224,512]{1,0:T(8,128)}, f32[224,512]{1,0:T(8,128)}, bf16[224,8192]{1,0:T(8,128)(2,1)}) custom-call(s32[4]{0:T(128)S(1)} %pad_add_fusion.s_ref, f32[224,512]{1,0:T(8,128)S(1)} %get-tuple-element.37.mine, bf16[224,512]{1,0:T(8,128)(2,1)S(1)} %collective-permute-done.23.got, f32[224,512]{1,0:T(8,128)S(1)} %copy-done, f32[224,512]{1,0:T(8,128)S(1)} %copy-done.1, ...), custom_call_target="tpu_custom_call" | custom-call | tf_op jit(solution)/shard_map/last/pallas_call | solution.py:199
  (73 shorter events, 22.0 us)
Async XLA Ops:
  12.6 8.5 %collective-permute-start.2 = (bf16[384,256]{1,0:T(8,128)(2,1)S(1)}, bf16[384,256]{1,0:T(8,128)(2,1)S(1)}, u32[]{:S(2)}, u32[]{:S(2)}) collective-permute-start(bf16[384,256]{1,0:T(8,128)(2,1)S(1)} %get-tuple-element.33), channel_id=1, source_target_pairs={{0,2},{2,0},{1,3},{3,1},{4,6},{6,4},{5,7},{7,5},{8,10},{10,8},{9,1... | collective-permute-start | bytes 589832 | tf_op jit(solution)/shard_map/ppermute | solution.py:24
  23.3 11.1 %collective-permute-start.7 = (bf16[384,512]{1,0:T(8,128)(2,1)S(1)}, bf16[384,512]{1,0:T(8,128)(2,1)}, u32[]{:S(2)}, u32[]{:S(2)}) collective-permute-start(bf16[384,512]{1,0:T(8,128)(2,1)S(1)} %join.1), channel_id=1, source_target_pairs={{0,32},{1,9},{2,34},{3,11},{4,36},{5,13},{6,38},{7,15},{8,40},{9,1... | collective-permute-start | bytes 1179656 | tf_op jit(solution)/shard_map/ppermute | solution.py:36
  24.8 21.1 %collective-permute-start.6 = (bf16[4,224,384]{2,1,0:T(8,128)(2,1)}, bf16[4,224,384]{2,1,0:T(8,128)(2,1)}, u32[]{:S(2)}, u32[]{:S(2)}) collective-permute-start(bf16[4,224,384]{2,1,0:T(8,128)(2,1)} %get-tuple-element.22), channel_id=1, source_target_pairs={{0,32},{32,64},{64,96},{96,0},{1,33},{33,65},{65,97},{97,1},{2,34}... | collective-permute-start | bytes 2064392 | tf_op jit(solution)/shard_map/ppermute | solution.py:24
  26.0 58.9 %collective-permute-start.25 = (bf16[2048,512]{1,0:T(8,128)(2,1)}, bf16[2048,512]{1,0:T(8,128)(2,1)}, u32[]{:S(2)}, u32[]{:S(2)}) collective-permute-start(bf16[2048,512]{1,0:T(8,128)(2,1)} %a.1), channel_id=1, source_target_pairs={{0,6},{6,0},{2,4},{4,2},{1,7},{7,1},{3,5},{5,3},{8,14},{14,8},{10,... | collective-permute-start | bytes 6291464 | tf_op jit(solution)/shard_map/ppermute | solution.py:235
  26.2 24.6 %collective-permute-start.17 = (bf16[4,224,384]{2,1,0:T(8,128)(2,1)}, bf16[4,224,384]{2,1,0:T(8,128)(2,1)}, u32[]{:S(2)}, u32[]{:S(2)}) collective-permute-start(bf16[4,224,384]{2,1,0:T(8,128)(2,1)} %get-tuple-element.27), channel_id=1, source_target_pairs={{0,8},{8,16},{16,24},{24,0},{1,9},{9,17},{17,25},{25,1},{2,10},{10... | collective-permute-start | bytes 2064392 | tf_op jit(solution)/shard_map/ppermute | solution.py:24
  28.2 20.2 %collective-permute-start.10 = (bf16[384,512]{1,0:T(8,128)(2,1)S(1)}, bf16[384,512]{1,0:T(8,128)(2,1)S(1)}, u32[]{:S(2)}, u32[]{:S(2)}) collective-permute-start(bf16[384,512]{1,0:T(8,128)(2,1)S(1)} %join.1), channel_id=1, source_target_pairs={{0,96},{1,25},{2,98},{3,27},{4,100},{5,29},{6,102},{7,31},{8,104},... | collective-permute-start | bytes 1179656 | tf_op jit(solution)/shard_map/ppermute | solution.py:36
  34.4 14.0 %collective-permute-start.8 = (bf16[384,512]{1,0:T(8,128)(2,1)}, bf16[384,512]{1,0:T(8,128)(2,1)S(1)}, u32[]{:S(2)}, u32[]{:S(2)}) collective-permute-start(bf16[384,512]{1,0:T(8,128)(2,1)} %collective-permute-done.7), channel_id=1, source_target_pairs={{0,1},{1,0},{2,3},{3,2},{4,5},{5,4},{6,7},{7,6},{8,9},{9,8},{10,11... | collective-permute-start | bytes 1179656 | tf_op jit(solution)/shard_map/ppermute | solution.py:24
  46.0 14.3 %collective-permute-start.9 = (bf16[4,224,384]{2,1,0:T(8,128)(2,1)S(1)}, bf16[4,224,384]{2,1,0:T(8,128)(2,1)S(1)}, u32[]{:S(2)}, u32[]{:S(2)}) collective-permute-start(bf16[4,224,384]{2,1,0:T(8,128)(2,1)S(1)} %get-tuple-element.23), channel_id=1, source_target_pairs={{0,96},{32,0},{64,32},{96,64},{1,97},{33,1},{65,33},{97,65},{2,98}... | collective-permute-start | bytes 2064392 | tf_op jit(solution)/shard_map/ppermute | solution.py:24
  48.3 68.3 %collective-permute-start.24 = (bf16[2048,512]{1,0:T(8,128)(2,1)}, bf16[2048,512]{1,0:T(8,128)(2,1)S(1)}, u32[]{:S(2)}, u32[]{:S(2)}) collective-permute-start(bf16[2048,512]{1,0:T(8,128)(2,1)} %a.1), channel_id=1, source_target_pairs={{0,1},{1,0},{2,3},{3,2},{4,5},{5,4},{6,7},{7,6},{8,9},{9,8},{10,11... | collective-permute-start | bytes 6291464 | tf_op jit(solution)/shard_map/ppermute | solution.py:24
  48.5 15.1 %collective-permute-start.11 = (bf16[384,512]{1,0:T(8,128)(2,1)S(1)}, bf16[384,512]{1,0:T(8,128)(2,1)S(1)}, u32[]{:S(2)}, u32[]{:S(2)}) collective-permute-start(bf16[384,512]{1,0:T(8,128)(2,1)S(1)} %collective-permute-done.10), channel_id=1, source_target_pairs={{0,1},{1,0},{2,3},{3,2},{4,5},{5,4},{6,7},{7,6},{8,9},{9,8},{10,11... | collective-permute-start | bytes 1179656 | tf_op jit(solution)/shard_map/ppermute | solution.py:24
  50.8 22.7 %collective-permute-start.18 = (bf16[4,224,384]{2,1,0:T(8,128)(2,1)S(1)}, bf16[4,224,384]{2,1,0:T(8,128)(2,1)S(1)}, u32[]{:S(2)}, u32[]{:S(2)}) collective-permute-start(bf16[4,224,384]{2,1,0:T(8,128)(2,1)S(1)} %get-tuple-element.28), channel_id=1, source_target_pairs={{0,24},{8,0},{16,8},{24,16},{1,25},{9,1},{17,9},{25,17},{2,26},{10... | collective-permute-start | bytes 2064392 | tf_op jit(solution)/shard_map/ppermute | solution.py:24
  60.2 24.3 %collective-permute-start.12 = (bf16[2,224,384]{2,1,0:T(8,128)(2,1)S(1)}, bf16[2,224,384]{2,1,0:T(8,128)(2,1)S(1)}, u32[]{:S(2)}, u32[]{:S(2)}) collective-permute-start(bf16[2,224,384]{2,1,0:T(8,128)(2,1)S(1)} %copy-done.5), channel_id=1, source_target_pairs={{0,64},{32,96},{64,0},{96,32},{1,65},{33,97},{65,1},{97,33},{2,66}... | collective-permute-start | bytes 1032200 | tf_op jit(solution)/shard_map/ppermute | solution.py:24
  63.6 9.9 %collective-permute-start.4 = (bf16[384,512]{1,0:T(8,128)(2,1)S(1)}, bf16[384,512]{1,0:T(8,128)(2,1)S(1)}, u32[]{:S(2)}, u32[]{:S(2)}) collective-permute-start(bf16[384,512]{1,0:T(8,128)(2,1)S(1)} %join.1), channel_id=1, source_target_pairs={{0,64},{1,17},{2,66},{3,19},{4,68},{5,21},{6,70},{7,23},{8,72},{9,... | collective-permute-start | bytes 1179656 | tf_op jit(solution)/shard_map/ppermute | solution.py:36
  73.5 10.5 %collective-permute-start.19 = (bf16[2,224,384]{2,1,0:T(8,128)(2,1)S(1)}, bf16[2,224,384]{2,1,0:T(8,128)(2,1)S(1)}, u32[]{:S(2)}, u32[]{:S(2)}) collective-permute-start(bf16[2,224,384]{2,1,0:T(8,128)(2,1)S(1)} %copy-done.7), channel_id=1, source_target_pairs={{0,16},{8,24},{16,0},{24,8},{1,17},{9,25},{17,1},{25,9},{2,18},{10... | collective-permute-start | bytes 1032200 | tf_op jit(solution)/shard_map/ppermute | solution.py:24
  75.3 19.8 %collective-permute-start = (bf16[2,224,384]{2,1,0:T(8,128)(2,1)S(1)}, bf16[2,224,384]{2,1,0:T(8,128)(2,1)S(1)}, u32[]{:S(2)}, u32[]{:S(2)}) collective-permute-start(bf16[2,224,384]{2,1,0:T(8,128)(2,1)S(1)} %get-tuple-element.18), channel_id=1, source_target_pairs={{0,64},{32,96},{64,0},{96,32},{1,65},{33,97},{65,1},{97,33},{2,66}... | collective-permute-start | bytes 1032200 | tf_op jit(solution)/shard_map/ppermute | solution.py:24
  84.0 9.6 %collective-permute-start.16 = (bf16[2,224,384]{2,1,0:T(8,128)(2,1)S(1)}, bf16[2,224,384]{2,1,0:T(8,128)(2,1)S(1)}, u32[]{:S(2)}, u32[]{:S(2)}) collective-permute-start(bf16[2,224,384]{2,1,0:T(8,128)(2,1)S(1)} %copy-done.3), channel_id=1, source_target_pairs={{0,16},{8,24},{16,0},{24,8},{1,17},{9,25},{17,1},{25,9},{2,18},{10... | collective-permute-start | bytes 1032200 | tf_op jit(solution)/shard_map/ppermute | solution.py:24
  84.6 12.2 %collective-permute-start.20 = (bf16[224,512]{1,0:T(8,128)(2,1)S(1)}, bf16[224,512]{1,0:T(8,128)(2,1)S(1)}, u32[]{:S(2)}, u32[]{:S(2)}) collective-permute-start(bf16[224,512]{1,0:T(8,128)(2,1)S(1)} %fusion.9), channel_id=1, source_target_pairs={{0,32},{32,64},{64,96},{96,0},{1,33},{33,65},{65,97},{97,1},{2,34}... | collective-permute-start | bytes 688136 | tf_op jit(solution)/shard_map/ppermute | solution.py:24
  84.9 38.3 %collective-permute-start.26 = (bf16[2048,512]{1,0:T(8,128)(2,1)}, bf16[2048,512]{1,0:T(8,128)(2,1)S(1)}, u32[]{:S(2)}, u32[]{:S(2)}) collective-permute-start(bf16[2048,512]{1,0:T(8,128)(2,1)} %collective-permute-done.25.c), channel_id=1, source_target_pairs={{0,1},{1,0},{2,3},{3,2},{4,5},{5,4},{6,7},{7,6},{8,9},{9,8},{10,11... | collective-permute-start | bytes 6291464 | tf_op jit(solution)/shard_map/ppermute | solution.py:24
  93.6 8.9 %collective-permute-start.21 = (bf16[224,512]{1,0:T(8,128)(2,1)S(1)}, bf16[224,512]{1,0:T(8,128)(2,1)S(1)}, u32[]{:S(2)}, u32[]{:S(2)}) collective-permute-start(bf16[224,512]{1,0:T(8,128)(2,1)S(1)} %fusion.10), channel_id=1, source_target_pairs={{0,64},{32,96},{64,0},{96,32},{1,65},{33,97},{65,1},{97,33},{2,66}... | collective-permute-start | bytes 688136 | tf_op jit(solution)/shard_map/ppermute | solution.py:24
  95.1 9.7 %collective-permute-start.22 = (bf16[224,512]{1,0:T(8,128)(2,1)S(1)}, bf16[224,512]{1,0:T(8,128)(2,1)S(1)}, u32[]{:S(2)}, u32[]{:S(2)}) collective-permute-start(bf16[224,512]{1,0:T(8,128)(2,1)S(1)} %fusion.11), channel_id=1, source_target_pairs={{0,96},{32,0},{64,32},{96,64},{1,97},{33,1},{65,33},{97,65},{2,98}... | collective-permute-start | bytes 688136 | tf_op jit(solution)/shard_map/ppermute | solution.py:24
  96.7 12.9 %collective-permute-start.13 = (bf16[224,512]{1,0:T(8,128)(2,1)S(1)}, bf16[224,512]{1,0:T(8,128)(2,1)S(1)}, u32[]{:S(2)}, u32[]{:S(2)}) collective-permute-start(bf16[224,512]{1,0:T(8,128)(2,1)S(1)} %fusion.6), channel_id=1, source_target_pairs={{0,8},{8,16},{16,24},{24,0},{1,9},{9,17},{17,25},{25,1},{2,10},{10... | collective-permute-start | bytes 688136 | tf_op jit(solution)/shard_map/ppermute | solution.py:24
  102.5 7.5 %collective-permute-start.14 = (bf16[224,512]{1,0:T(8,128)(2,1)S(1)}, bf16[224,512]{1,0:T(8,128)(2,1)S(1)}, u32[]{:S(2)}, u32[]{:S(2)}) collective-permute-start(bf16[224,512]{1,0:T(8,128)(2,1)S(1)} %fusion.7), channel_id=1, source_target_pairs={{0,16},{8,24},{16,0},{24,8},{1,17},{9,25},{17,1},{25,9},{2,18},{10... | collective-permute-start | bytes 688136 | tf_op jit(solution)/shard_map/ppermute | solution.py:24
  104.8 10.9 %collective-permute-start.15 = (bf16[224,512]{1,0:T(8,128)(2,1)S(1)}, bf16[224,512]{1,0:T(8,128)(2,1)S(1)}, u32[]{:S(2)}, u32[]{:S(2)}) collective-permute-start(bf16[224,512]{1,0:T(8,128)(2,1)S(1)} %fusion.8), channel_id=1, source_target_pairs={{0,24},{8,0},{16,8},{24,16},{1,25},{9,1},{17,9},{25,17},{2,26},{10... | collective-permute-start | bytes 688136 | tf_op jit(solution)/shard_map/ppermute | solution.py:24
  116.2 7.0 %collective-permute-start.23 = (bf16[224,512]{1,0:T(8,128)(2,1)S(1)}, bf16[224,512]{1,0:T(8,128)(2,1)S(1)}, u32[]{:S(2)}, u32[]{:S(2)}) collective-permute-start(bf16[224,512]{1,0:T(8,128)(2,1)S(1)} %select_convert_fusion), channel_id=1, source_target_pairs={{0,4},{4,0},{1,5},{5,1},{2,6},{6,2},{3,7},{7,3},{8,12},{12,8},{9,1... | collective-permute-start | bytes 688136 | tf_op jit(solution)/shard_map/ppermute | solution.py:24
  (13 other events, 94.9 us)

commit v4 on v3

--- a/solution.py
+++ b/solution.py
@@ -36,17 +36,9 @@
     return lax.ppermute(a, AXES, pairs)
 
 
-def store(whole, early, late, row, value):
-    if whole is None:
-        (early if row in (1, 2) else late)[{1: 0, 2: 1, 3: 0, 0: 1}[row]] = value
-    else:
-        whole[row] = value
-
-
 def front_kernel(s_ref, g_ref, h_ref, i_ref, w_ref, mine, theirs, *rest):
     outs, t_ref = rest[:-1], rest[-1]
-    to_x = (outs[0], outs[1], None, outs[2])
-    to_z = (outs[5], outs[6], None, outs[7])
+    to_x, to_z = outs[:4], outs[4:]
     i = pl.program_id(0)
     for b in range(14):
         cols = slice(b * 128, b * 128 + 128)
@@ -68,18 +60,17 @@
 
     for k in range(4):
         start = pl.multiple_of(lax.rem(s_ref[1] + k, 4) * 448, 448)
+        to_z[k][i] = t_ref[pl.ds(start + 224, 224), :]
         for j in range(4):
 
             @pl.when(i == j)
             def _():
-                store(to_x[j], outs[3], outs[4], k, t_ref[pl.ds(start, 224), :])
-                store(to_z[k], outs[8], outs[9], j, t_ref[pl.ds(start + 224, 224), :])
+                to_x[j][k] = t_ref[pl.ds(start, 224), :]
 
 
 def front(at, gate, hidden, inputs, projector):
     t = gate.shape[0]
     block = pl.BlockSpec((t, 1792), lambda i, s: (0, lax.rem(s[0] + i, 4)))
-    whole, part = pltpu.VMEM((4, 224, t), BF16), pltpu.VMEM((2, 224, t), BF16)
     args = [
         pltpu.with_memory_space_constraint(a, pltpu.HBM) for a in (gate, hidden, inputs, projector)
     ]
@@ -94,10 +85,10 @@
                 pl.BlockSpec((t, 512), lambda i, s: (0, i)),
                 pl.BlockSpec((512, 512), lambda i, s: (i, 0)),
             ],
-            out_specs=[VMEM] * 12,
+            out_specs=[VMEM] * 10,
             scratch_shapes=[pltpu.VMEM((1792, t), BF16)],
         ),
-        out_shape=[pltpu.VMEM((t, 256), F32)] * 2 + [whole, whole, whole, part, part] * 2,
+        out_shape=[pltpu.VMEM((t, 256), F32)] * 2 + [pltpu.VMEM((4, 224, t), BF16)] * 8,
         compiler_params=params(16),
         name="front",
     )(at, *args)
@@ -142,20 +133,84 @@
     )(*args)
 
 
-def partial_sums(near, late):
-    acc = None
-    for piece, coords in near:
-        part = jnp.dot(piece.reshape(896, -1), coords, preferred_element_type=F32)
-        acc = part if acc is None else acc + part
-    acc = lax.optimization_barrier(acc)
-    (first, second), coords = late
-    rows = {1: first[0], 2: first[1], 3: second[0], 0: second[1]}
-    out = {}
-    for j in (1, 2, 3, 0):
-        part = jnp.dot(rows[j], coords, preferred_element_type=F32)
-        part += acc[j * 224 : j * 224 + 224]
-        out[j] = part if j == 0 else part.astype(BF16)
-    return out
+def early_kernel(s_ref, g0, g1, g3, c0, along1, beyond1, along3, beyond3, out, rhs):
+    q = pl.program_id(0)
+
+    @pl.when(q == 0)
+    def _():
+        rhs[0:384, :] = c0[...]
+
+    for pick, ones, threes in ((0, along1, along3), (1, beyond1, beyond3)):
+
+        @pl.when((q == 0) & (s_ref[0] == pick))
+        def _():
+            rhs[384:768, :] = ones[...]
+            rhs[768:1152, :] = threes[...]
+
+    lhs = jnp.concatenate([g0[0], g1[0], g3[0]], axis=1)
+    out[q] = jnp.dot(lhs, rhs[...], preferred_element_type=F32)
+
+
+def early_sums(pick, pieces, coords):
+    t = pieces[0].shape[-1]
+    piece = pl.BlockSpec((1, 224, t), lambda q, s: (q, 0, 0))
+    whole = pl.BlockSpec((t, 512), lambda q, s: (0, 0))
+    return pl.pallas_call(
+        early_kernel,
+        grid_spec=pltpu.PrefetchScalarGridSpec(
+            num_scalar_prefetch=1,
+            grid=(4,),
+            in_specs=[piece] * 3 + [whole] * 5,
+            out_specs=VMEM,
+            scratch_shapes=[pltpu.VMEM((3 * t, 512), BF16)],
+        ),
+        out_shape=pltpu.VMEM((4, 224, 512), F32),
+        compiler_params=params(10),
+    )(pick.reshape(1), *pieces, *coords)
+
+
+def late_kernel(s_ref, acc, g2, along, beyond, o0, o1, o2, o3, rhs):
+    for pick, ref in ((0, along), (1, beyond)):
+
+        @pl.when(s_ref[0] == pick)
+        def _():
+            rhs[...] = ref[...]
+
+    for j, out in enumerate((o0, o1, o2, o3)):
+        part = acc[j] + jnp.dot(g2[j], rhs[...], preferred_element_type=F32)
+        out[...] = part.astype(out.dtype)
+
+
+def late_sums(pick, acc, piece, coords):
+    t = piece.shape[-1]
+    return pl.pallas_call(
+        late_kernel,
+        in_specs=[SMEM] + [VMEM] * 4,
+        out_specs=[VMEM] * 4,
+        out_shape=[pltpu.VMEM((224, 512), F32)] + [pltpu.VMEM((224, 512), BF16)] * 3,
+        scratch_shapes=[pltpu.VMEM((t, 512), BF16)],
+        compiler_params=params(6),
+    )(pick.reshape(1), pltpu.with_memory_space_constraint(acc, pltpu.VMEM), piece, *coords)
+
+
+def combine_kernel(s_ref, x0, x1, x2, x3, z0, z1, z2, z3, keep, give):
+    sum_x = x0[...] + x1[...].astype(F32) + x2[...].astype(F32) + x3[...].astype(F32)
+    sum_z = z0[...] + z1[...].astype(F32) + z2[...].astype(F32) + z3[...].astype(F32)
+    here = s_ref[0] == 0
+    keep[...] = jnp.where(here, sum_x, sum_z)
+    give[...] = jnp.where(here, sum_z, sum_x).astype(BF16)
+
+
+def combine(yl, parts_x, parts_z):
+    own = [pltpu.with_memory_space_constraint(p[0], pltpu.VMEM) for p in (parts_x, parts_z)]
+    return pl.pallas_call(
+        combine_kernel,
+        in_specs=[SMEM] + [VMEM] * 8,
+        out_specs=[VMEM] * 2,
+        out_shape=[pltpu.VMEM((224, 512), F32), pltpu.VMEM((224, 512), BF16)],
+        compiler_params=params(4),
+        name="combine",
+    )(yl.reshape(1), own[0], *parts_x[1:], own[1], *parts_z[1:])
 
 
 def last_kernel(
@@ -217,11 +272,8 @@
     at = jnp.stack([x, z, c, yh])
 
     mine, theirs, *pieces = front(at, gate_preact, hidden_grad, inputs, projector)
-    got_x, got_z = {}, {}
-    for got, parts, axis in ((got_x, pieces[:5], "x"), (got_z, pieces[5:], "z")):
-        got[0] = parts[0]
-        for key, k, part in (("1", 1, parts[1]), ("3", 3, parts[2]), ("2a", 2, parts[3]), ("2b", 2, parts[4])):
-            got[key] = shift(part, axis, k)
+    got_x = [pieces[0]] + [shift(pieces[k], "x", k) for k in (1, 2, 3)]
+    got_z = [pieces[4]] + [shift(pieces[4 + k], "z", k) for k in (1, 2, 3)]
 
     chip_sum = mine + shift(theirs, "c", 1)
     far = shift(chip_sum.astype(BF16), "yh", 1)
@@ -229,26 +281,19 @@
     own = join(at, half, shift(half, "c", 1))
     along = {k: cross(own, k) for k in (1, 3, 2)}
     beyond = {k: shift(along[k], "c", 1) for k in (1, 3, 2)}
-    coords_x = {k: jnp.where(c == 0, along[k], beyond[k]) for k in (1, 3, 2)}
-    coords_z = {k: jnp.where(c == 0, beyond[k], along[k]) for k in (1, 3, 2)}
 
     near_w = lax.ppermute(projector, ("yl", "yh"), [(0, 3), (3, 0), (1, 2), (2, 1)])
     beside_w = shift(projector, "c", 1)
     across_w = shift(near_w, "c", 1)
 
-    sums = []
-    for got, coords, axis in ((got_z, coords_z, "x"), (got_x, coords_x, "z")):
-        part = partial_sums(
-            [(got[0], own), (got["1"], coords[1]), (got["3"], coords[3])],
-            ((got["2a"], got["2b"]), coords[2]),
-        )
-        total = part[0]
-        for k in (1, 2, 3):
-            total += shift(part[k], axis, k).astype(F32)
-        sums.append(total)
-    sum_z, sum_x = sums
-    keep = jnp.where(yl == 0, sum_x, sum_z)
-    give = jnp.where(yl == 0, sum_z, sum_x).astype(BF16)
+    parts = []
+    for got, pick, axis in ((got_z, 1 - c, "x"), (got_x, c, "z")):
+        near = (own, along[1], beyond[1], along[3], beyond[3])
+        acc = early_sums(pick, (got[0], got[1], got[3]), near)
+        part = late_sums(pick, acc, got[2], (along[2], beyond[2]))
+        parts.append([part[0]] + [shift(part[k], axis, k) for k in (1, 2, 3)])
+    parts_z, parts_x = parts
+    keep, give = combine(yl, parts_x, parts_z)
     got = shift(give, "yl", 1)
     held = hold((projector, beside_w, near_w))
     return last_stage(at, keep, got, first_moment, second_moment, held, across_w)

time: 132 us -> 139 us (1.053)
  the two profiles are of different devices: /device:TPU:26 before, /device:TPU:32 now
where the time goes in v4:
time: 139 us; the launch traced here: 138 us
  waiting for transfers between devices  66.6 us (48%)
  starting transfers between devices  30 us (22%)
  Pallas kernels  29.3 us (21%)
  local copies, waits for them, and re-layouts  11.6 us (8%)
    ppermute x21, waiting for transfers between devices, shift(): return lax.ppermute(a, axis, [(i, (i + k) % n) for i in range(n)])  59.8 us
    ppermute x21, starting transfers between devices, shift(): return lax.ppermute(a, axis, [(i, (i + k) % n) for i in range(n)])  21.8 us
    unnamed x36, local copies, waits for them, and re-layouts  11.6 us
    pallas_call x1, Pallas kernels, front(): pl.pallas_call(front_kernel, grid_spec=pltpu.PrefetchScalarGridSpec(num_s...  10.3 us
    pallas_call x1, Pallas kernels, last_stage(): pl.pallas_call(last_kernel, in_specs=[SMEM] + [VMEM] * 7 + [HBM], out_spe...  7.21 us
    ppermute x3, waiting for transfers between devices, cross(): return lax.ppermute(a, AXES, pairs)  5.61 us
    pallas_call x2, Pallas kernels, early_sums(): pl.pallas_call(early_kernel, grid_spec=pltpu.PrefetchScalarGridSpec(num_s...  5.56 us
    ppermute x3, starting transfers between devices, cross(): return lax.ppermute(a, AXES, pairs)  5.12 us
  transfers between devices with their start and end apart: 25, of which 14 were waited for; matrix products, arithmetic and copies ran while one was open for 0% of the time, Pallas kernels for 16%

profile of v4, /device:TPU:32, one launch (start us, length us, event | category | flops | bytes accessed | tf_op | source)
XLA Modules:
  0.0 138.5 jit_solution(12697438964899981730)
XLA Ops:
  0.6 3.1 %collective-permute-start.23 = (bf16[2048,512]{1,0:T(8,128)(2,1)}, bf16[2048,512]{1,0:T(8,128)(2,1)}, u32[]{:S(2)}, u32[]{:S(2)}) collective-permute-start(bf16[2048,512]{1,0:T(8,128)(2,1)} %a.1), channel_id=1, source_target_pairs={{0,6},{6,0},{2,4},{4,2},{1,7},{7,1},{3,5},{5,3},{8,14},{14,8},{10,... | collective-permute-start | bytes 6291464 | tf_op jit(solution)/shard_map/ppermute | solution.py:285
  3.8 10.3 %front.1 = (f32[384,256]{1,0:T(8,128)S(1)}, f32[384,256]{1,0:T(8,128)S(1)}, bf16[4,224,384]{2,1,0:T(8,128)(2,1)S(1)}, bf16[4,224,384]{2,1,0:T(8,128)(2,1)}, bf16...) custom-call(s32[4]{0:T(128)S(1)} %pad_add_fusion.s_ref, ...), custom_call_target="tpu_custom_call" | custom-call | tf_op jit(solution)/shard_map/front/pallas_call | solution.py:77
  14.1 2.0 %collective-permute-start.15 = (bf16[4,224,384]{2,1,0:T(8,128)(2,1)S(1)}, bf16[4,224,384]{2,1,0:T(8,128)(2,1)S(1)}, u32[]{:S(2)}, u32[]{:S(2)}) collective-permute-start(bf16[4,224,384]{2,1,0:T(8,128)(2,1)S(1)} %get-tuple-element.37), channel_id=1, source_target_pairs={{0,8},{8,16},{16,24},{24,0},{1,9},{9,17},{17,25},{25,1},{2,10},{10... | collective-permute-start | bytes 2064392 | tf_op jit(solution)/shard_map/ppermute | solution.py:24
  17.0 3.0 %collective-permute-start.17 = (bf16[4,224,384]{2,1,0:T(8,128)(2,1)S(1)}, bf16[4,224,384]{2,1,0:T(8,128)(2,1)S(1)}, u32[]{:S(2)}, u32[]{:S(2)}) collective-permute-start(bf16[4,224,384]{2,1,0:T(8,128)(2,1)S(1)} %get-tuple-element.39), channel_id=1, source_target_pairs={{0,16},{8,24},{16,0},{24,8},{1,17},{9,25},{17,1},{25,9},{2,18},{10... | collective-permute-start | bytes 2064392 | tf_op jit(solution)/shard_map/ppermute | solution.py:24
  20.0 4.9 %collective-permute-done.3 = bf16[384,256]{1,0:T(8,128)(2,1)S(1)} collective-permute-done((bf16[384,256]{1,0:T(8,128)(2,1)S(1)}, bf16[384,256]{1,0:T(8,128)(2,1)S(1)}, u32[]{:S(2)}, u32[]{:S(2)}) %collective-permute-start.3) | collective-permute-done | bytes 196640 | tf_op jit(solution)/shard_map/ppermute | solution.py:24
  28.5 18.0 %collective-permute-done.15.g1 = bf16[4,224,384]{2,1,0:T(8,128)(2,1)S(1)} collective-permute-done((bf16[4,224,384]{2,1,0:T(8,128)(2,1)S(1)}, bf16[4,224,384]{2,1,0:T(8,128)(2,1)S(1)}, u32[]{:S(2)}, u32[]{:S(2)}) %collective-permute-start.15) | collective-permute-done | bytes 688160 | tf_op jit(solution)/shard_map/ppermute | solution.py:24
  47.4 2.8 %collective-permute-start.7 = (bf16[384,512]{1,0:T(8,128)(2,1)S(1)}, bf16[384,512]{1,0:T(8,128)(2,1)S(1)}, u32[]{:S(2)}, u32[]{:S(2)}) collective-permute-start(bf16[384,512]{1,0:T(8,128)(2,1)S(1)} %join.1.c0), channel_id=1, source_target_pairs={{0,96},{1,25},{2,98},{3,27},{4,100},{5,29},{6,102},{7,31},{8,104},... | collective-permute-start | bytes 1179656 | tf_op jit(solution)/shard_map/ppermute | solution.py:36
  54.7 5.0 %collective-permute-done.7.along3 = bf16[384,512]{1,0:T(8,128)(2,1)S(1)} collective-permute-done((bf16[384,512]{1,0:T(8,128)(2,1)S(1)}, bf16[384,512]{1,0:T(8,128)(2,1)S(1)}, u32[]{:S(2)}, u32[]{:S(2)}) %collective-permute-start.7) | collective-permute-done | bytes 393248 | tf_op jit(solution)/shard_map/ppermute | solution.py:36
  61.8 3.3 %collective-permute-start.1 = (bf16[4,224,384]{2,1,0:T(8,128)(2,1)}, bf16[4,224,384]{2,1,0:T(8,128)(2,1)}, u32[]{:S(2)}, u32[]{:S(2)}) collective-permute-start(bf16[4,224,384]{2,1,0:T(8,128)(2,1)} %get-tuple-element.28), channel_id=1, source_target_pairs={{0,96},{32,0},{64,32},{96,64},{1,97},{33,1},{65,33},{97,65},{2,98}... | collective-permute-start | bytes 2064392 | tf_op jit(solution)/shard_map/ppermute | solution.py:24
  68.7 2.0 %shard_map.87.acc = f32[4,224,512]{2,1,0:T(8,128)S(1)} custom-call(s32[1]{0:T(128)} %bitcast.5.s_ref, bf16[4,224,384]{2,1,0:T(8,128)(2,1)S(1)} %copy-done.1, bf16[4,224,384]{2,1,0:T(8,128)(2,1)S(1)} %copy-done.3, bf16[4,224,384]{2,1,0:T(8,128)(2,1)S(1)} %copy-done.5, bf16[384,512]{1,0:T(8,128)(2,1)S(1)} %join.1.c0, ...), custom_call_target="tpu_custom_call" | custom-call | tf_op jit(solution)/shard_map/pallas_call | solution.py:158
  72.2 7.6 %collective-permute-done.g1 = bf16[4,224,384]{2,1,0:T(8,128)(2,1)} collective-permute-done((bf16[4,224,384]{2,1,0:T(8,128)(2,1)}, bf16[4,224,384]{2,1,0:T(8,128)(2,1)}, u32[]{:S(2)}, u32[]{:S(2)}) %collective-permute-start) | collective-permute-done | bytes 688160 | tf_op jit(solution)/shard_map/ppermute | solution.py:24
  80.4 14.7 %collective-permute-done.1.g3 = bf16[4,224,384]{2,1,0:T(8,128)(2,1)} collective-permute-done((bf16[4,224,384]{2,1,0:T(8,128)(2,1)}, bf16[4,224,384]{2,1,0:T(8,128)(2,1)}, u32[]{:S(2)}, u32[]{:S(2)}) %collective-permute-start.1) | collective-permute-done | bytes 688160 | tf_op jit(solution)/shard_map/ppermute | solution.py:24
  96.7 2.1 %collective-permute-start.20 = (bf16[224,512]{1,0:T(8,128)(2,1)S(1)}, bf16[224,512]{1,0:T(8,128)(2,1)S(1)}, u32[]{:S(2)}, u32[]{:S(2)}) collective-permute-start(bf16[224,512]{1,0:T(8,128)(2,1)S(1)} %get-tuple-element.43), channel_id=1, source_target_pairs={{0,96},{32,0},{64,32},{96,64},{1,97},{33,1},{65,33},{97,65},{2,98}... | collective-permute-start | bytes 688136 | tf_op jit(solution)/shard_map/ppermute | solution.py:24
  98.8 3.6 %shard_map.85.acc = f32[4,224,512]{2,1,0:T(8,128)S(1)} custom-call(s32[1]{0:T(128)} %bitcast.2.s_ref, bf16[4,224,384]{2,1,0:T(8,128)(2,1)S(1)} %get-tuple-element.26.g0, bf16[4,224,384]{2,1,0:T(8,128)(2,1)} %collective-permute-done.g1, bf16[4,224,384]{2,1,0:T(8,128)(2,1)} %collective-permute-done.1.g3, bf16[384,512]{1,0:T(8,128)(2,1)S(1)} %join.1.c0, ...), custom_call_target="tpu_custom_call" | custom-call | tf_op jit(solution)/shard_map/pallas_call | solution.py:158
  102.4 1.8 %shard_map.86 = (f32[224,512]{1,0:T(8,128)S(1)}, bf16[224,512]{1,0:T(8,128)(2,1)S(1)}, bf16[224,512]{1,0:T(8,128)(2,1)S(1)}, bf16[224,512]{1,0:T(8,128)(2,1)S(1)}) custom-call(s32[1]{0:T(128)} %bitcast.2.s_ref, f32[4,224,512]{2,1,0:T(8,128)S(1)} %shard_map.85.acc, bf16[4,224,384]{2,1,0:T(8,128)(2,1)} %collective-permute-done.9.g2, ...), custom_call_target="tpu_custom_call" | custom-call | tf_op jit(solution)/shard_map/pallas_call | solution.py:186
  105.0 2.6 %collective-permute-start.12 = (bf16[224,512]{1,0:T(8,128)(2,1)S(1)}, bf16[224,512]{1,0:T(8,128)(2,1)S(1)}, u32[]{:S(2)}, u32[]{:S(2)}) collective-permute-start(bf16[224,512]{1,0:T(8,128)(2,1)S(1)} %get-tuple-element.33), channel_id=1, source_target_pairs={{0,8},{8,16},{16,24},{24,0},{1,9},{9,17},{17,25},{25,1},{2,10},{10... | collective-permute-start | bytes 688136 | tf_op jit(solution)/shard_map/ppermute | solution.py:24
  108.3 2.1 %collective-permute-start.13 = (bf16[224,512]{1,0:T(8,128)(2,1)S(1)}, bf16[224,512]{1,0:T(8,128)(2,1)S(1)}, u32[]{:S(2)}, u32[]{:S(2)}) collective-permute-start(bf16[224,512]{1,0:T(8,128)(2,1)S(1)} %get-tuple-element.34), channel_id=1, source_target_pairs={{0,16},{8,24},{16,0},{24,8},{1,17},{9,25},{17,1},{25,9},{2,18},{10... | collective-permute-start | bytes 688136 | tf_op jit(solution)/shard_map/ppermute | solution.py:24
  111.1 2.6 %collective-permute-start.14 = (bf16[224,512]{1,0:T(8,128)(2,1)S(1)}, bf16[224,512]{1,0:T(8,128)(2,1)S(1)}, u32[]{:S(2)}, u32[]{:S(2)}) collective-permute-start(bf16[224,512]{1,0:T(8,128)(2,1)S(1)} %get-tuple-element.35), channel_id=1, source_target_pairs={{0,24},{8,0},{16,8},{24,16},{1,25},{9,1},{17,9},{25,17},{2,26},{10... | collective-permute-start | bytes 688136 | tf_op jit(solution)/shard_map/ppermute | solution.py:24
  113.8 2.8 %collective-permute-done.12.x1 = bf16[224,512]{1,0:T(8,128)(2,1)S(1)} collective-permute-done((bf16[224,512]{1,0:T(8,128)(2,1)S(1)}, bf16[224,512]{1,0:T(8,128)(2,1)S(1)}, u32[]{:S(2)}, u32[]{:S(2)}) %collective-permute-start.12) | collective-permute-done | bytes 229408 | tf_op jit(solution)/shard_map/ppermute | solution.py:24
  116.6 1.7 %collective-permute-done.13.x2 = bf16[224,512]{1,0:T(8,128)(2,1)S(1)} collective-permute-done((bf16[224,512]{1,0:T(8,128)(2,1)S(1)}, bf16[224,512]{1,0:T(8,128)(2,1)S(1)}, u32[]{:S(2)}, u32[]{:S(2)}) %collective-permute-start.13) | collective-permute-done | bytes 229408 | tf_op jit(solution)/shard_map/ppermute | solution.py:24
  118.3 2.6 %collective-permute-done.14.x3 = bf16[224,512]{1,0:T(8,128)(2,1)S(1)} collective-permute-done((bf16[224,512]{1,0:T(8,128)(2,1)S(1)}, bf16[224,512]{1,0:T(8,128)(2,1)S(1)}, u32[]{:S(2)}, u32[]{:S(2)}) %collective-permute-start.14) | collective-permute-done | bytes 229408 | tf_op jit(solution)/shard_map/ppermute | solution.py:24
  124.2 2.9 %keep.1 = (bf16[2048,512]{1,0:T(8,128)(2,1)S(1)}, bf16[2048,512]{1,0:T(8,128)(2,1)S(1)}, bf16[2048,512]{1,0:T(8,128)(2,1)S(1)}) custom-call(bf16[2048,512]{1,0:T(8,128)(2,1)} %a.1, bf16[2048,512]{1,0:T(8,128)(2,1)} %collective-permute-done.22.b, bf16[2048,512]{1,0:T(8,128)(2,1)} %collective-permute-done.23.c), custom_call_target="tpu_custom_call" | custom-call | tf_op jit(solution)/shard_map/keep/pallas_call | solution.py:125
  127.2 4.1 %collective-permute-done.21.got = bf16[224,512]{1,0:T(8,128)(2,1)S(1)} collective-permute-done((bf16[224,512]{1,0:T(8,128)(2,1)S(1)}, bf16[224,512]{1,0:T(8,128)(2,1)S(1)}, u32[]{:S(2)}, u32[]{:S(2)}) %collective-permute-start.21) | collective-permute-done | bytes 229408 | tf_op jit(solution)/shard_map/ppermute | solution.py:24
  131.2 7.2 %last.1 = (f32[224,512]{1,0:T(8,128)}, f32[224,512]{1,0:T(8,128)}, bf16[224,8192]{1,0:T(8,128)(2,1)}) custom-call(s32[4]{0:T(128)S(1)} %pad_add_fusion.s_ref, f32[224,512]{1,0:T(8,128)S(1)} %get-tuple-element.44.mine, bf16[224,512]{1,0:T(8,128)(2,1)S(1)} %collective-permute-done.21.got, f32[224,512]{1,0:T(8,128)S(1)} %copy-done.10, ...), custom_call_target="tpu_custom_call" | custom-call | tf_op jit(solution)/shard_map/last/pallas_call | solution.py:254
  (74 shorter events, 24.8 us)
Async XLA Ops:
  0.6 53.3 %collective-permute-start.23 = (bf16[2048,512]{1,0:T(8,128)(2,1)}, bf16[2048,512]{1,0:T(8,128)(2,1)}, u32[]{:S(2)}, u32[]{:S(2)}) collective-permute-start(bf16[2048,512]{1,0:T(8,128)(2,1)} %a.1), channel_id=1, source_target_pairs={{0,6},{6,0},{2,4},{4,2},{1,7},{7,1},{3,5},{5,3},{8,14},{14,8},{10,... | collective-permute-start | bytes 6291464 | tf_op jit(solution)/shard_map/ppermute | solution.py:285
  14.1 2.1 %collective-permute-start.2 = (f32[384,256]{1,0:T(8,128)S(1)}, f32[384,256]{1,0:T(8,128)S(1)}, u32[]{:S(2)}, u32[]{:S(2)}) collective-permute-start(f32[384,256]{1,0:T(8,128)S(1)} %get-tuple-element.30), channel_id=1, source_target_pairs={{0,1},{1,0},{2,3},{3,2},{4,5},{5,4},{6,7},{7,6},{8,9},{9,8},{10,11... | collective-permute-start | bytes 1179656 | tf_op jit(solution)/shard_map/ppermute | solution.py:24
  14.1 32.4 %collective-permute-start.15 = (bf16[4,224,384]{2,1,0:T(8,128)(2,1)S(1)}, bf16[4,224,384]{2,1,0:T(8,128)(2,1)S(1)}, u32[]{:S(2)}, u32[]{:S(2)}) collective-permute-start(bf16[4,224,384]{2,1,0:T(8,128)(2,1)S(1)} %get-tuple-element.37), channel_id=1, source_target_pairs={{0,8},{8,16},{16,24},{24,0},{1,9},{9,17},{17,25},{25,1},{2,10},{10... | collective-permute-start | bytes 2064392 | tf_op jit(solution)/shard_map/ppermute | solution.py:24
  16.1 34.0 %collective-permute-start.16 = (bf16[4,224,384]{2,1,0:T(8,128)(2,1)S(1)}, bf16[4,224,384]{2,1,0:T(8,128)(2,1)S(1)}, u32[]{:S(2)}, u32[]{:S(2)}) collective-permute-start(bf16[4,224,384]{2,1,0:T(8,128)(2,1)S(1)} %get-tuple-element.38), channel_id=1, source_target_pairs={{0,24},{8,0},{16,8},{24,16},{1,25},{9,1},{17,9},{25,17},{2,26},{10... | collective-permute-start | bytes 2064392 | tf_op jit(solution)/shard_map/ppermute | solution.py:24
  16.3 8.5 %collective-permute-start.3 = (bf16[384,256]{1,0:T(8,128)(2,1)S(1)}, bf16[384,256]{1,0:T(8,128)(2,1)S(1)}, u32[]{:S(2)}, u32[]{:S(2)}) collective-permute-start(bf16[384,256]{1,0:T(8,128)(2,1)S(1)} %get-tuple-element.49), channel_id=1, source_target_pairs={{0,2},{2,0},{1,3},{3,1},{4,6},{6,4},{5,7},{7,5},{8,10},{10,8},{9,1... | collective-permute-start | bytes 589832 | tf_op jit(solution)/shard_map/ppermute | solution.py:24
  17.0 34.8 %collective-permute-start.17 = (bf16[4,224,384]{2,1,0:T(8,128)(2,1)S(1)}, bf16[4,224,384]{2,1,0:T(8,128)(2,1)S(1)}, u32[]{:S(2)}, u32[]{:S(2)}) collective-permute-start(bf16[4,224,384]{2,1,0:T(8,128)(2,1)S(1)} %get-tuple-element.39), channel_id=1, source_target_pairs={{0,16},{8,24},{16,0},{24,8},{1,17},{9,25},{17,1},{25,9},{2,18},{10... | collective-permute-start | bytes 2064392 | tf_op jit(solution)/shard_map/ppermute | solution.py:24
  27.0 26.9 %collective-permute-start.5 = (bf16[384,512]{1,0:T(8,128)(2,1)S(1)}, bf16[384,512]{1,0:T(8,128)(2,1)S(1)}, u32[]{:S(2)}, u32[]{:S(2)}) collective-permute-start(bf16[384,512]{1,0:T(8,128)(2,1)S(1)} %join.1.c0), channel_id=1, source_target_pairs={{0,32},{1,9},{2,34},{3,11},{4,36},{5,13},{6,38},{7,15},{8,40},{9,1... | collective-permute-start | bytes 1179656 | tf_op jit(solution)/shard_map/ppermute | solution.py:36
  47.4 12.3 %collective-permute-start.7 = (bf16[384,512]{1,0:T(8,128)(2,1)S(1)}, bf16[384,512]{1,0:T(8,128)(2,1)S(1)}, u32[]{:S(2)}, u32[]{:S(2)}) collective-permute-start(bf16[384,512]{1,0:T(8,128)(2,1)S(1)} %join.1.c0), channel_id=1, source_target_pairs={{0,96},{1,25},{2,98},{3,27},{4,100},{5,29},{6,102},{7,31},{8,104},... | collective-permute-start | bytes 1179656 | tf_op jit(solution)/shard_map/ppermute | solution.py:36
  51.0 9.3 %collective-permute-start.10 = (bf16[384,512]{1,0:T(8,128)(2,1)S(1)}, bf16[384,512]{1,0:T(8,128)(2,1)S(1)}, u32[]{:S(2)}, u32[]{:S(2)}) collective-permute-start(bf16[384,512]{1,0:T(8,128)(2,1)S(1)} %join.1.c0), channel_id=1, source_target_pairs={{0,64},{1,17},{2,66},{3,19},{4,68},{5,21},{6,70},{7,23},{8,72},{9,... | collective-permute-start | bytes 1179656 | tf_op jit(solution)/shard_map/ppermute | solution.py:36
  52.7 71.5 %collective-permute-start.22 = (bf16[2048,512]{1,0:T(8,128)(2,1)}, bf16[2048,512]{1,0:T(8,128)(2,1)}, u32[]{:S(2)}, u32[]{:S(2)}) collective-permute-start(bf16[2048,512]{1,0:T(8,128)(2,1)} %a.1), channel_id=1, source_target_pairs={{0,1},{1,0},{2,3},{3,2},{4,5},{5,4},{6,7},{7,6},{8,9},{9,8},{10,11... | collective-permute-start | bytes 6291464 | tf_op jit(solution)/shard_map/ppermute | solution.py:24
  53.9 77.4 %collective-permute-start.24 = (bf16[2048,512]{1,0:T(8,128)(2,1)}, bf16[2048,512]{1,0:T(8,128)(2,1)}, u32[]{:S(2)}, u32[]{:S(2)}) collective-permute-start(bf16[2048,512]{1,0:T(8,128)(2,1)} %collective-permute-done.23.c), channel_id=1, source_target_pairs={{0,1},{1,0},{2,3},{3,2},{4,5},{5,4},{6,7},{7,6},{8,9},{9,8},{10,11... | collective-permute-start | bytes 6291464 | tf_op jit(solution)/shard_map/ppermute | solution.py:24
  53.9 6.7 %collective-permute-start.6 = (bf16[384,512]{1,0:T(8,128)(2,1)S(1)}, bf16[384,512]{1,0:T(8,128)(2,1)S(1)}, u32[]{:S(2)}, u32[]{:S(2)}) collective-permute-start(bf16[384,512]{1,0:T(8,128)(2,1)S(1)} %collective-permute-done.5.along1), channel_id=1, source_target_pairs={{0,1},{1,0},{2,3},{3,2},{4,5},{5,4},{6,7},{7,6},{8,9},{9,8},{10,11... | collective-permute-start | bytes 1179656 | tf_op jit(solution)/shard_map/ppermute | solution.py:24
  59.7 2.1 %collective-permute-start.8 = (bf16[384,512]{1,0:T(8,128)(2,1)S(1)}, bf16[384,512]{1,0:T(8,128)(2,1)S(1)}, u32[]{:S(2)}, u32[]{:S(2)}) collective-permute-start(bf16[384,512]{1,0:T(8,128)(2,1)S(1)} %collective-permute-done.7.along3), channel_id=1, source_target_pairs={{0,1},{1,0},{2,3},{3,2},{4,5},{5,4},{6,7},{7,6},{8,9},{9,8},{10,11... | collective-permute-start | bytes 1179656 | tf_op jit(solution)/shard_map/ppermute | solution.py:24
  60.3 4.8 %collective-permute-start.11 = (bf16[384,512]{1,0:T(8,128)(2,1)S(1)}, bf16[384,512]{1,0:T(8,128)(2,1)S(1)}, u32[]{:S(2)}, u32[]{:S(2)}) collective-permute-start(bf16[384,512]{1,0:T(8,128)(2,1)S(1)} %collective-permute-done.10.along), channel_id=1, source_target_pairs={{0,1},{1,0},{2,3},{3,2},{4,5},{5,4},{6,7},{7,6},{8,9},{9,8},{10,11... | collective-permute-start | bytes 1179656 | tf_op jit(solution)/shard_map/ppermute | solution.py:24
  60.6 19.2 %collective-permute-start = (bf16[4,224,384]{2,1,0:T(8,128)(2,1)}, bf16[4,224,384]{2,1,0:T(8,128)(2,1)}, u32[]{:S(2)}, u32[]{:S(2)}) collective-permute-start(bf16[4,224,384]{2,1,0:T(8,128)(2,1)} %get-tuple-element.27), channel_id=1, source_target_pairs={{0,32},{32,64},{64,96},{96,0},{1,33},{33,65},{65,97},{97,1},{2,34}... | collective-permute-start | bytes 2064392 | tf_op jit(solution)/shard_map/ppermute | solution.py:24
  61.8 33.3 %collective-permute-start.1 = (bf16[4,224,384]{2,1,0:T(8,128)(2,1)}, bf16[4,224,384]{2,1,0:T(8,128)(2,1)}, u32[]{:S(2)}, u32[]{:S(2)}) collective-permute-start(bf16[4,224,384]{2,1,0:T(8,128)(2,1)} %get-tuple-element.28), channel_id=1, source_target_pairs={{0,96},{32,0},{64,32},{96,64},{1,97},{33,1},{65,33},{97,65},{2,98}... | collective-permute-start | bytes 2064392 | tf_op jit(solution)/shard_map/ppermute | solution.py:24
  65.1 31.6 %collective-permute-start.9 = (bf16[4,224,384]{2,1,0:T(8,128)(2,1)}, bf16[4,224,384]{2,1,0:T(8,128)(2,1)}, u32[]{:S(2)}, u32[]{:S(2)}) collective-permute-start(bf16[4,224,384]{2,1,0:T(8,128)(2,1)} %get-tuple-element.31), channel_id=1, source_target_pairs={{0,64},{32,96},{64,0},{96,32},{1,65},{33,97},{65,1},{97,33},{2,66}... | collective-permute-start | bytes 2064392 | tf_op jit(solution)/shard_map/ppermute | solution.py:24
  79.8 24.4 %collective-permute-start.18 = (bf16[224,512]{1,0:T(8,128)(2,1)S(1)}, bf16[224,512]{1,0:T(8,128)(2,1)S(1)}, u32[]{:S(2)}, u32[]{:S(2)}) collective-permute-start(bf16[224,512]{1,0:T(8,128)(2,1)S(1)} %get-tuple-element.41), channel_id=1, source_target_pairs={{0,32},{32,64},{64,96},{96,0},{1,33},{33,65},{65,97},{97,1},{2,34}... | collective-permute-start | bytes 688136 | tf_op jit(solution)/shard_map/ppermute | solution.py:24
  95.1 12.5 %collective-permute-start.19 = (bf16[224,512]{1,0:T(8,128)(2,1)S(1)}, bf16[224,512]{1,0:T(8,128)(2,1)S(1)}, u32[]{:S(2)}, u32[]{:S(2)}) collective-permute-start(bf16[224,512]{1,0:T(8,128)(2,1)S(1)} %get-tuple-element.42), channel_id=1, source_target_pairs={{0,64},{32,96},{64,0},{96,32},{1,65},{33,97},{65,1},{97,33},{2,66}... | collective-permute-start | bytes 688136 | tf_op jit(solution)/shard_map/ppermute | solution.py:24
  96.7 13.7 %collective-permute-start.20 = (bf16[224,512]{1,0:T(8,128)(2,1)S(1)}, bf16[224,512]{1,0:T(8,128)(2,1)S(1)}, u32[]{:S(2)}, u32[]{:S(2)}) collective-permute-start(bf16[224,512]{1,0:T(8,128)(2,1)S(1)} %get-tuple-element.43), channel_id=1, source_target_pairs={{0,96},{32,0},{64,32},{96,64},{1,97},{33,1},{65,33},{97,65},{2,98}... | collective-permute-start | bytes 688136 | tf_op jit(solution)/shard_map/ppermute | solution.py:24
  105.0 11.6 %collective-permute-start.12 = (bf16[224,512]{1,0:T(8,128)(2,1)S(1)}, bf16[224,512]{1,0:T(8,128)(2,1)S(1)}, u32[]{:S(2)}, u32[]{:S(2)}) collective-permute-start(bf16[224,512]{1,0:T(8,128)(2,1)S(1)} %get-tuple-element.33), channel_id=1, source_target_pairs={{0,8},{8,16},{16,24},{24,0},{1,9},{9,17},{17,25},{25,1},{2,10},{10... | collective-permute-start | bytes 688136 | tf_op jit(solution)/shard_map/ppermute | solution.py:24
  108.3 10.0 %collective-permute-start.13 = (bf16[224,512]{1,0:T(8,128)(2,1)S(1)}, bf16[224,512]{1,0:T(8,128)(2,1)S(1)}, u32[]{:S(2)}, u32[]{:S(2)}) collective-permute-start(bf16[224,512]{1,0:T(8,128)(2,1)S(1)} %get-tuple-element.34), channel_id=1, source_target_pairs={{0,16},{8,24},{16,0},{24,8},{1,17},{9,25},{17,1},{25,9},{2,18},{10... | collective-permute-start | bytes 688136 | tf_op jit(solution)/shard_map/ppermute | solution.py:24
  111.1 9.8 %collective-permute-start.14 = (bf16[224,512]{1,0:T(8,128)(2,1)S(1)}, bf16[224,512]{1,0:T(8,128)(2,1)S(1)}, u32[]{:S(2)}, u32[]{:S(2)}) collective-permute-start(bf16[224,512]{1,0:T(8,128)(2,1)S(1)} %get-tuple-element.35), channel_id=1, source_target_pairs={{0,24},{8,0},{16,8},{24,16},{1,25},{9,1},{17,9},{25,17},{2,26},{10... | collective-permute-start | bytes 688136 | tf_op jit(solution)/shard_map/ppermute | solution.py:24
  124.0 7.2 %collective-permute-start.21 = (bf16[224,512]{1,0:T(8,128)(2,1)S(1)}, bf16[224,512]{1,0:T(8,128)(2,1)S(1)}, u32[]{:S(2)}, u32[]{:S(2)}) collective-permute-start(bf16[224,512]{1,0:T(8,128)(2,1)S(1)} %get-tuple-element.45), channel_id=1, source_target_pairs={{0,4},{4,0},{1,5},{5,1},{2,6},{6,2},{3,7},{7,3},{8,12},{12,8},{9,1... | collective-permute-start | bytes 688136 | tf_op jit(solution)/shard_map/ppermute | solution.py:24
  (19 other events, 99.1 us)

commit v5 on v4

--- a/solution.py
+++ b/solution.py
@@ -112,8 +112,12 @@
     )(at, *args)
 
 
-def hold_kernel(a, b, c, x, y, z, sem):
-    copies = [pltpu.make_async_copy(s, d, sem.at[k]) for k, (s, d) in enumerate(((a, x), (b, y), (c, z)))]
+def hold_kernel(a, b, x, y, sem):
+    copies = []
+    for k, (src, dst) in enumerate(((a, x), (b, y))):
+        for q in range(2):
+            rows = pl.ds(q * 1024, 1024)
+            copies.append(pltpu.make_async_copy(src.at[rows], dst.at[rows], sem.at[2 * k + q]))
     for copy in copies:
         copy.start()
     for copy in copies:
@@ -124,10 +128,10 @@
     args = [pltpu.with_memory_space_constraint(a, pltpu.HBM) for a in blocks]
     return pl.pallas_call(
         hold_kernel,
-        in_specs=[HBM] * 3,
-        out_specs=[VMEM] * 3,
-        out_shape=[pltpu.VMEM((2048, 512), BF16)] * 3,
-        scratch_shapes=[pltpu.SemaphoreType.DMA((3,))],
+        in_specs=[HBM] * 2,
+        out_specs=[VMEM] * 2,
+        out_shape=[pltpu.VMEM((2048, 512), BF16)] * 2,
+        scratch_shapes=[pltpu.SemaphoreType.DMA((4,))],
         compiler_params=params(1),
         name="keep",
     )(*args)
@@ -169,28 +173,39 @@
     )(pick.reshape(1), *pieces, *coords)
 
 
-def late_kernel(s_ref, acc, g2, along, beyond, o0, o1, o2, o3, rhs):
+def late_kernel(s_ref, acc, along, beyond, g2, o0, o1, o2, o3, rhs, lhs, sem):
+    order = (1, 3, 2, 0)
+    loads = {j: pltpu.make_async_copy(g2.at[j], lhs.at[j], sem.at[j]) for j in order}
+    for j in order:
+        loads[j].start()
     for pick, ref in ((0, along), (1, beyond)):
 
         @pl.when(s_ref[0] == pick)
         def _():
             rhs[...] = ref[...]
 
-    for j, out in enumerate((o0, o1, o2, o3)):
-        part = acc[j] + jnp.dot(g2[j], rhs[...], preferred_element_type=F32)
+    for j in order:
+        out = (o0, o1, o2, o3)[j]
+        loads[j].wait()
+        part = acc[j] + jnp.dot(lhs[j], rhs[...], preferred_element_type=F32)
         out[...] = part.astype(out.dtype)
 
 
 def late_sums(pick, acc, piece, coords):
     t = piece.shape[-1]
+    args = [pltpu.with_memory_space_constraint(a, pltpu.VMEM) for a in (acc,) + coords]
     return pl.pallas_call(
         late_kernel,
-        in_specs=[SMEM] + [VMEM] * 4,
+        in_specs=[SMEM] + [VMEM] * 3 + [HBM],
         out_specs=[VMEM] * 4,
         out_shape=[pltpu.VMEM((224, 512), F32)] + [pltpu.VMEM((224, 512), BF16)] * 3,
-        scratch_shapes=[pltpu.VMEM((t, 512), BF16)],
+        scratch_shapes=[
+            pltpu.VMEM((t, 512), BF16),
+            pltpu.VMEM((4, 224, t), BF16),
+            pltpu.SemaphoreType.DMA((4,)),
+        ],
         compiler_params=params(6),
-    )(pick.reshape(1), pltpu.with_memory_space_constraint(acc, pltpu.VMEM), piece, *coords)
+    )(pick.reshape(1), *args, pltpu.with_memory_space_constraint(piece, pltpu.HBM))
 
 
 def combine_kernel(s_ref, x0, x1, x2, x3, z0, z1, z2, z3, keep, give):
@@ -215,56 +230,73 @@
 
 def last_kernel(
     s_ref, mine, got, first, second, w0, w1, w2, w3, new_first, new_second, update,
-    w_ref, o_ref, sem, w_sem,
+    w_ref, m_ref, o_ref, w_sem, m_sem, o_sem,
 ):
     yh, c = s_ref[3], s_ref[2]
-    load = pltpu.make_async_copy(w3, w_ref, w_sem)
-    load.start()
+    loads = []
+    for k, w in enumerate((w2, w3)):
+        for q in range(2):
+            rows = pl.ds(q * 1024, 1024)
+            loads.append(pltpu.make_async_copy(w.at[rows], w_ref.at[k, rows], w_sem.at[2 * k + q]))
+    for load in loads:
+        load.start()
     projected = mine[...] + got[...].astype(F32)
     m = 0.9 * first[...] + 0.1 * projected
     v = 0.95 * second[...] + 0.05 * projected * projected
-    new_first[...] = m
-    new_second[...] = v
+    m_ref[0] = m
+    m_ref[1] = v
+    stores = [
+        pltpu.make_async_copy(m_ref.at[k], out, m_sem.at[k])
+        for k, out in enumerate((new_first, new_second))
+    ]
+    for out in stores:
+        out.start()
     root = jnp.sqrt(v * (1.0 / (1.0 - 0.9025)))
     direction = (m * (1.0 / (1.0 - 0.81)) / (root + 1e-08)).astype(BF16)
     blocks = (2 * yh + c, 2 * yh + 1 - c, 2 - 2 * yh + c, 3 - 2 * yh - c)
-    stores = []
-    for k, w in enumerate((w0, w1, w2, w_ref)):
-        if k == 3:
-            load.wait()
-        part = 4.0 * lax.dot_general(
-            direction, w[...], (((1,), (1,)), ((), ())), preferred_element_type=F32
-        )
-        o_ref[k] = part.astype(BF16)
-        cols = pl.ds(pl.multiple_of(blocks[k] * 2048, 2048), 2048)
-        out = pltpu.make_async_copy(o_ref.at[k], update.at[:, cols], sem.at[k])
-        out.start()
-        stores.append(out)
+    for k, w in enumerate((w0, w1, w_ref.at[0], w_ref.at[1])):
+        for q in range(2):
+            if k >= 2:
+                loads[2 * k - 4 + q].wait()
+            part = 4.0 * lax.dot_general(
+                direction,
+                w[q * 1024 : q * 1024 + 1024, :],
+                (((1,), (1,)), ((), ())),
+                preferred_element_type=F32,
+            )
+            o_ref[2 * k + q] = part.astype(BF16)
+            cols = pl.ds(pl.multiple_of(blocks[k] * 2048 + q * 1024, 1024), 1024)
+            out = pltpu.make_async_copy(o_ref.at[2 * k + q], update.at[:, cols], o_sem.at[2 * k + q])
+            out.start()
+            stores.append(out)
     for out in stores:
         out.wait()
 
 
-def last_stage(at, mine, got, first, second, held, across):
+def last_stage(at, mine, got, first, second, held, late):
     rows = first.shape[0]
     moment = jax.ShapeDtypeStruct((rows, 512), F32)
     args = [
         pltpu.with_memory_space_constraint(a, pltpu.VMEM)
         for a in (mine, got, first, second) + tuple(held)
     ]
+    args += [pltpu.with_memory_space_constraint(a, pltpu.HBM) for a in late]
     return pl.pallas_call(
         last_kernel,
-        in_specs=[SMEM] + [VMEM] * 7 + [HBM],
-        out_specs=[VMEM, VMEM, HBM],
+        in_specs=[SMEM] + [VMEM] * 6 + [HBM] * 2,
+        out_specs=[HBM] * 3,
         out_shape=[moment, moment, jax.ShapeDtypeStruct((rows, 8192), BF16)],
         scratch_shapes=[
-            pltpu.VMEM((2048, 512), BF16),
-            pltpu.VMEM((4, rows, 2048), BF16),
+            pltpu.VMEM((2, 2048, 512), BF16),
+            pltpu.VMEM((2, rows, 512), F32),
+            pltpu.VMEM((8, rows, 1024), BF16),
             pltpu.SemaphoreType.DMA((4,)),
-            pltpu.SemaphoreType.DMA,
+            pltpu.SemaphoreType.DMA((2,)),
+            pltpu.SemaphoreType.DMA((8,)),
         ],
         compiler_params=params(12),
         name="last",
-    )(at, *args, pltpu.with_memory_space_constraint(across, pltpu.HBM))
+    )(at, *args)
 
 
 def step(inputs, gate_preact, hidden_grad, projector, first_moment, second_moment):
@@ -295,8 +327,8 @@
     parts_z, parts_x = parts
     keep, give = combine(yl, parts_x, parts_z)
     got = shift(give, "yl", 1)
-    held = hold((projector, beside_w, near_w))
-    return last_stage(at, keep, got, first_moment, second_moment, held, across_w)
+    held = hold((projector, beside_w))
+    return last_stage(at, keep, got, first_moment, second_moment, held, (near_w, across_w))
 
 
 def solution(mesh):

time: 139 us -> 139 us (level)
    unnamed x36 -> x34, local copies, waits for them, and re-layouts: 11.6 us -> 10.7 us
  transfers between devices with their start and end apart: 25 -> 25, of which waited for: 14 -> 13; matrix products, arithmetic and copies ran while one was open for 0% -> 0% of each run, Pallas kernels for 16% -> 17%
where the time goes in v5:
time: 139 us; the launch traced here: 138 us
  waiting for transfers between devices  67.7 us (49%)
  Pallas kernels  29.6 us (21%)
  starting transfers between devices  29.4 us (21%)
  local copies, waits for them, and re-layouts  10.7 us (8%)
    ppermute x21, waiting for transfers between devices, shift(): return lax.ppermute(a, axis, [(i, (i + k) % n) for i in range(n)])  60 us
    ppermute x21, starting transfers between devices, shift(): return lax.ppermute(a, axis, [(i, (i + k) % n) for i in range(n)])  21.2 us
    unnamed x34, local copies, waits for them, and re-layouts  10.7 us
    pallas_call x1, Pallas kernels, front(): pl.pallas_call(front_kernel, grid_spec=pltpu.PrefetchScalarGridSpec(num_s...  10.3 us
    pallas_call x1, Pallas kernels, last_stage(): pl.pallas_call(last_kernel, in_specs=[SMEM] + [VMEM] * 6 + [HBM] * 2, out...  6.43 us
    ppermute x3, waiting for transfers between devices, cross(): return lax.ppermute(a, AXES, pairs)  5.58 us
    pallas_call x2, Pallas kernels, early_sums(): pl.pallas_call(early_kernel, grid_spec=pltpu.PrefetchScalarGridSpec(num_s...  5.56 us
    ppermute x3, starting transfers between devices, cross(): return lax.ppermute(a, AXES, pairs)  5.12 us
  transfers between devices with their start and end apart: 25, of which 13 were waited for; matrix products, arithmetic and copies ran while one was open for 0% of the time, Pallas kernels for 17%

profile of v5, /device:TPU:32, one launch (start us, length us, event | category | flops | bytes accessed | tf_op | source)
XLA Modules:
  0.0 138.3 jit_solution(1903677576951618031)
XLA Ops:
  0.6 3.1 %collective-permute-start.23 = (bf16[2048,512]{1,0:T(8,128)(2,1)}, bf16[2048,512]{1,0:T(8,128)(2,1)}, u32[]{:S(2)}, u32[]{:S(2)}) collective-permute-start(bf16[2048,512]{1,0:T(8,128)(2,1)} %a.1), channel_id=1, source_target_pairs={{0,6},{6,0},{2,4},{4,2},{1,7},{7,1},{3,5},{5,3},{8,14},{14,8},{10,... | collective-permute-start | bytes 6291464 | tf_op jit(solution)/shard_map/ppermute | solution.py:317
  3.8 10.3 %front.1 = (f32[384,256]{1,0:T(8,128)S(1)}, f32[384,256]{1,0:T(8,128)S(1)}, bf16[4,224,384]{2,1,0:T(8,128)(2,1)S(1)}, bf16[4,224,384]{2,1,0:T(8,128)(2,1)}, bf16...) custom-call(s32[4]{0:T(128)S(1)} %pad_add_fusion.s_ref, ...), custom_call_target="tpu_custom_call" | custom-call | tf_op jit(solution)/shard_map/front/pallas_call | solution.py:77
  14.1 2.0 %collective-permute-start.15 = (bf16[4,224,384]{2,1,0:T(8,128)(2,1)S(1)}, bf16[4,224,384]{2,1,0:T(8,128)(2,1)S(1)}, u32[]{:S(2)}, u32[]{:S(2)}) collective-permute-start(bf16[4,224,384]{2,1,0:T(8,128)(2,1)S(1)} %get-tuple-element.36), channel_id=1, source_target_pairs={{0,8},{8,16},{16,24},{24,0},{1,9},{9,17},{17,25},{25,1},{2,10},{10... | collective-permute-start | bytes 2064392 | tf_op jit(solution)/shard_map/ppermute | solution.py:24
  17.0 3.0 %collective-permute-start.17 = (bf16[4,224,384]{2,1,0:T(8,128)(2,1)S(1)}, bf16[4,224,384]{2,1,0:T(8,128)(2,1)S(1)}, u32[]{:S(2)}, u32[]{:S(2)}) collective-permute-start(bf16[4,224,384]{2,1,0:T(8,128)(2,1)S(1)} %get-tuple-element.38), channel_id=1, source_target_pairs={{0,16},{8,24},{16,0},{24,8},{1,17},{9,25},{17,1},{25,9},{2,18},{10... | collective-permute-start | bytes 2064392 | tf_op jit(solution)/shard_map/ppermute | solution.py:24
  20.0 4.9 %collective-permute-done.3 = bf16[384,256]{1,0:T(8,128)(2,1)S(1)} collective-permute-done((bf16[384,256]{1,0:T(8,128)(2,1)S(1)}, bf16[384,256]{1,0:T(8,128)(2,1)S(1)}, u32[]{:S(2)}, u32[]{:S(2)}) %collective-permute-start.3) | collective-permute-done | bytes 196640 | tf_op jit(solution)/shard_map/ppermute | solution.py:24
  28.5 18.0 %collective-permute-done.15.g1 = bf16[4,224,384]{2,1,0:T(8,128)(2,1)S(1)} collective-permute-done((bf16[4,224,384]{2,1,0:T(8,128)(2,1)S(1)}, bf16[4,224,384]{2,1,0:T(8,128)(2,1)S(1)}, u32[]{:S(2)}, u32[]{:S(2)}) %collective-permute-start.15) | collective-permute-done | bytes 688160 | tf_op jit(solution)/shard_map/ppermute | solution.py:24
  47.4 2.8 %collective-permute-start.7 = (bf16[384,512]{1,0:T(8,128)(2,1)S(1)}, bf16[384,512]{1,0:T(8,128)(2,1)S(1)}, u32[]{:S(2)}, u32[]{:S(2)}) collective-permute-start(bf16[384,512]{1,0:T(8,128)(2,1)S(1)} %join.1.c0), channel_id=1, source_target_pairs={{0,96},{1,25},{2,98},{3,27},{4,100},{5,29},{6,102},{7,31},{8,104},... | collective-permute-start | bytes 1179656 | tf_op jit(solution)/shard_map/ppermute | solution.py:36
  51.8 2.1 %collective-permute-done.23.w2 = bf16[2048,512]{1,0:T(8,128)(2,1)} collective-permute-done((bf16[2048,512]{1,0:T(8,128)(2,1)}, bf16[2048,512]{1,0:T(8,128)(2,1)}, u32[]{:S(2)}, u32[]{:S(2)}) %collective-permute-start.23) | collective-permute-done | bytes 2097184 | tf_op jit(solution)/shard_map/ppermute | solution.py:317
  54.7 5.0 %collective-permute-done.7.along3 = bf16[384,512]{1,0:T(8,128)(2,1)S(1)} collective-permute-done((bf16[384,512]{1,0:T(8,128)(2,1)S(1)}, bf16[384,512]{1,0:T(8,128)(2,1)S(1)}, u32[]{:S(2)}, u32[]{:S(2)}) %collective-permute-start.7) | collective-permute-done | bytes 393248 | tf_op jit(solution)/shard_map/ppermute | solution.py:36
  61.8 3.3 %collective-permute-start.1 = (bf16[4,224,384]{2,1,0:T(8,128)(2,1)}, bf16[4,224,384]{2,1,0:T(8,128)(2,1)}, u32[]{:S(2)}, u32[]{:S(2)}) collective-permute-start(bf16[4,224,384]{2,1,0:T(8,128)(2,1)} %get-tuple-element.27), channel_id=1, source_target_pairs={{0,96},{32,0},{64,32},{96,64},{1,97},{33,1},{65,33},{97,65},{2,98}... | collective-permute-start | bytes 2064392 | tf_op jit(solution)/shard_map/ppermute | solution.py:24
  68.7 2.0 %shard_map.87.acc = f32[4,224,512]{2,1,0:T(8,128)S(1)} custom-call(s32[1]{0:T(128)} %bitcast.5.s_ref, bf16[4,224,384]{2,1,0:T(8,128)(2,1)S(1)} %copy-done.1, bf16[4,224,384]{2,1,0:T(8,128)(2,1)S(1)} %copy-done.3, bf16[4,224,384]{2,1,0:T(8,128)(2,1)S(1)} %copy-done.5, bf16[384,512]{1,0:T(8,128)(2,1)S(1)} %join.1.c0, ...), custom_call_target="tpu_custom_call" | custom-call | tf_op jit(solution)/shard_map/pallas_call | solution.py:162
  70.7 2.1 %shard_map.88 = (f32[224,512]{1,0:T(8,128)S(1)}, bf16[224,512]{1,0:T(8,128)(2,1)S(1)}, bf16[224,512]{1,0:T(8,128)(2,1)S(1)}, bf16[224,512]{1,0:T(8,128)(2,1)S(1)}) custom-call(s32[1]{0:T(128)} %bitcast.5.s_ref, f32[4,224,512]{2,1,0:T(8,128)S(1)} %shard_map.87.acc, bf16[384,512]{1,0:T(8,128)(2,1)S(1)} %collective-permute-done.9.along, ...), custom_call_target="tpu_custom_call" | custom-call | tf_op jit(solution)/shard_map/pallas_call | solution.py:197
  73.6 6.3 %collective-permute-done.g1 = bf16[4,224,384]{2,1,0:T(8,128)(2,1)} collective-permute-done((bf16[4,224,384]{2,1,0:T(8,128)(2,1)}, bf16[4,224,384]{2,1,0:T(8,128)(2,1)}, u32[]{:S(2)}, u32[]{:S(2)}) %collective-permute-start) | collective-permute-done | bytes 688160 | tf_op jit(solution)/shard_map/ppermute | solution.py:24
  80.4 14.7 %collective-permute-done.1.g3 = bf16[4,224,384]{2,1,0:T(8,128)(2,1)} collective-permute-done((bf16[4,224,384]{2,1,0:T(8,128)(2,1)}, bf16[4,224,384]{2,1,0:T(8,128)(2,1)}, u32[]{:S(2)}, u32[]{:S(2)}) %collective-permute-start.1) | collective-permute-done | bytes 688160 | tf_op jit(solution)/shard_map/ppermute | solution.py:24
  96.7 2.1 %collective-permute-start.20 = (bf16[224,512]{1,0:T(8,128)(2,1)S(1)}, bf16[224,512]{1,0:T(8,128)(2,1)S(1)}, u32[]{:S(2)}, u32[]{:S(2)}) collective-permute-start(bf16[224,512]{1,0:T(8,128)(2,1)S(1)} %get-tuple-element.42), channel_id=1, source_target_pairs={{0,96},{32,0},{64,32},{96,64},{1,97},{33,1},{65,33},{97,65},{2,98}... | collective-permute-start | bytes 688136 | tf_op jit(solution)/shard_map/ppermute | solution.py:24
  98.8 3.6 %shard_map.85.acc = f32[4,224,512]{2,1,0:T(8,128)S(1)} custom-call(s32[1]{0:T(128)} %bitcast.2.s_ref, bf16[4,224,384]{2,1,0:T(8,128)(2,1)S(1)} %get-tuple-element.25.g0, bf16[4,224,384]{2,1,0:T(8,128)(2,1)} %collective-permute-done.g1, bf16[4,224,384]{2,1,0:T(8,128)(2,1)} %collective-permute-done.1.g3, bf16[384,512]{1,0:T(8,128)(2,1)S(1)} %join.1.c0, ...), custom_call_target="tpu_custom_call" | custom-call | tf_op jit(solution)/shard_map/pallas_call | solution.py:162
  102.4 2.1 %shard_map.86 = (f32[224,512]{1,0:T(8,128)S(1)}, bf16[224,512]{1,0:T(8,128)(2,1)S(1)}, bf16[224,512]{1,0:T(8,128)(2,1)S(1)}, bf16[224,512]{1,0:T(8,128)(2,1)S(1)}) custom-call(s32[1]{0:T(128)} %bitcast.2.s_ref, f32[4,224,512]{2,1,0:T(8,128)S(1)} %shard_map.85.acc, bf16[384,512]{1,0:T(8,128)(2,1)S(1)} %collective-permute-done.9.along, ...), custom_call_target="tpu_custom_call" | custom-call | tf_op jit(solution)/shard_map/pallas_call | solution.py:197
  105.3 2.6 %collective-permute-start.12 = (bf16[224,512]{1,0:T(8,128)(2,1)S(1)}, bf16[224,512]{1,0:T(8,128)(2,1)S(1)}, u32[]{:S(2)}, u32[]{:S(2)}) collective-permute-start(bf16[224,512]{1,0:T(8,128)(2,1)S(1)} %get-tuple-element.32), channel_id=1, source_target_pairs={{0,8},{8,16},{16,24},{24,0},{1,9},{9,17},{17,25},{25,1},{2,10},{10... | collective-permute-start | bytes 688136 | tf_op jit(solution)/shard_map/ppermute | solution.py:24
  110.5 2.6 %collective-permute-start.14 = (bf16[224,512]{1,0:T(8,128)(2,1)S(1)}, bf16[224,512]{1,0:T(8,128)(2,1)S(1)}, u32[]{:S(2)}, u32[]{:S(2)}) collective-permute-start(bf16[224,512]{1,0:T(8,128)(2,1)S(1)} %get-tuple-element.34), channel_id=1, source_target_pairs={{0,24},{8,0},{16,8},{24,16},{1,25},{9,1},{17,9},{25,17},{2,26},{10... | collective-permute-start | bytes 688136 | tf_op jit(solution)/shard_map/ppermute | solution.py:24
  113.2 3.7 %collective-permute-done.12.x1 = bf16[224,512]{1,0:T(8,128)(2,1)S(1)} collective-permute-done((bf16[224,512]{1,0:T(8,128)(2,1)S(1)}, bf16[224,512]{1,0:T(8,128)(2,1)S(1)}, u32[]{:S(2)}, u32[]{:S(2)}) %collective-permute-start.12) | collective-permute-done | bytes 229408 | tf_op jit(solution)/shard_map/ppermute | solution.py:24
  118.6 2.6 %collective-permute-done.14.x3 = bf16[224,512]{1,0:T(8,128)(2,1)S(1)} collective-permute-done((bf16[224,512]{1,0:T(8,128)(2,1)S(1)}, bf16[224,512]{1,0:T(8,128)(2,1)S(1)}, u32[]{:S(2)}, u32[]{:S(2)}) %collective-permute-start.14) | collective-permute-done | bytes 229408 | tf_op jit(solution)/shard_map/ppermute | solution.py:24
  124.5 2.2 %keep.1 = (bf16[2048,512]{1,0:T(8,128)(2,1)S(1)}, bf16[2048,512]{1,0:T(8,128)(2,1)S(1)}) custom-call(bf16[2048,512]{1,0:T(8,128)(2,1)} %a.1, bf16[2048,512]{1,0:T(8,128)(2,1)} %collective-permute-done.22.b), custom_call_target="tpu_custom_call" | custom-call | tf_op jit(solution)/shard_map/keep/pallas_call | solution.py:129
  126.8 5.1 %collective-permute-done.21.got = bf16[224,512]{1,0:T(8,128)(2,1)S(1)} collective-permute-done((bf16[224,512]{1,0:T(8,128)(2,1)S(1)}, bf16[224,512]{1,0:T(8,128)(2,1)S(1)}, u32[]{:S(2)}, u32[]{:S(2)}) %collective-permute-start.21) | collective-permute-done | bytes 229408 | tf_op jit(solution)/shard_map/ppermute | solution.py:24
  131.9 6.4 %last.1 = (f32[224,512]{1,0:T(8,128)}, f32[224,512]{1,0:T(8,128)}, bf16[224,8192]{1,0:T(8,128)(2,1)}) custom-call(s32[4]{0:T(128)S(1)} %pad_add_fusion.s_ref, f32[224,512]{1,0:T(8,128)S(1)} %get-tuple-element.43.mine, bf16[224,512]{1,0:T(8,128)(2,1)S(1)} %collective-permute-done.21.got, f32[224,512]{1,0:T(8,128)S(1)} %copy-done.8, f32[224,512]{1,0:T(8,128)S(1)} %copy-done.9, ...), custom_call_target="tpu_custom_call" | custom-call | tf_op jit(solution)/shard_map/last/pallas_call | solution.py:284
  (72 shorter events, 25.0 us)
Async XLA Ops:
  0.6 53.3 %collective-permute-start.23 = (bf16[2048,512]{1,0:T(8,128)(2,1)}, bf16[2048,512]{1,0:T(8,128)(2,1)}, u32[]{:S(2)}, u32[]{:S(2)}) collective-permute-start(bf16[2048,512]{1,0:T(8,128)(2,1)} %a.1), channel_id=1, source_target_pairs={{0,6},{6,0},{2,4},{4,2},{1,7},{7,1},{3,5},{5,3},{8,14},{14,8},{10,... | collective-permute-start | bytes 6291464 | tf_op jit(solution)/shard_map/ppermute | solution.py:317
  14.1 2.1 %collective-permute-start.2 = (f32[384,256]{1,0:T(8,128)S(1)}, f32[384,256]{1,0:T(8,128)S(1)}, u32[]{:S(2)}, u32[]{:S(2)}) collective-permute-start(f32[384,256]{1,0:T(8,128)S(1)} %get-tuple-element.29), channel_id=1, source_target_pairs={{0,1},{1,0},{2,3},{3,2},{4,5},{5,4},{6,7},{7,6},{8,9},{9,8},{10,11... | collective-permute-start | bytes 1179656 | tf_op jit(solution)/shard_map/ppermute | solution.py:24
  14.1 32.4 %collective-permute-start.15 = (bf16[4,224,384]{2,1,0:T(8,128)(2,1)S(1)}, bf16[4,224,384]{2,1,0:T(8,128)(2,1)S(1)}, u32[]{:S(2)}, u32[]{:S(2)}) collective-permute-start(bf16[4,224,384]{2,1,0:T(8,128)(2,1)S(1)} %get-tuple-element.36), channel_id=1, source_target_pairs={{0,8},{8,16},{16,24},{24,0},{1,9},{9,17},{17,25},{25,1},{2,10},{10... | collective-permute-start | bytes 2064392 | tf_op jit(solution)/shard_map/ppermute | solution.py:24
  16.1 34.0 %collective-permute-start.16 = (bf16[4,224,384]{2,1,0:T(8,128)(2,1)S(1)}, bf16[4,224,384]{2,1,0:T(8,128)(2,1)S(1)}, u32[]{:S(2)}, u32[]{:S(2)}) collective-permute-start(bf16[4,224,384]{2,1,0:T(8,128)(2,1)S(1)} %get-tuple-element.37), channel_id=1, source_target_pairs={{0,24},{8,0},{16,8},{24,16},{1,25},{9,1},{17,9},{25,17},{2,26},{10... | collective-permute-start | bytes 2064392 | tf_op jit(solution)/shard_map/ppermute | solution.py:24
  16.3 8.5 %collective-permute-start.3 = (bf16[384,256]{1,0:T(8,128)(2,1)S(1)}, bf16[384,256]{1,0:T(8,128)(2,1)S(1)}, u32[]{:S(2)}, u32[]{:S(2)}) collective-permute-start(bf16[384,256]{1,0:T(8,128)(2,1)S(1)} %get-tuple-element.47), channel_id=1, source_target_pairs={{0,2},{2,0},{1,3},{3,1},{4,6},{6,4},{5,7},{7,5},{8,10},{10,8},{9,1... | collective-permute-start | bytes 589832 | tf_op jit(solution)/shard_map/ppermute | solution.py:24
  17.0 34.8 %collective-permute-start.17 = (bf16[4,224,384]{2,1,0:T(8,128)(2,1)S(1)}, bf16[4,224,384]{2,1,0:T(8,128)(2,1)S(1)}, u32[]{:S(2)}, u32[]{:S(2)}) collective-permute-start(bf16[4,224,384]{2,1,0:T(8,128)(2,1)S(1)} %get-tuple-element.38), channel_id=1, source_target_pairs={{0,16},{8,24},{16,0},{24,8},{1,17},{9,25},{17,1},{25,9},{2,18},{10... | collective-permute-start | bytes 2064392 | tf_op jit(solution)/shard_map/ppermute | solution.py:24
  27.0 26.9 %collective-permute-start.5 = (bf16[384,512]{1,0:T(8,128)(2,1)S(1)}, bf16[384,512]{1,0:T(8,128)(2,1)S(1)}, u32[]{:S(2)}, u32[]{:S(2)}) collective-permute-start(bf16[384,512]{1,0:T(8,128)(2,1)S(1)} %join.1.c0), channel_id=1, source_target_pairs={{0,32},{1,9},{2,34},{3,11},{4,36},{5,13},{6,38},{7,15},{8,40},{9,1... | collective-permute-start | bytes 1179656 | tf_op jit(solution)/shard_map/ppermute | solution.py:36
  47.4 12.3 %collective-permute-start.7 = (bf16[384,512]{1,0:T(8,128)(2,1)S(1)}, bf16[384,512]{1,0:T(8,128)(2,1)S(1)}, u32[]{:S(2)}, u32[]{:S(2)}) collective-permute-start(bf16[384,512]{1,0:T(8,128)(2,1)S(1)} %join.1.c0), channel_id=1, source_target_pairs={{0,96},{1,25},{2,98},{3,27},{4,100},{5,29},{6,102},{7,31},{8,104},... | collective-permute-start | bytes 1179656 | tf_op jit(solution)/shard_map/ppermute | solution.py:36
  51.0 9.3 %collective-permute-start.9 = (bf16[384,512]{1,0:T(8,128)(2,1)S(1)}, bf16[384,512]{1,0:T(8,128)(2,1)S(1)}, u32[]{:S(2)}, u32[]{:S(2)}) collective-permute-start(bf16[384,512]{1,0:T(8,128)(2,1)S(1)} %join.1.c0), channel_id=1, source_target_pairs={{0,64},{1,17},{2,66},{3,19},{4,68},{5,21},{6,70},{7,23},{8,72},{9,... | collective-permute-start | bytes 1179656 | tf_op jit(solution)/shard_map/ppermute | solution.py:36
  51.8 72.7 %collective-permute-start.22 = (bf16[2048,512]{1,0:T(8,128)(2,1)}, bf16[2048,512]{1,0:T(8,128)(2,1)}, u32[]{:S(2)}, u32[]{:S(2)}) collective-permute-start(bf16[2048,512]{1,0:T(8,128)(2,1)} %a.1), channel_id=1, source_target_pairs={{0,1},{1,0},{2,3},{3,2},{4,5},{5,4},{6,7},{7,6},{8,9},{9,8},{10,11... | collective-permute-start | bytes 6291464 | tf_op jit(solution)/shard_map/ppermute | solution.py:24
  53.9 78.0 %collective-permute-start.24 = (bf16[2048,512]{1,0:T(8,128)(2,1)}, bf16[2048,512]{1,0:T(8,128)(2,1)}, u32[]{:S(2)}, u32[]{:S(2)}) collective-permute-start(bf16[2048,512]{1,0:T(8,128)(2,1)} %collective-permute-done.23.w2), channel_id=1, source_target_pairs={{0,1},{1,0},{2,3},{3,2},{4,5},{5,4},{6,7},{7,6},{8,9},{9,8},{10,11... | collective-permute-start | bytes 6291464 | tf_op jit(solution)/shard_map/ppermute | solution.py:24
  53.9 6.4 %collective-permute-start.6 = (bf16[384,512]{1,0:T(8,128)(2,1)S(1)}, bf16[384,512]{1,0:T(8,128)(2,1)S(1)}, u32[]{:S(2)}, u32[]{:S(2)}) collective-permute-start(bf16[384,512]{1,0:T(8,128)(2,1)S(1)} %collective-permute-done.5.along1), channel_id=1, source_target_pairs={{0,1},{1,0},{2,3},{3,2},{4,5},{5,4},{6,7},{7,6},{8,9},{9,8},{10,11... | collective-permute-start | bytes 1179656 | tf_op jit(solution)/shard_map/ppermute | solution.py:24
  59.7 2.1 %collective-permute-start.8 = (bf16[384,512]{1,0:T(8,128)(2,1)S(1)}, bf16[384,512]{1,0:T(8,128)(2,1)S(1)}, u32[]{:S(2)}, u32[]{:S(2)}) collective-permute-start(bf16[384,512]{1,0:T(8,128)(2,1)S(1)} %collective-permute-done.7.along3), channel_id=1, source_target_pairs={{0,1},{1,0},{2,3},{3,2},{4,5},{5,4},{6,7},{7,6},{8,9},{9,8},{10,11... | collective-permute-start | bytes 1179656 | tf_op jit(solution)/shard_map/ppermute | solution.py:24
  60.3 4.8 %collective-permute-start.10 = (bf16[384,512]{1,0:T(8,128)(2,1)S(1)}, bf16[384,512]{1,0:T(8,128)(2,1)S(1)}, u32[]{:S(2)}, u32[]{:S(2)}) collective-permute-start(bf16[384,512]{1,0:T(8,128)(2,1)S(1)} %collective-permute-done.9.along), channel_id=1, source_target_pairs={{0,1},{1,0},{2,3},{3,2},{4,5},{5,4},{6,7},{7,6},{8,9},{9,8},{10,11... | collective-permute-start | bytes 1179656 | tf_op jit(solution)/shard_map/ppermute | solution.py:24
  60.3 19.6 %collective-permute-start = (bf16[4,224,384]{2,1,0:T(8,128)(2,1)}, bf16[4,224,384]{2,1,0:T(8,128)(2,1)}, u32[]{:S(2)}, u32[]{:S(2)}) collective-permute-start(bf16[4,224,384]{2,1,0:T(8,128)(2,1)} %get-tuple-element.26), channel_id=1, source_target_pairs={{0,32},{32,64},{64,96},{96,0},{1,33},{33,65},{65,97},{97,1},{2,34}... | collective-permute-start | bytes 2064392 | tf_op jit(solution)/shard_map/ppermute | solution.py:24
  61.8 33.3 %collective-permute-start.1 = (bf16[4,224,384]{2,1,0:T(8,128)(2,1)}, bf16[4,224,384]{2,1,0:T(8,128)(2,1)}, u32[]{:S(2)}, u32[]{:S(2)}) collective-permute-start(bf16[4,224,384]{2,1,0:T(8,128)(2,1)} %get-tuple-element.27), channel_id=1, source_target_pairs={{0,96},{32,0},{64,32},{96,64},{1,97},{33,1},{65,33},{97,65},{2,98}... | collective-permute-start | bytes 2064392 | tf_op jit(solution)/shard_map/ppermute | solution.py:24
  65.1 31.6 %collective-permute-start.11 = (bf16[4,224,384]{2,1,0:T(8,128)(2,1)}, bf16[4,224,384]{2,1,0:T(8,128)(2,1)}, u32[]{:S(2)}, u32[]{:S(2)}) collective-permute-start(bf16[4,224,384]{2,1,0:T(8,128)(2,1)} %get-tuple-element.30), channel_id=1, source_target_pairs={{0,64},{32,96},{64,0},{96,32},{1,65},{33,97},{65,1},{97,33},{2,66}... | collective-permute-start | bytes 2064392 | tf_op jit(solution)/shard_map/ppermute | solution.py:24
  79.8 24.7 %collective-permute-start.18 = (bf16[224,512]{1,0:T(8,128)(2,1)S(1)}, bf16[224,512]{1,0:T(8,128)(2,1)S(1)}, u32[]{:S(2)}, u32[]{:S(2)}) collective-permute-start(bf16[224,512]{1,0:T(8,128)(2,1)S(1)} %get-tuple-element.40), channel_id=1, source_target_pairs={{0,32},{32,64},{64,96},{96,0},{1,33},{33,65},{65,97},{97,1},{2,34}... | collective-permute-start | bytes 688136 | tf_op jit(solution)/shard_map/ppermute | solution.py:24
  95.1 12.8 %collective-permute-start.19 = (bf16[224,512]{1,0:T(8,128)(2,1)S(1)}, bf16[224,512]{1,0:T(8,128)(2,1)S(1)}, u32[]{:S(2)}, u32[]{:S(2)}) collective-permute-start(bf16[224,512]{1,0:T(8,128)(2,1)S(1)} %get-tuple-element.41), channel_id=1, source_target_pairs={{0,64},{32,96},{64,0},{96,32},{1,65},{33,97},{65,1},{97,33},{2,66}... | collective-permute-start | bytes 688136 | tf_op jit(solution)/shard_map/ppermute | solution.py:24
  96.7 13.1 %collective-permute-start.20 = (bf16[224,512]{1,0:T(8,128)(2,1)S(1)}, bf16[224,512]{1,0:T(8,128)(2,1)S(1)}, u32[]{:S(2)}, u32[]{:S(2)}) collective-permute-start(bf16[224,512]{1,0:T(8,128)(2,1)S(1)} %get-tuple-element.42), channel_id=1, source_target_pairs={{0,96},{32,0},{64,32},{96,64},{1,97},{33,1},{65,33},{97,65},{2,98}... | collective-permute-start | bytes 688136 | tf_op jit(solution)/shard_map/ppermute | solution.py:24
  105.3 11.6 %collective-permute-start.12 = (bf16[224,512]{1,0:T(8,128)(2,1)S(1)}, bf16[224,512]{1,0:T(8,128)(2,1)S(1)}, u32[]{:S(2)}, u32[]{:S(2)}) collective-permute-start(bf16[224,512]{1,0:T(8,128)(2,1)S(1)} %get-tuple-element.32), channel_id=1, source_target_pairs={{0,8},{8,16},{16,24},{24,0},{1,9},{9,17},{17,25},{25,1},{2,10},{10... | collective-permute-start | bytes 688136 | tf_op jit(solution)/shard_map/ppermute | solution.py:24
  108.6 10.0 %collective-permute-start.13 = (bf16[224,512]{1,0:T(8,128)(2,1)S(1)}, bf16[224,512]{1,0:T(8,128)(2,1)S(1)}, u32[]{:S(2)}, u32[]{:S(2)}) collective-permute-start(bf16[224,512]{1,0:T(8,128)(2,1)S(1)} %get-tuple-element.33), channel_id=1, source_target_pairs={{0,16},{8,24},{16,0},{24,8},{1,17},{9,25},{17,1},{25,9},{2,18},{10... | collective-permute-start | bytes 688136 | tf_op jit(solution)/shard_map/ppermute | solution.py:24
  110.5 10.7 %collective-permute-start.14 = (bf16[224,512]{1,0:T(8,128)(2,1)S(1)}, bf16[224,512]{1,0:T(8,128)(2,1)S(1)}, u32[]{:S(2)}, u32[]{:S(2)}) collective-permute-start(bf16[224,512]{1,0:T(8,128)(2,1)S(1)} %get-tuple-element.34), channel_id=1, source_target_pairs={{0,24},{8,0},{16,8},{24,16},{1,25},{9,1},{17,9},{25,17},{2,26},{10... | collective-permute-start | bytes 688136 | tf_op jit(solution)/shard_map/ppermute | solution.py:24
  124.3 7.6 %collective-permute-start.21 = (bf16[224,512]{1,0:T(8,128)(2,1)S(1)}, bf16[224,512]{1,0:T(8,128)(2,1)S(1)}, u32[]{:S(2)}, u32[]{:S(2)}) collective-permute-start(bf16[224,512]{1,0:T(8,128)(2,1)S(1)} %get-tuple-element.44), channel_id=1, source_target_pairs={{0,4},{4,0},{1,5},{5,1},{2,6},{6,2},{3,7},{7,3},{8,12},{12,8},{9,1... | collective-permute-start | bytes 688136 | tf_op jit(solution)/shard_map/ppermute | solution.py:24
  (18 other events, 110.5 us)

commit v6 on v5

--- a/solution.py
+++ b/solution.py
@@ -24,11 +24,11 @@
     return lax.ppermute(a, axis, [(i, (i + k) % n) for i in range(n)])
 
 
-def cross(a, k):
+def cross(a, first, k):
     pairs = []
     for i in range(128):
         x, z, rest = i // 32, i // 8 % 4, i % 8
-        if i % 2 == 0:
+        if (i % 2 == 0) == (first == "x"):
             x = (x + k) % 4
         else:
             z = (z + k) % 4
@@ -137,87 +137,85 @@
     )(*args)
 
 
-def early_kernel(s_ref, g0, g1, g3, c0, along1, beyond1, along3, beyond3, out, rhs):
-    q = pl.program_id(0)
-
-    @pl.when(q == 0)
-    def _():
-        rhs[0:384, :] = c0[...]
-
-    for pick, ones, threes in ((0, along1, along3), (1, beyond1, beyond3)):
-
-        @pl.when((q == 0) & (s_ref[0] == pick))
+def load(use_x, piece_x, piece_z, dst, sem):
+    for use, src in ((1, piece_x), (0, piece_z)):
+
+        @pl.when(use_x == use)
         def _():
-            rhs[384:768, :] = ones[...]
-            rhs[768:1152, :] = threes[...]
-
-    lhs = jnp.concatenate([g0[0], g1[0], g3[0]], axis=1)
-    out[q] = jnp.dot(lhs, rhs[...], preferred_element_type=F32)
-
-
-def early_sums(pick, pieces, coords):
+            pltpu.make_async_copy(src, dst, sem).start()
+
+    return pltpu.make_async_copy(piece_x, dst, sem)
+
+
+def early_kernel(s_ref, x0, x1, x3, z0, z1, z3, c0, c1, c3, out, lhs, rhs, sem):
+    pairs = ((x0, z0), (x1, z1), (x3, z3))
+    loads = [
+        [
+            load(s_ref[0], a.at[j], b.at[j], lhs.at[j, :, pl.ds(n * 384, 384)], sem.at[j, n])
+            for n, (a, b) in enumerate(pairs)
+        ]
+        for j in range(4)
+    ]
+    for n, coords in enumerate((c0, c1, c3)):
+        rhs[n * 384 : n * 384 + 384, :] = coords[...]
+    for j in range(4):
+        for copy in loads[j]:
+            copy.wait()
+        out[j] = jnp.dot(lhs[j], rhs[...], preferred_element_type=F32)
+
+
+def early_sums(use_x, pieces, coords):
     t = pieces[0].shape[-1]
-    piece = pl.BlockSpec((1, 224, t), lambda q, s: (q, 0, 0))
-    whole = pl.BlockSpec((t, 512), lambda q, s: (0, 0))
+    args = [pltpu.with_memory_space_constraint(a, pltpu.HBM) for a in pieces]
+    args += [pltpu.with_memory_space_constraint(a, pltpu.VMEM) for a in coords]
     return pl.pallas_call(
         early_kernel,
-        grid_spec=pltpu.PrefetchScalarGridSpec(
-            num_scalar_prefetch=1,
-            grid=(4,),
-            in_specs=[piece] * 3 + [whole] * 5,
-            out_specs=VMEM,
-            scratch_shapes=[pltpu.VMEM((3 * t, 512), BF16)],
-        ),
+        in_specs=[SMEM] + [HBM] * 6 + [VMEM] * 3,
+        out_specs=VMEM,
         out_shape=pltpu.VMEM((4, 224, 512), F32),
-        compiler_params=params(10),
-    )(pick.reshape(1), *pieces, *coords)
-
-
-def late_kernel(s_ref, acc, along, beyond, g2, o0, o1, o2, o3, rhs, lhs, sem):
+        scratch_shapes=[
+            pltpu.VMEM((4, 224, 3 * t), BF16),
+            pltpu.VMEM((3 * t, 512), BF16),
+            pltpu.SemaphoreType.DMA((4, 3)),
+        ],
+        compiler_params=params(8),
+    )(use_x.reshape(1), *args)
+
+
+def late_kernel(s_ref, acc, coords, x2, z2, o0, o1, o2, o3, lhs, sem):
     order = (1, 3, 2, 0)
-    loads = {j: pltpu.make_async_copy(g2.at[j], lhs.at[j], sem.at[j]) for j in order}
-    for j in order:
-        loads[j].start()
-    for pick, ref in ((0, along), (1, beyond)):
-
-        @pl.when(s_ref[0] == pick)
-        def _():
-            rhs[...] = ref[...]
-
+    loads = {j: load(s_ref[0], x2.at[j], z2.at[j], lhs.at[j], sem.at[j]) for j in order}
     for j in order:
         out = (o0, o1, o2, o3)[j]
         loads[j].wait()
-        part = acc[j] + jnp.dot(lhs[j], rhs[...], preferred_element_type=F32)
+        part = acc[j] + jnp.dot(lhs[j], coords[...], preferred_element_type=F32)
         out[...] = part.astype(out.dtype)
 
 
-def late_sums(pick, acc, piece, coords):
-    t = piece.shape[-1]
-    args = [pltpu.with_memory_space_constraint(a, pltpu.VMEM) for a in (acc,) + coords]
+def late_sums(use_x, acc, coords, pieces):
+    t = pieces[0].shape[-1]
+    args = [pltpu.with_memory_space_constraint(a, pltpu.VMEM) for a in (acc, coords)]
+    args += [pltpu.with_memory_space_constraint(a, pltpu.HBM) for a in pieces]
     return pl.pallas_call(
         late_kernel,
-        in_specs=[SMEM] + [VMEM] * 3 + [HBM],
+        in_specs=[SMEM] + [VMEM] * 2 + [HBM] * 2,
         out_specs=[VMEM] * 4,
         out_shape=[pltpu.VMEM((224, 512), F32)] + [pltpu.VMEM((224, 512), BF16)] * 3,
-        scratch_shapes=[
-            pltpu.VMEM((t, 512), BF16),
-            pltpu.VMEM((4, 224, t), BF16),
-            pltpu.SemaphoreType.DMA((4,)),
-        ],
+        scratch_shapes=[pltpu.VMEM((4, 224, t), BF16), pltpu.SemaphoreType.DMA((4,))],
         compiler_params=params(6),
-    )(pick.reshape(1), *args, pltpu.with_memory_space_constraint(piece, pltpu.HBM))
-
-
-def combine_kernel(s_ref, x0, x1, x2, x3, z0, z1, z2, z3, keep, give):
-    sum_x = x0[...] + x1[...].astype(F32) + x2[...].astype(F32) + x3[...].astype(F32)
-    sum_z = z0[...] + z1[...].astype(F32) + z2[...].astype(F32) + z3[...].astype(F32)
-    here = s_ref[0] == 0
-    keep[...] = jnp.where(here, sum_x, sum_z)
-    give[...] = jnp.where(here, sum_z, sum_x).astype(BF16)
-
-
-def combine(yl, parts_x, parts_z):
-    own = [pltpu.with_memory_space_constraint(p[0], pltpu.VMEM) for p in (parts_x, parts_z)]
+    )(use_x.reshape(1), *args)
+
+
+def combine_kernel(s_ref, m0, m1, m2, m3, t0, t1, t2, t3, keep, give):
+    mine = m0[...] + m1[...].astype(F32) + m2[...].astype(F32) + m3[...].astype(F32)
+    theirs = t0[...] + t1[...].astype(F32) + t2[...].astype(F32) + t3[...].astype(F32)
+    here = s_ref[0] == 1
+    keep[...] = jnp.where(here, mine, theirs)
+    give[...] = jnp.where(here, theirs, mine).astype(BF16)
+
+
+def combine(keep_mine, mine, theirs):
+    args = [pltpu.with_memory_space_constraint(a, pltpu.VMEM) for a in (*mine, *theirs)]
     return pl.pallas_call(
         combine_kernel,
         in_specs=[SMEM] + [VMEM] * 8,
@@ -225,7 +223,7 @@
         out_shape=[pltpu.VMEM((224, 512), F32), pltpu.VMEM((224, 512), BF16)],
         compiler_params=params(4),
         name="combine",
-    )(yl.reshape(1), own[0], *parts_x[1:], own[1], *parts_z[1:])
+    )(keep_mine.reshape(1), *args)
 
 
 def last_kernel(
@@ -234,12 +232,10 @@
 ):
     yh, c = s_ref[3], s_ref[2]
     loads = []
-    for k, w in enumerate((w2, w3)):
-        for q in range(2):
-            rows = pl.ds(q * 1024, 1024)
-            loads.append(pltpu.make_async_copy(w.at[rows], w_ref.at[k, rows], w_sem.at[2 * k + q]))
-    for load in loads:
-        load.start()
+    for q in range(2):
+        rows = pl.ds(q * 1024, 1024)
+        loads.append(pltpu.make_async_copy(w3.at[rows], w_ref.at[rows], w_sem.at[q]))
+        loads[q].start()
     projected = mine[...] + got[...].astype(F32)
     m = 0.9 * first[...] + 0.1 * projected
     v = 0.95 * second[...] + 0.05 * projected * projected
@@ -253,11 +249,11 @@
         out.start()
     root = jnp.sqrt(v * (1.0 / (1.0 - 0.9025)))
     direction = (m * (1.0 / (1.0 - 0.81)) / (root + 1e-08)).astype(BF16)
-    blocks = (2 * yh + c, 2 * yh + 1 - c, 2 - 2 * yh + c, 3 - 2 * yh - c)
-    for k, w in enumerate((w0, w1, w_ref.at[0], w_ref.at[1])):
+    blocks = (2 * yh + c, 2 * yh + 1 - c, 3 - 2 * yh - c, 2 - 2 * yh + c)
+    for k, w in enumerate((w0, w1, w2, w_ref)):
         for q in range(2):
-            if k >= 2:
-                loads[2 * k - 4 + q].wait()
+            if k == 3:
+                loads[q].wait()
             part = 4.0 * lax.dot_general(
                 direction,
                 w[q * 1024 : q * 1024 + 1024, :],
@@ -273,24 +269,24 @@
         out.wait()
 
 
-def last_stage(at, mine, got, first, second, held, late):
+def last_stage(at, mine, got, first, second, blocks, near):
     rows = first.shape[0]
     moment = jax.ShapeDtypeStruct((rows, 512), F32)
     args = [
         pltpu.with_memory_space_constraint(a, pltpu.VMEM)
-        for a in (mine, got, first, second) + tuple(held)
+        for a in (mine, got, first, second) + tuple(blocks)
     ]
-    args += [pltpu.with_memory_space_constraint(a, pltpu.HBM) for a in late]
+    args.append(pltpu.with_memory_space_constraint(near, pltpu.HBM))
     return pl.pallas_call(
         last_kernel,
-        in_specs=[SMEM] + [VMEM] * 6 + [HBM] * 2,
+        in_specs=[SMEM] + [VMEM] * 7 + [HBM],
         out_specs=[HBM] * 3,
         out_shape=[moment, moment, jax.ShapeDtypeStruct((rows, 8192), BF16)],
         scratch_shapes=[
-            pltpu.VMEM((2, 2048, 512), BF16),
+            pltpu.VMEM((2048, 512), BF16),
             pltpu.VMEM((2, rows, 512), F32),
             pltpu.VMEM((8, rows, 1024), BF16),
-            pltpu.SemaphoreType.DMA((4,)),
+            pltpu.SemaphoreType.DMA((2,)),
             pltpu.SemaphoreType.DMA((2,)),
             pltpu.SemaphoreType.DMA((8,)),
         ],
@@ -311,24 +307,23 @@
     far = shift(chip_sum.astype(BF16), "yh", 1)
     half = (chip_sum + far.astype(F32)).astype(BF16)
     own = join(at, half, shift(half, "c", 1))
-    along = {k: cross(own, k) for k in (1, 3, 2)}
+    along = {k: cross(own, "x", k) for k in (1, 3, 2)}
     beyond = {k: shift(along[k], "c", 1) for k in (1, 3, 2)}
 
     near_w = lax.ppermute(projector, ("yl", "yh"), [(0, 3), (3, 0), (1, 2), (2, 1)])
     beside_w = shift(projector, "c", 1)
     across_w = shift(near_w, "c", 1)
 
-    parts = []
-    for got, pick, axis in ((got_z, 1 - c, "x"), (got_x, c, "z")):
-        near = (own, along[1], beyond[1], along[3], beyond[3])
-        acc = early_sums(pick, (got[0], got[1], got[3]), near)
-        part = late_sums(pick, acc, got[2], (along[2], beyond[2]))
-        parts.append([part[0]] + [shift(part[k], axis, k) for k in (1, 2, 3)])
-    parts_z, parts_x = parts
-    keep, give = combine(yl, parts_x, parts_z)
+    near = [got[k] for got in (got_x, got_z) for k in (0, 1, 3)]
+    sums = []
+    for use_x, coords, axis in ((1 - c, along, "z"), (c, beyond, "x")):
+        acc = early_sums(use_x, near, (own, coords[1], coords[3]))
+        part = late_sums(use_x, acc, coords[2], (got_x[2], got_z[2]))
+        sums.append([part[0]] + [cross(part[k], axis, k) for k in (1, 2, 3)])
+    keep, give = combine(1 - jnp.bitwise_xor(c, yl), *sums)
     got = shift(give, "yl", 1)
     held = hold((projector, beside_w))
-    return last_stage(at, keep, got, first_moment, second_moment, held, (near_w, across_w))
+    return last_stage(at, keep, got, first_moment, second_moment, (*held, across_w), near_w)
 
 
 def solution(mesh):

time: 139 us -> 130 us (0.935)
  the two profiles are of different devices: /device:TPU:32 before, /device:TPU:0 now
where the time goes in v6:
time: 130 us
  waiting for transfers between devices  58.6 us (45%)
  Pallas kernels  34.5 us (27%)
  starting transfers between devices  30.4 us (23%)
  local copies, waits for them, and re-layouts  4.92 us (4%)
    ppermute x15, waiting for transfers between devices, shift(): return lax.ppermute(a, axis, [(i, (i + k) % n) for i in range(n)])  27.5 us
    ppermute x9, waiting for transfers between devices, cross(): return lax.ppermute(a, AXES, pairs)  15.8 us
    ppermute x1, waiting for transfers between devices, step(): lax.ppermute(projector, ('yl', 'yh'), [(0, 3), (3, 0), (1, 2), (2, 1)])  15.3 us
    ppermute x9, starting transfers between devices, cross(): return lax.ppermute(a, AXES, pairs)  13.7 us
    ppermute x15, starting transfers between devices, shift(): return lax.ppermute(a, axis, [(i, (i + k) % n) for i in range(n)])  13.4 us
    pallas_call x1, Pallas kernels, front(): pl.pallas_call(front_kernel, grid_spec=pltpu.PrefetchScalarGridSpec(num_s...  8.99 us
    pallas_call x2, Pallas kernels, early_sums(): pl.pallas_call(early_kernel, in_specs=[SMEM] + [HBM] * 6 + [VMEM] * 3, ou...  8.28 us
    pallas_call x2, Pallas kernels, late_sums(): pl.pallas_call(late_kernel, in_specs=[SMEM] + [VMEM] * 2 + [HBM] * 2, out...  6.81 us
  transfers between devices with their start and end apart: 25, of which 9 were waited for; matrix products, arithmetic and copies ran while one was open for 0% of the time, Pallas kernels for 22%

profile of v6, /device:TPU:0, one launch (start us, length us, event | category | flops | bytes accessed | tf_op | source)
XLA Modules:
  0.0 129.5 jit_solution(13379326399733074941)
XLA Ops:
  0.6 3.2 %collective-permute-start.23 = (bf16[2048,512]{1,0:T(8,128)(2,1)}, bf16[2048,512]{1,0:T(8,128)(2,1)}, u32[]{:S(2)}, u32[]{:S(2)}) collective-permute-start(bf16[2048,512]{1,0:T(8,128)(2,1)} %a.1), channel_id=1, source_target_pairs={{0,6},{6,0},{2,4},{4,2},{1,7},{7,1},{3,5},{5,3},{8,14},{14,8},{10,... | collective-permute-start | bytes 6291464 | tf_op jit(solution)/shard_map/ppermute | solution.py:313
  3.9 9.0 %front.1 = (f32[384,256]{1,0:T(8,128)S(1)}, f32[384,256]{1,0:T(8,128)S(1)}, bf16[4,224,384]{2,1,0:T(8,128)(2,1)S(1)}, bf16[4,224,384]{2,1,0:T(8,128)(2,1)S(1)}, ...) custom-call(s32[4]{0:T(128)S(1)} %pad_add_fusion.s_ref, ...), custom_call_target="tpu_custom_call" | custom-call | tf_op jit(solution)/shard_map/front/pallas_call | solution.py:77
  13.0 1.6 %collective-permute-start = (bf16[4,224,384]{2,1,0:T(8,128)(2,1)S(1)}, bf16[4,224,384]{2,1,0:T(8,128)(2,1)S(1)}, u32[]{:S(2)}, u32[]{:S(2)}) collective-permute-start(bf16[4,224,384]{2,1,0:T(8,128)(2,1)S(1)} %get-tuple-element.26), channel_id=1, source_target_pairs={{0,32},{32,64},{64,96},{96,0},{1,33},{33,65},{65,97},{97,1},{2,34}... | collective-permute-start | bytes 2064392 | tf_op jit(solution)/shard_map/ppermute | solution.py:24
  14.6 1.7 %collective-permute-start.1 = (bf16[4,224,384]{2,1,0:T(8,128)(2,1)S(1)}, bf16[4,224,384]{2,1,0:T(8,128)(2,1)S(1)}, u32[]{:S(2)}, u32[]{:S(2)}) collective-permute-start(bf16[4,224,384]{2,1,0:T(8,128)(2,1)S(1)} %get-tuple-element.27), channel_id=1, source_target_pairs={{0,96},{32,0},{64,32},{96,64},{1,97},{33,1},{65,33},{97,65},{2,98}... | collective-permute-start | bytes 2064392 | tf_op jit(solution)/shard_map/ppermute | solution.py:24
  16.3 1.9 %collective-permute-start.2 = (bf16[4,224,384]{2,1,0:T(8,128)(2,1)S(1)}, bf16[4,224,384]{2,1,0:T(8,128)(2,1)S(1)}, u32[]{:S(2)}, u32[]{:S(2)}) collective-permute-start(bf16[4,224,384]{2,1,0:T(8,128)(2,1)S(1)} %get-tuple-element.29), channel_id=1, source_target_pairs={{0,8},{8,16},{16,24},{24,0},{1,9},{9,17},{17,25},{25,1},{2,10},{10... | collective-permute-start | bytes 2064392 | tf_op jit(solution)/shard_map/ppermute | solution.py:24
  19.0 7.4 %collective-permute-done.5 = bf16[384,256]{1,0:T(8,128)(2,1)S(1)} collective-permute-done((bf16[384,256]{1,0:T(8,128)(2,1)S(1)}, bf16[384,256]{1,0:T(8,128)(2,1)S(1)}, u32[]{:S(2)}, u32[]{:S(2)}) %collective-permute-start.5) | collective-permute-done | bytes 196640 | tf_op jit(solution)/shard_map/ppermute | solution.py:24
  26.5 5.5 %collective-permute-done.x1 = bf16[4,224,384]{2,1,0:T(8,128)(2,1)S(1)} collective-permute-done((bf16[4,224,384]{2,1,0:T(8,128)(2,1)S(1)}, bf16[4,224,384]{2,1,0:T(8,128)(2,1)S(1)}, u32[]{:S(2)}, u32[]{:S(2)}) %collective-permute-start) | collective-permute-done | bytes 688160 | tf_op jit(solution)/shard_map/ppermute | solution.py:24
  32.1 4.0 %collective-permute-start.3 = (bf16[4,224,384]{2,1,0:T(8,128)(2,1)S(1)}, bf16[4,224,384]{2,1,0:T(8,128)(2,1)S(1)}, u32[]{:S(2)}, u32[]{:S(2)}) collective-permute-start(bf16[4,224,384]{2,1,0:T(8,128)(2,1)S(1)} %get-tuple-element.30), channel_id=1, source_target_pairs={{0,24},{8,0},{16,8},{24,16},{1,25},{9,1},{17,9},{25,17},{2,26},{10... | collective-permute-start | bytes 2064392 | tf_op jit(solution)/shard_map/ppermute | solution.py:24
  36.1 1.8 %collective-permute-start.10 = (bf16[4,224,384]{2,1,0:T(8,128)(2,1)S(1)}, bf16[4,224,384]{2,1,0:T(8,128)(2,1)S(1)}, u32[]{:S(2)}, u32[]{:S(2)}) collective-permute-start(bf16[4,224,384]{2,1,0:T(8,128)(2,1)S(1)} %get-tuple-element.33), channel_id=1, source_target_pairs={{0,64},{32,96},{64,0},{96,32},{1,65},{33,97},{65,1},{97,33},{2,66}... | collective-permute-start | bytes 2064392 | tf_op jit(solution)/shard_map/ppermute | solution.py:24
  38.7 15.3 %collective-permute-done.23.w3 = bf16[2048,512]{1,0:T(8,128)(2,1)} collective-permute-done((bf16[2048,512]{1,0:T(8,128)(2,1)}, bf16[2048,512]{1,0:T(8,128)(2,1)}, u32[]{:S(2)}, u32[]{:S(2)}) %collective-permute-start.23) | collective-permute-done | bytes 2097184 | tf_op jit(solution)/shard_map/ppermute | solution.py:313
  54.6 10.8 %collective-permute-done.3.z3 = bf16[4,224,384]{2,1,0:T(8,128)(2,1)S(1)} collective-permute-done((bf16[4,224,384]{2,1,0:T(8,128)(2,1)S(1)}, bf16[4,224,384]{2,1,0:T(8,128)(2,1)S(1)}, u32[]{:S(2)}, u32[]{:S(2)}) %collective-permute-start.3) | collective-permute-done | bytes 688160 | tf_op jit(solution)/shard_map/ppermute | solution.py:24
  65.7 3.0 %collective-permute-start.8 = (bf16[384,512]{1,0:T(8,128)(2,1)S(1)}, bf16[384,512]{1,0:T(8,128)(2,1)}, u32[]{:S(2)}, u32[]{:S(2)}) collective-permute-start(bf16[384,512]{1,0:T(8,128)(2,1)S(1)} %join.1.c0), channel_id=1, source_target_pairs={{0,96},{1,25},{2,98},{3,27},{4,100},{5,29},{6,102},{7,31},{8,104},... | collective-permute-start | bytes 1179656 | tf_op jit(solution)/shard_map/ppermute | solution.py:36
  69.2 9.5 %collective-permute-done.7.c1 = bf16[384,512]{1,0:T(8,128)(2,1)} collective-permute-done((bf16[384,512]{1,0:T(8,128)(2,1)S(1)}, bf16[384,512]{1,0:T(8,128)(2,1)}, u32[]{:S(2)}, u32[]{:S(2)}) %collective-permute-start.7) | collective-permute-done | bytes 393248 | tf_op jit(solution)/shard_map/ppermute | solution.py:36
  79.4 4.2 %shard_map.85.acc = f32[4,224,512]{2,1,0:T(8,128)S(1)} custom-call(s32[1]{0:T(128)} %bitcast.5.s_ref, bf16[4,224,384]{2,1,0:T(8,128)(2,1)} %copy-done, bf16[4,224,384]{2,1,0:T(8,128)(2,1)} %copy-done.10, bf16[4,224,384]{2,1,0:T(8,128)(2,1)} %copy-done.11, bf16[4,224,384]{2,1,0:T(8,128)(2,1)} %copy-done.1, bf16[4,224,384]{2,1,0:T(8,128)(2,1)} %copy-done.12, ...), custom_call_target="tpu_custom_call" | custom-call | tf_op jit(solution)/shard_map/pallas_call | solution.py:171
  83.6 3.1 %shard_map.86 = (f32[224,512]{1,0:T(8,128)S(1)}, bf16[224,512]{1,0:T(8,128)(2,1)S(1)}, bf16[224,512]{1,0:T(8,128)(2,1)S(1)}, bf16[224,512]{1,0:T(8,128)(2,1)S(1)}) custom-call(s32[1]{0:T(128)} %bitcast.5.s_ref, f32[4,224,512]{2,1,0:T(8,128)S(1)} %shard_map.85.acc, bf16[384,512]{1,0:T(8,128)(2,1)} %collective-permute-done.9.coords, ...), custom_call_target="tpu_custom_call" | custom-call | tf_op jit(solution)/shard_map/pallas_call | solution.py:199
  86.9 5.0 %collective-permute-start.13 = (bf16[224,512]{1,0:T(8,128)(2,1)S(1)}, bf16[224,512]{1,0:T(8,128)(2,1)S(1)}, u32[]{:S(2)}, u32[]{:S(2)}) collective-permute-start(bf16[224,512]{1,0:T(8,128)(2,1)S(1)} %get-tuple-element.37), channel_id=1, source_target_pairs={{0,16},{1,65},{2,18},{3,67},{4,20},{5,69},{6,22},{7,71},{8,24},{9,... | collective-permute-start | bytes 688136 | tf_op jit(solution)/shard_map/ppermute | solution.py:36
  91.9 4.1 %shard_map.87.acc = f32[4,224,512]{2,1,0:T(8,128)S(1)} custom-call(s32[1]{0:T(128)} %bitcast.2.s_ref, bf16[4,224,384]{2,1,0:T(8,128)(2,1)} %copy-done, bf16[4,224,384]{2,1,0:T(8,128)(2,1)} %copy-done.10, bf16[4,224,384]{2,1,0:T(8,128)(2,1)} %copy-done.11, bf16[4,224,384]{2,1,0:T(8,128)(2,1)} %copy-done.1, bf16[4,224,384]{2,1,0:T(8,128)(2,1)} %copy-done.12, ...), custom_call_target="tpu_custom_call" | custom-call | tf_op jit(solution)/shard_map/pallas_call | solution.py:171
  96.0 3.7 %shard_map.88 = (f32[224,512]{1,0:T(8,128)S(1)}, bf16[224,512]{1,0:T(8,128)(2,1)}, bf16[224,512]{1,0:T(8,128)(2,1)}, bf16[224,512]{1,0:T(8,128)(2,1)}) custom-call(s32[1]{0:T(128)} %bitcast.2.s_ref, f32[4,224,512]{2,1,0:T(8,128)S(1)} %shard_map.87.acc, bf16[384,512]{1,0:T(8,128)(2,1)} %collective-permute-done.17.coords, bf16[4,224,384]{2,1,0:T(8,128)(2,1)} %copy-done.14, ...), custom_call_target="tpu_custom_call" | custom-call | tf_op jit(solution)/shard_map/pallas_call | solution.py:199
  101.8 4.0 %collective-permute-start.19 = (bf16[224,512]{1,0:T(8,128)(2,1)}, bf16[224,512]{1,0:T(8,128)(2,1)}, u32[]{:S(2)}, u32[]{:S(2)}) collective-permute-start(bf16[224,512]{1,0:T(8,128)(2,1)} %get-tuple-element.41), channel_id=1, source_target_pairs={{0,64},{1,17},{2,66},{3,19},{4,68},{5,21},{6,70},{7,23},{8,72},{9,... | collective-permute-start | bytes 688136 | tf_op jit(solution)/shard_map/ppermute | solution.py:36
  106.5 1.4 %collective-permute-done.18.t1 = bf16[224,512]{1,0:T(8,128)(2,1)S(1)} collective-permute-done((bf16[224,512]{1,0:T(8,128)(2,1)}, bf16[224,512]{1,0:T(8,128)(2,1)S(1)}, u32[]{:S(2)}, u32[]{:S(2)}) %collective-permute-start.18) | collective-permute-done | bytes 229408 | tf_op jit(solution)/shard_map/ppermute | solution.py:36
  107.9 4.0 %collective-permute-done.19.t2 = bf16[224,512]{1,0:T(8,128)(2,1)} collective-permute-done((bf16[224,512]{1,0:T(8,128)(2,1)}, bf16[224,512]{1,0:T(8,128)(2,1)}, u32[]{:S(2)}, u32[]{:S(2)}) %collective-permute-start.19) | collective-permute-done | bytes 229408 | tf_op jit(solution)/shard_map/ppermute | solution.py:36
  117.1 2.3 %keep.1 = (bf16[2048,512]{1,0:T(8,128)(2,1)S(1)}, bf16[2048,512]{1,0:T(8,128)(2,1)S(1)}) custom-call(bf16[2048,512]{1,0:T(8,128)(2,1)} %a.1, bf16[2048,512]{1,0:T(8,128)(2,1)} %collective-permute-done.22.b), custom_call_target="tpu_custom_call" | custom-call | tf_op jit(solution)/shard_map/keep/pallas_call | solution.py:129
  119.4 3.7 %collective-permute-done.21.got = bf16[224,512]{1,0:T(8,128)(2,1)S(1)} collective-permute-done((bf16[224,512]{1,0:T(8,128)(2,1)S(1)}, bf16[224,512]{1,0:T(8,128)(2,1)S(1)}, u32[]{:S(2)}, u32[]{:S(2)}) %collective-permute-start.21) | collective-permute-done | bytes 229408 | tf_op jit(solution)/shard_map/ppermute | solution.py:24
  123.1 6.2 %last.1 = (f32[224,512]{1,0:T(8,128)}, f32[224,512]{1,0:T(8,128)}, bf16[224,8192]{1,0:T(8,128)(2,1)}) custom-call(s32[4]{0:T(128)S(1)} %pad_add_fusion.s_ref, f32[224,512]{1,0:T(8,128)S(1)} %get-tuple-element.43.mine, bf16[224,512]{1,0:T(8,128)(2,1)S(1)} %collective-permute-done.21.got, f32[224,512]{1,0:T(8,128)S(1)} %copy-done.2, f32[224,512]{1,0:T(8,128)S(1)} %copy-done.3, ...), custom_call_target="tpu_custom_call" | custom-call | tf_op jit(solution)/shard_map/last/pallas_call | solution.py:280
  (70 shorter events, 12.1 us)
Async XLA Ops:
  0.6 53.4 %collective-permute-start.23 = (bf16[2048,512]{1,0:T(8,128)(2,1)}, bf16[2048,512]{1,0:T(8,128)(2,1)}, u32[]{:S(2)}, u32[]{:S(2)}) collective-permute-start(bf16[2048,512]{1,0:T(8,128)(2,1)} %a.1), channel_id=1, source_target_pairs={{0,6},{6,0},{2,4},{4,2},{1,7},{7,1},{3,5},{5,3},{8,14},{14,8},{10,... | collective-permute-start | bytes 6291464 | tf_op jit(solution)/shard_map/ppermute | solution.py:313
  13.0 19.0 %collective-permute-start = (bf16[4,224,384]{2,1,0:T(8,128)(2,1)S(1)}, bf16[4,224,384]{2,1,0:T(8,128)(2,1)S(1)}, u32[]{:S(2)}, u32[]{:S(2)}) collective-permute-start(bf16[4,224,384]{2,1,0:T(8,128)(2,1)S(1)} %get-tuple-element.26), channel_id=1, source_target_pairs={{0,32},{32,64},{64,96},{96,0},{1,33},{33,65},{65,97},{97,1},{2,34}... | collective-permute-start | bytes 2064392 | tf_op jit(solution)/shard_map/ppermute | solution.py:24
  14.6 21.5 %collective-permute-start.1 = (bf16[4,224,384]{2,1,0:T(8,128)(2,1)S(1)}, bf16[4,224,384]{2,1,0:T(8,128)(2,1)S(1)}, u32[]{:S(2)}, u32[]{:S(2)}) collective-permute-start(bf16[4,224,384]{2,1,0:T(8,128)(2,1)S(1)} %get-tuple-element.27), channel_id=1, source_target_pairs={{0,96},{32,0},{64,32},{96,64},{1,97},{33,1},{65,33},{97,65},{2,98}... | collective-permute-start | bytes 2064392 | tf_op jit(solution)/shard_map/ppermute | solution.py:24
  16.3 21.6 %collective-permute-start.2 = (bf16[4,224,384]{2,1,0:T(8,128)(2,1)S(1)}, bf16[4,224,384]{2,1,0:T(8,128)(2,1)S(1)}, u32[]{:S(2)}, u32[]{:S(2)}) collective-permute-start(bf16[4,224,384]{2,1,0:T(8,128)(2,1)S(1)} %get-tuple-element.29), channel_id=1, source_target_pairs={{0,8},{8,16},{16,24},{24,0},{1,9},{9,17},{17,25},{25,1},{2,10},{10... | collective-permute-start | bytes 2064392 | tf_op jit(solution)/shard_map/ppermute | solution.py:24
  18.3 8.1 %collective-permute-start.5 = (bf16[384,256]{1,0:T(8,128)(2,1)S(1)}, bf16[384,256]{1,0:T(8,128)(2,1)S(1)}, u32[]{:S(2)}, u32[]{:S(2)}) collective-permute-start(bf16[384,256]{1,0:T(8,128)(2,1)S(1)} %get-tuple-element.47), channel_id=1, source_target_pairs={{0,2},{2,0},{1,3},{3,1},{4,6},{6,4},{5,7},{7,5},{8,10},{10,8},{9,1... | collective-permute-start | bytes 589832 | tf_op jit(solution)/shard_map/ppermute | solution.py:24
  26.4 12.3 %collective-permute-start.6 = (bf16[384,256]{1,0:T(8,128)(2,1)S(1)}, bf16[384,256]{1,0:T(8,128)(2,1)S(1)}, u32[]{:S(2)}, u32[]{:S(2)}) collective-permute-start(bf16[384,256]{1,0:T(8,128)(2,1)S(1)} %add_convert_fusion.half), channel_id=1, source_target_pairs={{0,1},{1,0},{2,3},{3,2},{4,5},{5,4},{6,7},{7,6},{8,9},{9,8},{10,11... | collective-permute-start | bytes 589832 | tf_op jit(solution)/shard_map/ppermute | solution.py:24
  32.1 33.3 %collective-permute-start.3 = (bf16[4,224,384]{2,1,0:T(8,128)(2,1)S(1)}, bf16[4,224,384]{2,1,0:T(8,128)(2,1)S(1)}, u32[]{:S(2)}, u32[]{:S(2)}) collective-permute-start(bf16[4,224,384]{2,1,0:T(8,128)(2,1)S(1)} %get-tuple-element.30), channel_id=1, source_target_pairs={{0,24},{8,0},{16,8},{24,16},{1,25},{9,1},{17,9},{25,17},{2,26},{10... | collective-permute-start | bytes 2064392 | tf_op jit(solution)/shard_map/ppermute | solution.py:24
  36.1 29.6 %collective-permute-start.10 = (bf16[4,224,384]{2,1,0:T(8,128)(2,1)S(1)}, bf16[4,224,384]{2,1,0:T(8,128)(2,1)S(1)}, u32[]{:S(2)}, u32[]{:S(2)}) collective-permute-start(bf16[4,224,384]{2,1,0:T(8,128)(2,1)S(1)} %get-tuple-element.33), channel_id=1, source_target_pairs={{0,64},{32,96},{64,0},{96,32},{1,65},{33,97},{65,1},{97,33},{2,66}... | collective-permute-start | bytes 2064392 | tf_op jit(solution)/shard_map/ppermute | solution.py:24
  37.9 30.7 %collective-permute-start.11 = (bf16[4,224,384]{2,1,0:T(8,128)(2,1)S(1)}, bf16[4,224,384]{2,1,0:T(8,128)(2,1)S(1)}, u32[]{:S(2)}, u32[]{:S(2)}) collective-permute-start(bf16[4,224,384]{2,1,0:T(8,128)(2,1)S(1)} %get-tuple-element.34), channel_id=1, source_target_pairs={{0,16},{8,24},{16,0},{24,8},{1,17},{9,25},{17,1},{25,9},{2,18},{10... | collective-permute-start | bytes 2064392 | tf_op jit(solution)/shard_map/ppermute | solution.py:24
  38.7 78.4 %collective-permute-start.22 = (bf16[2048,512]{1,0:T(8,128)(2,1)}, bf16[2048,512]{1,0:T(8,128)(2,1)}, u32[]{:S(2)}, u32[]{:S(2)}) collective-permute-start(bf16[2048,512]{1,0:T(8,128)(2,1)} %a.1), channel_id=1, source_target_pairs={{0,1},{1,0},{2,3},{3,2},{4,5},{5,4},{6,7},{7,6},{8,9},{9,8},{10,11... | collective-permute-start | bytes 6291464 | tf_op jit(solution)/shard_map/ppermute | solution.py:24
  54.0 69.1 %collective-permute-start.24 = (bf16[2048,512]{1,0:T(8,128)(2,1)}, bf16[2048,512]{1,0:T(8,128)(2,1)S(1)}, u32[]{:S(2)}, u32[]{:S(2)}) collective-permute-start(bf16[2048,512]{1,0:T(8,128)(2,1)} %collective-permute-done.23.w3), channel_id=1, source_target_pairs={{0,1},{1,0},{2,3},{3,2},{4,5},{5,4},{6,7},{7,6},{8,9},{9,8},{10,11... | collective-permute-start | bytes 6291464 | tf_op jit(solution)/shard_map/ppermute | solution.py:24
  65.4 13.3 %collective-permute-start.7 = (bf16[384,512]{1,0:T(8,128)(2,1)S(1)}, bf16[384,512]{1,0:T(8,128)(2,1)}, u32[]{:S(2)}, u32[]{:S(2)}) collective-permute-start(bf16[384,512]{1,0:T(8,128)(2,1)S(1)} %join.1.c0), channel_id=1, source_target_pairs={{0,32},{1,9},{2,34},{3,11},{4,36},{5,13},{6,38},{7,15},{8,40},{9,1... | collective-permute-start | bytes 1179656 | tf_op jit(solution)/shard_map/ppermute | solution.py:36
  65.7 13.0 %collective-permute-start.8 = (bf16[384,512]{1,0:T(8,128)(2,1)S(1)}, bf16[384,512]{1,0:T(8,128)(2,1)}, u32[]{:S(2)}, u32[]{:S(2)}) collective-permute-start(bf16[384,512]{1,0:T(8,128)(2,1)S(1)} %join.1.c0), channel_id=1, source_target_pairs={{0,96},{1,25},{2,98},{3,27},{4,100},{5,29},{6,102},{7,31},{8,104},... | collective-permute-start | bytes 1179656 | tf_op jit(solution)/shard_map/ppermute | solution.py:36
  68.6 10.6 %collective-permute-start.9 = (bf16[384,512]{1,0:T(8,128)(2,1)S(1)}, bf16[384,512]{1,0:T(8,128)(2,1)}, u32[]{:S(2)}, u32[]{:S(2)}) collective-permute-start(bf16[384,512]{1,0:T(8,128)(2,1)S(1)} %join.1.c0), channel_id=1, source_target_pairs={{0,64},{1,17},{2,66},{3,19},{4,68},{5,21},{6,70},{7,23},{8,72},{9,... | collective-permute-start | bytes 1179656 | tf_op jit(solution)/shard_map/ppermute | solution.py:36
  78.7 8.0 %collective-permute-start.15 = (bf16[384,512]{1,0:T(8,128)(2,1)}, bf16[384,512]{1,0:T(8,128)(2,1)S(1)}, u32[]{:S(2)}, u32[]{:S(2)}) collective-permute-start(bf16[384,512]{1,0:T(8,128)(2,1)} %collective-permute-done.7.c1), channel_id=1, source_target_pairs={{0,1},{1,0},{2,3},{3,2},{4,5},{5,4},{6,7},{7,6},{8,9},{9,8},{10,11... | collective-permute-start | bytes 1179656 | tf_op jit(solution)/shard_map/ppermute | solution.py:24
  78.7 8.2 %collective-permute-start.16 = (bf16[384,512]{1,0:T(8,128)(2,1)}, bf16[384,512]{1,0:T(8,128)(2,1)}, u32[]{:S(2)}, u32[]{:S(2)}) collective-permute-start(bf16[384,512]{1,0:T(8,128)(2,1)} %collective-permute-done.8.c3), channel_id=1, source_target_pairs={{0,1},{1,0},{2,3},{3,2},{4,5},{5,4},{6,7},{7,6},{8,9},{9,8},{10,11... | collective-permute-start | bytes 1179656 | tf_op jit(solution)/shard_map/ppermute | solution.py:24
  79.3 12.6 %collective-permute-start.17 = (bf16[384,512]{1,0:T(8,128)(2,1)}, bf16[384,512]{1,0:T(8,128)(2,1)}, u32[]{:S(2)}, u32[]{:S(2)}) collective-permute-start(bf16[384,512]{1,0:T(8,128)(2,1)} %collective-permute-done.9.coords), channel_id=1, source_target_pairs={{0,1},{1,0},{2,3},{3,2},{4,5},{5,4},{6,7},{7,6},{8,9},{9,8},{10,11... | collective-permute-start | bytes 1179656 | tf_op jit(solution)/shard_map/ppermute | solution.py:24
  86.7 13.1 %collective-permute-start.12 = (bf16[224,512]{1,0:T(8,128)(2,1)S(1)}, bf16[224,512]{1,0:T(8,128)(2,1)S(1)}, u32[]{:S(2)}, u32[]{:S(2)}) collective-permute-start(bf16[224,512]{1,0:T(8,128)(2,1)S(1)} %get-tuple-element.36), channel_id=1, source_target_pairs={{0,8},{1,33},{2,10},{3,35},{4,12},{5,37},{6,14},{7,39},{8,16},{9,4... | collective-permute-start | bytes 688136 | tf_op jit(solution)/shard_map/ppermute | solution.py:36
  86.9 14.2 %collective-permute-start.13 = (bf16[224,512]{1,0:T(8,128)(2,1)S(1)}, bf16[224,512]{1,0:T(8,128)(2,1)S(1)}, u32[]{:S(2)}, u32[]{:S(2)}) collective-permute-start(bf16[224,512]{1,0:T(8,128)(2,1)S(1)} %get-tuple-element.37), channel_id=1, source_target_pairs={{0,16},{1,65},{2,18},{3,67},{4,20},{5,69},{6,22},{7,71},{8,24},{9,... | collective-permute-start | bytes 688136 | tf_op jit(solution)/shard_map/ppermute | solution.py:36
  91.9 13.9 %collective-permute-start.14 = (bf16[224,512]{1,0:T(8,128)(2,1)S(1)}, bf16[224,512]{1,0:T(8,128)(2,1)S(1)}, u32[]{:S(2)}, u32[]{:S(2)}) collective-permute-start(bf16[224,512]{1,0:T(8,128)(2,1)S(1)} %get-tuple-element.38), channel_id=1, source_target_pairs={{0,24},{1,97},{2,26},{3,99},{4,28},{5,101},{6,30},{7,103},{8,0},{9... | collective-permute-start | bytes 688136 | tf_op jit(solution)/shard_map/ppermute | solution.py:36
  100.4 7.4 %collective-permute-start.18 = (bf16[224,512]{1,0:T(8,128)(2,1)}, bf16[224,512]{1,0:T(8,128)(2,1)S(1)}, u32[]{:S(2)}, u32[]{:S(2)}) collective-permute-start(bf16[224,512]{1,0:T(8,128)(2,1)} %get-tuple-element.40), channel_id=1, source_target_pairs={{0,32},{1,9},{2,34},{3,11},{4,36},{5,13},{6,38},{7,15},{8,40},{9,1... | collective-permute-start | bytes 688136 | tf_op jit(solution)/shard_map/ppermute | solution.py:36
  101.8 10.1 %collective-permute-start.19 = (bf16[224,512]{1,0:T(8,128)(2,1)}, bf16[224,512]{1,0:T(8,128)(2,1)}, u32[]{:S(2)}, u32[]{:S(2)}) collective-permute-start(bf16[224,512]{1,0:T(8,128)(2,1)} %get-tuple-element.41), channel_id=1, source_target_pairs={{0,64},{1,17},{2,66},{3,19},{4,68},{5,21},{6,70},{7,23},{8,72},{9,... | collective-permute-start | bytes 688136 | tf_op jit(solution)/shard_map/ppermute | solution.py:36
  106.5 6.3 %collective-permute-start.20 = (bf16[224,512]{1,0:T(8,128)(2,1)}, bf16[224,512]{1,0:T(8,128)(2,1)}, u32[]{:S(2)}, u32[]{:S(2)}) collective-permute-start(bf16[224,512]{1,0:T(8,128)(2,1)} %get-tuple-element.42), channel_id=1, source_target_pairs={{0,96},{1,25},{2,98},{3,27},{4,100},{5,29},{6,102},{7,31},{8,104},... | collective-permute-start | bytes 688136 | tf_op jit(solution)/shard_map/ppermute | solution.py:36
  117.0 6.1 %collective-permute-start.21 = (bf16[224,512]{1,0:T(8,128)(2,1)S(1)}, bf16[224,512]{1,0:T(8,128)(2,1)S(1)}, u32[]{:S(2)}, u32[]{:S(2)}) collective-permute-start(bf16[224,512]{1,0:T(8,128)(2,1)S(1)} %get-tuple-element.44), channel_id=1, source_target_pairs={{0,4},{4,0},{1,5},{5,1},{2,6},{6,2},{3,7},{7,3},{8,12},{12,8},{9,1... | collective-permute-start | bytes 688136 | tf_op jit(solution)/shard_map/ppermute | solution.py:24
  (17 other events, 324.8 us)

commit v7 on v6

--- a/solution.py
+++ b/solution.py
@@ -182,27 +182,24 @@
     )(use_x.reshape(1), *args)
 
 
-def late_kernel(s_ref, acc, coords, x2, z2, o0, o1, o2, o3, lhs, sem):
-    order = (1, 3, 2, 0)
-    loads = {j: load(s_ref[0], x2.at[j], z2.at[j], lhs.at[j], sem.at[j]) for j in order}
-    for j in order:
-        out = (o0, o1, o2, o3)[j]
-        loads[j].wait()
-        part = acc[j] + jnp.dot(lhs[j], coords[...], preferred_element_type=F32)
-        out[...] = part.astype(out.dtype)
+def late_kernel(s_ref, acc, coords, x2, z2, o0, o1, o2, o3):
+    for use, piece in ((1, x2), (0, z2)):
+
+        @pl.when(s_ref[0] == use)
+        def _():
+            for j, out in enumerate((o0, o1, o2, o3)):
+                part = acc[j] + jnp.dot(piece[j], coords[...], preferred_element_type=F32)
+                out[...] = part.astype(out.dtype)
 
 
 def late_sums(use_x, acc, coords, pieces):
-    t = pieces[0].shape[-1]
-    args = [pltpu.with_memory_space_constraint(a, pltpu.VMEM) for a in (acc, coords)]
-    args += [pltpu.with_memory_space_constraint(a, pltpu.HBM) for a in pieces]
+    args = [pltpu.with_memory_space_constraint(a, pltpu.VMEM) for a in (acc, coords, *pieces)]
     return pl.pallas_call(
         late_kernel,
-        in_specs=[SMEM] + [VMEM] * 2 + [HBM] * 2,
+        in_specs=[SMEM] + [VMEM] * 4,
         out_specs=[VMEM] * 4,
         out_shape=[pltpu.VMEM((224, 512), F32)] + [pltpu.VMEM((224, 512), BF16)] * 3,
-        scratch_shapes=[pltpu.VMEM((4, 224, t), BF16), pltpu.SemaphoreType.DMA((4,))],
-        compiler_params=params(6),
+        compiler_params=params(4),
     )(use_x.reshape(1), *args)
 
 

time: 130 us -> 122 us (0.938)
  Pallas kernels: 34.5 us -> 30 us
  local copies, waits for them, and re-layouts: 4.92 us -> 2.56 us
    pallas_call x2, Pallas kernels: 6.81 us -> 4.09 us  [late_sums(): pl.pallas_call(late_kernel, in_specs=[SMEM] + [VMEM] * 4, out_specs=[VMEM...]
    unnamed x32 -> x18, local copies, waits for them, and re-layouts: 4.92 us -> 2.56 us
  transfers between devices with their start and end apart: 25 -> 25, of which waited for: 9 -> 10; matrix products, arithmetic and copies ran while one was open for 0% -> 0% of each run, Pallas kernels for 22% -> 19%
where the time goes in v7:
time: 122 us
  waiting for transfers between devices  57.7 us (47%)
  starting transfers between devices  30.4 us (25%)
  Pallas kernels  30 us (25%)
  local copies, waits for them, and re-layouts  2.56 us (2%)
    ppermute x15, waiting for transfers between devices, shift(): return lax.ppermute(a, axis, [(i, (i + k) % n) for i in range(n)])  27.5 us
    ppermute x9, waiting for transfers between devices, cross(): return lax.ppermute(a, AXES, pairs)  15.9 us
    ppermute x1, waiting for transfers between devices, step(): lax.ppermute(projector, ('yl', 'yh'), [(0, 3), (3, 0), (1, 2), (2, 1)])  14.4 us
    ppermute x9, starting transfers between devices, cross(): return lax.ppermute(a, AXES, pairs)  13.8 us
    ppermute x15, starting transfers between devices, shift(): return lax.ppermute(a, axis, [(i, (i + k) % n) for i in range(n)])  13.4 us
    pallas_call x1, Pallas kernels, front(): pl.pallas_call(front_kernel, grid_spec=pltpu.PrefetchScalarGridSpec(num_s...  8.99 us
    pallas_call x2, Pallas kernels, early_sums(): pl.pallas_call(early_kernel, in_specs=[SMEM] + [HBM] * 6 + [VMEM] * 3, ou...  7.15 us
    pallas_call x1, Pallas kernels, last_stage(): pl.pallas_call(last_kernel, in_specs=[SMEM] + [VMEM] * 7 + [HBM], out_spe...  6.67 us
  transfers between devices with their start and end apart: 25, of which 10 were waited for; matrix products, arithmetic and copies ran while one was open for 0% of the time, Pallas kernels for 19%

profile of v7, /device:TPU:0, one launch (start us, length us, event | category | flops | bytes accessed | tf_op | source)
XLA Modules:
  0.0 121.8 jit_solution(14122349593666638204)
XLA Ops:
  0.6 3.2 %collective-permute-start.23 = (bf16[2048,512]{1,0:T(8,128)(2,1)}, bf16[2048,512]{1,0:T(8,128)(2,1)}, u32[]{:S(2)}, u32[]{:S(2)}) collective-permute-start(bf16[2048,512]{1,0:T(8,128)(2,1)} %a.1), channel_id=1, source_target_pairs={{0,6},{6,0},{2,4},{4,2},{1,7},{7,1},{3,5},{5,3},{8,14},{14,8},{10,... | collective-permute-start | bytes 6291464 | tf_op jit(solution)/shard_map/ppermute | solution.py:310
  3.9 9.0 %front.1 = (f32[384,256]{1,0:T(8,128)S(1)}, f32[384,256]{1,0:T(8,128)S(1)}, bf16[4,224,384]{2,1,0:T(8,128)(2,1)S(1)}, bf16[4,224,384]{2,1,0:T(8,128)(2,1)S(1)}, ...) custom-call(s32[4]{0:T(128)S(1)} %pad_add_fusion.s_ref, ...), custom_call_target="tpu_custom_call" | custom-call | tf_op jit(solution)/shard_map/front/pallas_call | solution.py:77
  13.0 1.6 %collective-permute-start = (bf16[4,224,384]{2,1,0:T(8,128)(2,1)S(1)}, bf16[4,224,384]{2,1,0:T(8,128)(2,1)S(1)}, u32[]{:S(2)}, u32[]{:S(2)}) collective-permute-start(bf16[4,224,384]{2,1,0:T(8,128)(2,1)S(1)} %get-tuple-element.26), channel_id=1, source_target_pairs={{0,32},{32,64},{64,96},{96,0},{1,33},{33,65},{65,97},{97,1},{2,34}... | collective-permute-start | bytes 2064392 | tf_op jit(solution)/shard_map/ppermute | solution.py:24
  14.6 1.7 %collective-permute-start.1 = (bf16[4,224,384]{2,1,0:T(8,128)(2,1)S(1)}, bf16[4,224,384]{2,1,0:T(8,128)(2,1)S(1)}, u32[]{:S(2)}, u32[]{:S(2)}) collective-permute-start(bf16[4,224,384]{2,1,0:T(8,128)(2,1)S(1)} %get-tuple-element.27), channel_id=1, source_target_pairs={{0,96},{32,0},{64,32},{96,64},{1,97},{33,1},{65,33},{97,65},{2,98}... | collective-permute-start | bytes 2064392 | tf_op jit(solution)/shard_map/ppermute | solution.py:24
  16.3 1.9 %collective-permute-start.2 = (bf16[4,224,384]{2,1,0:T(8,128)(2,1)S(1)}, bf16[4,224,384]{2,1,0:T(8,128)(2,1)S(1)}, u32[]{:S(2)}, u32[]{:S(2)}) collective-permute-start(bf16[4,224,384]{2,1,0:T(8,128)(2,1)S(1)} %get-tuple-element.29), channel_id=1, source_target_pairs={{0,8},{8,16},{16,24},{24,0},{1,9},{9,17},{17,25},{25,1},{2,10},{10... | collective-permute-start | bytes 2064392 | tf_op jit(solution)/shard_map/ppermute | solution.py:24
  19.0 7.4 %collective-permute-done.5 = bf16[384,256]{1,0:T(8,128)(2,1)S(1)} collective-permute-done((bf16[384,256]{1,0:T(8,128)(2,1)S(1)}, bf16[384,256]{1,0:T(8,128)(2,1)S(1)}, u32[]{:S(2)}, u32[]{:S(2)}) %collective-permute-start.5) | collective-permute-done | bytes 196640 | tf_op jit(solution)/shard_map/ppermute | solution.py:24
  26.5 5.5 %collective-permute-done.x1 = bf16[4,224,384]{2,1,0:T(8,128)(2,1)S(1)} collective-permute-done((bf16[4,224,384]{2,1,0:T(8,128)(2,1)S(1)}, bf16[4,224,384]{2,1,0:T(8,128)(2,1)S(1)}, u32[]{:S(2)}, u32[]{:S(2)}) %collective-permute-start) | collective-permute-done | bytes 688160 | tf_op jit(solution)/shard_map/ppermute | solution.py:24
  32.1 4.0 %collective-permute-start.3 = (bf16[4,224,384]{2,1,0:T(8,128)(2,1)S(1)}, bf16[4,224,384]{2,1,0:T(8,128)(2,1)}, u32[]{:S(2)}, u32[]{:S(2)}) collective-permute-start(bf16[4,224,384]{2,1,0:T(8,128)(2,1)S(1)} %get-tuple-element.30), channel_id=1, source_target_pairs={{0,24},{8,0},{16,8},{24,16},{1,25},{9,1},{17,9},{25,17},{2,26},{10... | collective-permute-start | bytes 2064392 | tf_op jit(solution)/shard_map/ppermute | solution.py:24
  36.1 1.8 %collective-permute-start.10 = (bf16[4,224,384]{2,1,0:T(8,128)(2,1)S(1)}, bf16[4,224,384]{2,1,0:T(8,128)(2,1)S(1)}, u32[]{:S(2)}, u32[]{:S(2)}) collective-permute-start(bf16[4,224,384]{2,1,0:T(8,128)(2,1)S(1)} %get-tuple-element.33), channel_id=1, source_target_pairs={{0,64},{32,96},{64,0},{96,32},{1,65},{33,97},{65,1},{97,33},{2,66}... | collective-permute-start | bytes 2064392 | tf_op jit(solution)/shard_map/ppermute | solution.py:24
  39.6 14.4 %collective-permute-done.23.w3 = bf16[2048,512]{1,0:T(8,128)(2,1)} collective-permute-done((bf16[2048,512]{1,0:T(8,128)(2,1)}, bf16[2048,512]{1,0:T(8,128)(2,1)}, u32[]{:S(2)}, u32[]{:S(2)}) %collective-permute-start.23) | collective-permute-done | bytes 2097184 | tf_op jit(solution)/shard_map/ppermute | solution.py:310
  54.6 10.8 %collective-permute-done.3.z3 = bf16[4,224,384]{2,1,0:T(8,128)(2,1)} collective-permute-done((bf16[4,224,384]{2,1,0:T(8,128)(2,1)S(1)}, bf16[4,224,384]{2,1,0:T(8,128)(2,1)}, u32[]{:S(2)}, u32[]{:S(2)}) %collective-permute-start.3) | collective-permute-done | bytes 688160 | tf_op jit(solution)/shard_map/ppermute | solution.py:24
  65.7 3.0 %collective-permute-start.8 = (bf16[384,512]{1,0:T(8,128)(2,1)S(1)}, bf16[384,512]{1,0:T(8,128)(2,1)}, u32[]{:S(2)}, u32[]{:S(2)}) collective-permute-start(bf16[384,512]{1,0:T(8,128)(2,1)S(1)} %join.1.c0), channel_id=1, source_target_pairs={{0,96},{1,25},{2,98},{3,27},{4,100},{5,29},{6,102},{7,31},{8,104},... | collective-permute-start | bytes 1179656 | tf_op jit(solution)/shard_map/ppermute | solution.py:36
  69.2 9.4 %collective-permute-done.7.c1 = bf16[384,512]{1,0:T(8,128)(2,1)S(1)} collective-permute-done((bf16[384,512]{1,0:T(8,128)(2,1)S(1)}, bf16[384,512]{1,0:T(8,128)(2,1)S(1)}, u32[]{:S(2)}, u32[]{:S(2)}) %collective-permute-start.7) | collective-permute-done | bytes 393248 | tf_op jit(solution)/shard_map/ppermute | solution.py:36
  79.2 4.1 %shard_map.85.acc = f32[4,224,512]{2,1,0:T(8,128)S(1)} custom-call(s32[1]{0:T(128)} %bitcast.5.s_ref, bf16[4,224,384]{2,1,0:T(8,128)(2,1)} %copy-done, bf16[4,224,384]{2,1,0:T(8,128)(2,1)} %copy-done.6, bf16[4,224,384]{2,1,0:T(8,128)(2,1)} %copy-done.7, bf16[4,224,384]{2,1,0:T(8,128)(2,1)} %copy-done.1, bf16[4,224,384]{2,1,0:T(8,128)(2,1)} %copy-done.8, ...), custom_call_target="tpu_custom_call" | custom-call | tf_op jit(solution)/shard_map/pallas_call | solution.py:171
  83.3 1.7 %shard_map.86 = (f32[224,512]{1,0:T(8,128)S(1)}, bf16[224,512]{1,0:T(8,128)(2,1)S(1)}, bf16[224,512]{1,0:T(8,128)(2,1)S(1)}, bf16[224,512]{1,0:T(8,128)(2,1)S(1)}) custom-call(s32[1]{0:T(128)} %bitcast.5.s_ref, f32[4,224,512]{2,1,0:T(8,128)S(1)} %shard_map.85.acc, bf16[384,512]{1,0:T(8,128)(2,1)} %collective-permute-done.9.coords, ...), custom_call_target="tpu_custom_call" | custom-call | tf_op jit(solution)/shard_map/pallas_call | solution.py:197
  85.5 4.9 %collective-permute-start.13 = (bf16[224,512]{1,0:T(8,128)(2,1)S(1)}, bf16[224,512]{1,0:T(8,128)(2,1)S(1)}, u32[]{:S(2)}, u32[]{:S(2)}) collective-permute-start(bf16[224,512]{1,0:T(8,128)(2,1)S(1)} %get-tuple-element.37), channel_id=1, source_target_pairs={{0,16},{1,65},{2,18},{3,67},{4,20},{5,69},{6,22},{7,71},{8,24},{9,... | collective-permute-start | bytes 688136 | tf_op jit(solution)/shard_map/ppermute | solution.py:36
  90.4 3.1 %shard_map.87.acc = f32[4,224,512]{2,1,0:T(8,128)S(1)} custom-call(s32[1]{0:T(128)} %bitcast.2.s_ref, bf16[4,224,384]{2,1,0:T(8,128)(2,1)} %copy-done, bf16[4,224,384]{2,1,0:T(8,128)(2,1)} %copy-done.6, bf16[4,224,384]{2,1,0:T(8,128)(2,1)} %copy-done.7, bf16[4,224,384]{2,1,0:T(8,128)(2,1)} %copy-done.1, bf16[4,224,384]{2,1,0:T(8,128)(2,1)} %copy-done.8, ...), custom_call_target="tpu_custom_call" | custom-call | tf_op jit(solution)/shard_map/pallas_call | solution.py:171
  93.4 2.4 %shard_map.88 = (f32[224,512]{1,0:T(8,128)S(1)}, bf16[224,512]{1,0:T(8,128)(2,1)}, bf16[224,512]{1,0:T(8,128)(2,1)}, bf16[224,512]{1,0:T(8,128)(2,1)S(1)}) custom-call(s32[1]{0:T(128)} %bitcast.2.s_ref, f32[4,224,512]{2,1,0:T(8,128)S(1)} %shard_map.87.acc, bf16[384,512]{1,0:T(8,128)(2,1)} %collective-permute-done.17.coords, ...), custom_call_target="tpu_custom_call" | custom-call | tf_op jit(solution)/shard_map/pallas_call | solution.py:197
  96.8 3.9 %collective-permute-start.19 = (bf16[224,512]{1,0:T(8,128)(2,1)}, bf16[224,512]{1,0:T(8,128)(2,1)S(1)}, u32[]{:S(2)}, u32[]{:S(2)}) collective-permute-start(bf16[224,512]{1,0:T(8,128)(2,1)} %get-tuple-element.41), channel_id=1, source_target_pairs={{0,64},{1,17},{2,66},{3,19},{4,68},{5,21},{6,70},{7,23},{8,72},{9,... | collective-permute-start | bytes 688136 | tf_op jit(solution)/shard_map/ppermute | solution.py:36
  101.3 2.0 %collective-permute-done.18.t1 = bf16[224,512]{1,0:T(8,128)(2,1)S(1)} collective-permute-done((bf16[224,512]{1,0:T(8,128)(2,1)}, bf16[224,512]{1,0:T(8,128)(2,1)S(1)}, u32[]{:S(2)}, u32[]{:S(2)}) %collective-permute-start.18) | collective-permute-done | bytes 229408 | tf_op jit(solution)/shard_map/ppermute | solution.py:36
  103.4 3.9 %collective-permute-done.19.t2 = bf16[224,512]{1,0:T(8,128)(2,1)S(1)} collective-permute-done((bf16[224,512]{1,0:T(8,128)(2,1)}, bf16[224,512]{1,0:T(8,128)(2,1)S(1)}, u32[]{:S(2)}, u32[]{:S(2)}) %collective-permute-start.19) | collective-permute-done | bytes 229408 | tf_op jit(solution)/shard_map/ppermute | solution.py:36
  109.0 2.3 %keep.1 = (bf16[2048,512]{1,0:T(8,128)(2,1)S(1)}, bf16[2048,512]{1,0:T(8,128)(2,1)S(1)}) custom-call(bf16[2048,512]{1,0:T(8,128)(2,1)} %a.1, bf16[2048,512]{1,0:T(8,128)(2,1)} %collective-permute-done.22.b), custom_call_target="tpu_custom_call" | custom-call | tf_op jit(solution)/shard_map/keep/pallas_call | solution.py:129
  111.3 3.7 %collective-permute-done.21.got = bf16[224,512]{1,0:T(8,128)(2,1)S(1)} collective-permute-done((bf16[224,512]{1,0:T(8,128)(2,1)S(1)}, bf16[224,512]{1,0:T(8,128)(2,1)S(1)}, u32[]{:S(2)}, u32[]{:S(2)}) %collective-permute-start.21) | collective-permute-done | bytes 229408 | tf_op jit(solution)/shard_map/ppermute | solution.py:24
  115.0 6.7 %last.1 = (f32[224,512]{1,0:T(8,128)}, f32[224,512]{1,0:T(8,128)}, bf16[224,8192]{1,0:T(8,128)(2,1)}) custom-call(s32[4]{0:T(128)S(1)} %pad_add_fusion.s_ref, f32[224,512]{1,0:T(8,128)S(1)} %get-tuple-element.43.mine, bf16[224,512]{1,0:T(8,128)(2,1)S(1)} %collective-permute-done.21.got, f32[224,512]{1,0:T(8,128)S(1)} %copy-done.2, f32[224,512]{1,0:T(8,128)S(1)} %copy-done.3, ...), custom_call_target="tpu_custom_call" | custom-call | tf_op jit(solution)/shard_map/last/pallas_call | solution.py:277
  (56 shorter events, 8.6 us)
Async XLA Ops:
  0.6 53.4 %collective-permute-start.23 = (bf16[2048,512]{1,0:T(8,128)(2,1)}, bf16[2048,512]{1,0:T(8,128)(2,1)}, u32[]{:S(2)}, u32[]{:S(2)}) collective-permute-start(bf16[2048,512]{1,0:T(8,128)(2,1)} %a.1), channel_id=1, source_target_pairs={{0,6},{6,0},{2,4},{4,2},{1,7},{7,1},{3,5},{5,3},{8,14},{14,8},{10,... | collective-permute-start | bytes 6291464 | tf_op jit(solution)/shard_map/ppermute | solution.py:310
  13.0 19.0 %collective-permute-start = (bf16[4,224,384]{2,1,0:T(8,128)(2,1)S(1)}, bf16[4,224,384]{2,1,0:T(8,128)(2,1)S(1)}, u32[]{:S(2)}, u32[]{:S(2)}) collective-permute-start(bf16[4,224,384]{2,1,0:T(8,128)(2,1)S(1)} %get-tuple-element.26), channel_id=1, source_target_pairs={{0,32},{32,64},{64,96},{96,0},{1,33},{33,65},{65,97},{97,1},{2,34}... | collective-permute-start | bytes 2064392 | tf_op jit(solution)/shard_map/ppermute | solution.py:24
  14.6 21.5 %collective-permute-start.1 = (bf16[4,224,384]{2,1,0:T(8,128)(2,1)S(1)}, bf16[4,224,384]{2,1,0:T(8,128)(2,1)S(1)}, u32[]{:S(2)}, u32[]{:S(2)}) collective-permute-start(bf16[4,224,384]{2,1,0:T(8,128)(2,1)S(1)} %get-tuple-element.27), channel_id=1, source_target_pairs={{0,96},{32,0},{64,32},{96,64},{1,97},{33,1},{65,33},{97,65},{2,98}... | collective-permute-start | bytes 2064392 | tf_op jit(solution)/shard_map/ppermute | solution.py:24
  16.3 21.6 %collective-permute-start.2 = (bf16[4,224,384]{2,1,0:T(8,128)(2,1)S(1)}, bf16[4,224,384]{2,1,0:T(8,128)(2,1)S(1)}, u32[]{:S(2)}, u32[]{:S(2)}) collective-permute-start(bf16[4,224,384]{2,1,0:T(8,128)(2,1)S(1)} %get-tuple-element.29), channel_id=1, source_target_pairs={{0,8},{8,16},{16,24},{24,0},{1,9},{9,17},{17,25},{25,1},{2,10},{10... | collective-permute-start | bytes 2064392 | tf_op jit(solution)/shard_map/ppermute | solution.py:24
  18.3 8.1 %collective-permute-start.5 = (bf16[384,256]{1,0:T(8,128)(2,1)S(1)}, bf16[384,256]{1,0:T(8,128)(2,1)S(1)}, u32[]{:S(2)}, u32[]{:S(2)}) collective-permute-start(bf16[384,256]{1,0:T(8,128)(2,1)S(1)} %get-tuple-element.47), channel_id=1, source_target_pairs={{0,2},{2,0},{1,3},{3,1},{4,6},{6,4},{5,7},{7,5},{8,10},{10,8},{9,1... | collective-permute-start | bytes 589832 | tf_op jit(solution)/shard_map/ppermute | solution.py:24
  26.4 13.2 %collective-permute-start.6 = (bf16[384,256]{1,0:T(8,128)(2,1)S(1)}, bf16[384,256]{1,0:T(8,128)(2,1)S(1)}, u32[]{:S(2)}, u32[]{:S(2)}) collective-permute-start(bf16[384,256]{1,0:T(8,128)(2,1)S(1)} %add_convert_fusion.half), channel_id=1, source_target_pairs={{0,1},{1,0},{2,3},{3,2},{4,5},{5,4},{6,7},{7,6},{8,9},{9,8},{10,11... | collective-permute-start | bytes 589832 | tf_op jit(solution)/shard_map/ppermute | solution.py:24
  32.1 33.3 %collective-permute-start.3 = (bf16[4,224,384]{2,1,0:T(8,128)(2,1)S(1)}, bf16[4,224,384]{2,1,0:T(8,128)(2,1)}, u32[]{:S(2)}, u32[]{:S(2)}) collective-permute-start(bf16[4,224,384]{2,1,0:T(8,128)(2,1)S(1)} %get-tuple-element.30), channel_id=1, source_target_pairs={{0,24},{8,0},{16,8},{24,16},{1,25},{9,1},{17,9},{25,17},{2,26},{10... | collective-permute-start | bytes 2064392 | tf_op jit(solution)/shard_map/ppermute | solution.py:24
  36.1 29.6 %collective-permute-start.10 = (bf16[4,224,384]{2,1,0:T(8,128)(2,1)S(1)}, bf16[4,224,384]{2,1,0:T(8,128)(2,1)S(1)}, u32[]{:S(2)}, u32[]{:S(2)}) collective-permute-start(bf16[4,224,384]{2,1,0:T(8,128)(2,1)S(1)} %get-tuple-element.33), channel_id=1, source_target_pairs={{0,64},{32,96},{64,0},{96,32},{1,65},{33,97},{65,1},{97,33},{2,66}... | collective-permute-start | bytes 2064392 | tf_op jit(solution)/shard_map/ppermute | solution.py:24
  38.8 29.8 %collective-permute-start.11 = (bf16[4,224,384]{2,1,0:T(8,128)(2,1)S(1)}, bf16[4,224,384]{2,1,0:T(8,128)(2,1)S(1)}, u32[]{:S(2)}, u32[]{:S(2)}) collective-permute-start(bf16[4,224,384]{2,1,0:T(8,128)(2,1)S(1)} %get-tuple-element.34), channel_id=1, source_target_pairs={{0,16},{8,24},{16,0},{24,8},{1,17},{9,25},{17,1},{25,9},{2,18},{10... | collective-permute-start | bytes 2064392 | tf_op jit(solution)/shard_map/ppermute | solution.py:24
  39.6 69.4 %collective-permute-start.22 = (bf16[2048,512]{1,0:T(8,128)(2,1)}, bf16[2048,512]{1,0:T(8,128)(2,1)}, u32[]{:S(2)}, u32[]{:S(2)}) collective-permute-start(bf16[2048,512]{1,0:T(8,128)(2,1)} %a.1), channel_id=1, source_target_pairs={{0,1},{1,0},{2,3},{3,2},{4,5},{5,4},{6,7},{7,6},{8,9},{9,8},{10,11... | collective-permute-start | bytes 6291464 | tf_op jit(solution)/shard_map/ppermute | solution.py:24
  54.0 61.0 %collective-permute-start.24 = (bf16[2048,512]{1,0:T(8,128)(2,1)}, bf16[2048,512]{1,0:T(8,128)(2,1)}, u32[]{:S(2)}, u32[]{:S(2)}) collective-permute-start(bf16[2048,512]{1,0:T(8,128)(2,1)} %collective-permute-done.23.w3), channel_id=1, source_target_pairs={{0,1},{1,0},{2,3},{3,2},{4,5},{5,4},{6,7},{7,6},{8,9},{9,8},{10,11... | collective-permute-start | bytes 6291464 | tf_op jit(solution)/shard_map/ppermute | solution.py:24
  65.4 13.2 %collective-permute-start.7 = (bf16[384,512]{1,0:T(8,128)(2,1)S(1)}, bf16[384,512]{1,0:T(8,128)(2,1)S(1)}, u32[]{:S(2)}, u32[]{:S(2)}) collective-permute-start(bf16[384,512]{1,0:T(8,128)(2,1)S(1)} %join.1.c0), channel_id=1, source_target_pairs={{0,32},{1,9},{2,34},{3,11},{4,36},{5,13},{6,38},{7,15},{8,40},{9,1... | collective-permute-start | bytes 1179656 | tf_op jit(solution)/shard_map/ppermute | solution.py:36
  65.7 12.9 %collective-permute-start.8 = (bf16[384,512]{1,0:T(8,128)(2,1)S(1)}, bf16[384,512]{1,0:T(8,128)(2,1)}, u32[]{:S(2)}, u32[]{:S(2)}) collective-permute-start(bf16[384,512]{1,0:T(8,128)(2,1)S(1)} %join.1.c0), channel_id=1, source_target_pairs={{0,96},{1,25},{2,98},{3,27},{4,100},{5,29},{6,102},{7,31},{8,104},... | collective-permute-start | bytes 1179656 | tf_op jit(solution)/shard_map/ppermute | solution.py:36
  68.6 10.5 %collective-permute-start.9 = (bf16[384,512]{1,0:T(8,128)(2,1)S(1)}, bf16[384,512]{1,0:T(8,128)(2,1)}, u32[]{:S(2)}, u32[]{:S(2)}) collective-permute-start(bf16[384,512]{1,0:T(8,128)(2,1)S(1)} %join.1.c0), channel_id=1, source_target_pairs={{0,64},{1,17},{2,66},{3,19},{4,68},{5,21},{6,70},{7,23},{8,72},{9,... | collective-permute-start | bytes 1179656 | tf_op jit(solution)/shard_map/ppermute | solution.py:36
  78.6 6.4 %collective-permute-start.15 = (bf16[384,512]{1,0:T(8,128)(2,1)S(1)}, bf16[384,512]{1,0:T(8,128)(2,1)S(1)}, u32[]{:S(2)}, u32[]{:S(2)}) collective-permute-start(bf16[384,512]{1,0:T(8,128)(2,1)S(1)} %collective-permute-done.7.c1), channel_id=1, source_target_pairs={{0,1},{1,0},{2,3},{3,2},{4,5},{5,4},{6,7},{7,6},{8,9},{9,8},{10,11... | collective-permute-start | bytes 1179656 | tf_op jit(solution)/shard_map/ppermute | solution.py:24
  78.6 6.9 %collective-permute-start.16 = (bf16[384,512]{1,0:T(8,128)(2,1)}, bf16[384,512]{1,0:T(8,128)(2,1)S(1)}, u32[]{:S(2)}, u32[]{:S(2)}) collective-permute-start(bf16[384,512]{1,0:T(8,128)(2,1)} %collective-permute-done.8.c3), channel_id=1, source_target_pairs={{0,1},{1,0},{2,3},{3,2},{4,5},{5,4},{6,7},{7,6},{8,9},{9,8},{10,11... | collective-permute-start | bytes 1179656 | tf_op jit(solution)/shard_map/ppermute | solution.py:24
  79.1 11.2 %collective-permute-start.17 = (bf16[384,512]{1,0:T(8,128)(2,1)}, bf16[384,512]{1,0:T(8,128)(2,1)}, u32[]{:S(2)}, u32[]{:S(2)}) collective-permute-start(bf16[384,512]{1,0:T(8,128)(2,1)} %collective-permute-done.9.coords), channel_id=1, source_target_pairs={{0,1},{1,0},{2,3},{3,2},{4,5},{5,4},{6,7},{7,6},{8,9},{9,8},{10,11... | collective-permute-start | bytes 1179656 | tf_op jit(solution)/shard_map/ppermute | solution.py:24
  85.0 10.8 %collective-permute-start.12 = (bf16[224,512]{1,0:T(8,128)(2,1)S(1)}, bf16[224,512]{1,0:T(8,128)(2,1)S(1)}, u32[]{:S(2)}, u32[]{:S(2)}) collective-permute-start(bf16[224,512]{1,0:T(8,128)(2,1)S(1)} %get-tuple-element.36), channel_id=1, source_target_pairs={{0,8},{1,33},{2,10},{3,35},{4,12},{5,37},{6,14},{7,39},{8,16},{9,4... | collective-permute-start | bytes 688136 | tf_op jit(solution)/shard_map/ppermute | solution.py:36
  85.5 11.3 %collective-permute-start.13 = (bf16[224,512]{1,0:T(8,128)(2,1)S(1)}, bf16[224,512]{1,0:T(8,128)(2,1)S(1)}, u32[]{:S(2)}, u32[]{:S(2)}) collective-permute-start(bf16[224,512]{1,0:T(8,128)(2,1)S(1)} %get-tuple-element.37), channel_id=1, source_target_pairs={{0,16},{1,65},{2,18},{3,67},{4,20},{5,69},{6,22},{7,71},{8,24},{9,... | collective-permute-start | bytes 688136 | tf_op jit(solution)/shard_map/ppermute | solution.py:36
  90.4 10.3 %collective-permute-start.14 = (bf16[224,512]{1,0:T(8,128)(2,1)S(1)}, bf16[224,512]{1,0:T(8,128)(2,1)S(1)}, u32[]{:S(2)}, u32[]{:S(2)}) collective-permute-start(bf16[224,512]{1,0:T(8,128)(2,1)S(1)} %get-tuple-element.38), channel_id=1, source_target_pairs={{0,24},{1,97},{2,26},{3,99},{4,28},{5,101},{6,30},{7,103},{8,0},{9... | collective-permute-start | bytes 688136 | tf_op jit(solution)/shard_map/ppermute | solution.py:36
  95.8 7.5 %collective-permute-start.18 = (bf16[224,512]{1,0:T(8,128)(2,1)}, bf16[224,512]{1,0:T(8,128)(2,1)S(1)}, u32[]{:S(2)}, u32[]{:S(2)}) collective-permute-start(bf16[224,512]{1,0:T(8,128)(2,1)} %get-tuple-element.40), channel_id=1, source_target_pairs={{0,32},{1,9},{2,34},{3,11},{4,36},{5,13},{6,38},{7,15},{8,40},{9,1... | collective-permute-start | bytes 688136 | tf_op jit(solution)/shard_map/ppermute | solution.py:36
  96.8 10.5 %collective-permute-start.19 = (bf16[224,512]{1,0:T(8,128)(2,1)}, bf16[224,512]{1,0:T(8,128)(2,1)S(1)}, u32[]{:S(2)}, u32[]{:S(2)}) collective-permute-start(bf16[224,512]{1,0:T(8,128)(2,1)} %get-tuple-element.41), channel_id=1, source_target_pairs={{0,64},{1,17},{2,66},{3,19},{4,68},{5,21},{6,70},{7,23},{8,72},{9,... | collective-permute-start | bytes 688136 | tf_op jit(solution)/shard_map/ppermute | solution.py:36
  101.3 6.3 %collective-permute-start.20 = (bf16[224,512]{1,0:T(8,128)(2,1)S(1)}, bf16[224,512]{1,0:T(8,128)(2,1)S(1)}, u32[]{:S(2)}, u32[]{:S(2)}) collective-permute-start(bf16[224,512]{1,0:T(8,128)(2,1)S(1)} %get-tuple-element.42), channel_id=1, source_target_pairs={{0,96},{1,25},{2,98},{3,27},{4,100},{5,29},{6,102},{7,31},{8,104},... | collective-permute-start | bytes 688136 | tf_op jit(solution)/shard_map/ppermute | solution.py:36
  108.9 6.1 %collective-permute-start.21 = (bf16[224,512]{1,0:T(8,128)(2,1)S(1)}, bf16[224,512]{1,0:T(8,128)(2,1)S(1)}, u32[]{:S(2)}, u32[]{:S(2)}) collective-permute-start(bf16[224,512]{1,0:T(8,128)(2,1)S(1)} %get-tuple-element.44), channel_id=1, source_target_pairs={{0,4},{4,0},{1,5},{5,1},{2,6},{6,2},{3,7},{7,3},{8,12},{12,8},{9,1... | collective-permute-start | bytes 688136 | tf_op jit(solution)/shard_map/ppermute | solution.py:24
  (10 other events, 242.6 us)

commit v8 on v7

--- a/solution.py
+++ b/solution.py
@@ -147,16 +147,15 @@
     return pltpu.make_async_copy(piece_x, dst, sem)
 
 
-def early_kernel(s_ref, x0, x1, x3, z0, z1, z3, c0, c1, c3, out, lhs, rhs, sem):
-    pairs = ((x0, z0), (x1, z1), (x3, z3))
+def early_kernel(s_ref, x0, x2, z0, z2, c0, c2, out, lhs, rhs, sem):
     loads = [
         [
             load(s_ref[0], a.at[j], b.at[j], lhs.at[j, :, pl.ds(n * 384, 384)], sem.at[j, n])
-            for n, (a, b) in enumerate(pairs)
+            for n, (a, b) in enumerate(((x0, z0), (x2, z2)))
         ]
         for j in range(4)
     ]
-    for n, coords in enumerate((c0, c1, c3)):
+    for n, coords in enumerate((c0, c2)):
         rhs[n * 384 : n * 384 + 384, :] = coords[...]
     for j in range(4):
         for copy in loads[j]:
@@ -170,36 +169,37 @@
     args += [pltpu.with_memory_space_constraint(a, pltpu.VMEM) for a in coords]
     return pl.pallas_call(
         early_kernel,
-        in_specs=[SMEM] + [HBM] * 6 + [VMEM] * 3,
+        in_specs=[SMEM] + [HBM] * 4 + [VMEM] * 2,
         out_specs=VMEM,
         out_shape=pltpu.VMEM((4, 224, 512), F32),
         scratch_shapes=[
-            pltpu.VMEM((4, 224, 3 * t), BF16),
-            pltpu.VMEM((3 * t, 512), BF16),
-            pltpu.SemaphoreType.DMA((4, 3)),
+            pltpu.VMEM((4, 224, 2 * t), BF16),
+            pltpu.VMEM((2 * t, 512), BF16),
+            pltpu.SemaphoreType.DMA((4, 2)),
         ],
         compiler_params=params(8),
     )(use_x.reshape(1), *args)
 
 
-def late_kernel(s_ref, acc, coords, x2, z2, o0, o1, o2, o3):
-    for use, piece in ((1, x2), (0, z2)):
+def late_kernel(s_ref, acc, c1, c3, x1, x3, z1, z3, o0, o1, o2, o3):
+    for use, ones, threes in ((1, x1, x3), (0, z1, z3)):
 
         @pl.when(s_ref[0] == use)
         def _():
             for j, out in enumerate((o0, o1, o2, o3)):
-                part = acc[j] + jnp.dot(piece[j], coords[...], preferred_element_type=F32)
+                part = acc[j] + jnp.dot(ones[j], c1[...], preferred_element_type=F32)
+                part += jnp.dot(threes[j], c3[...], preferred_element_type=F32)
                 out[...] = part.astype(out.dtype)
 
 
 def late_sums(use_x, acc, coords, pieces):
-    args = [pltpu.with_memory_space_constraint(a, pltpu.VMEM) for a in (acc, coords, *pieces)]
+    args = [pltpu.with_memory_space_constraint(a, pltpu.VMEM) for a in (acc, *coords, *pieces)]
     return pl.pallas_call(
         late_kernel,
-        in_specs=[SMEM] + [VMEM] * 4,
+        in_specs=[SMEM] + [VMEM] * 7,
         out_specs=[VMEM] * 4,
         out_shape=[pltpu.VMEM((224, 512), F32)] + [pltpu.VMEM((224, 512), BF16)] * 3,
-        compiler_params=params(4),
+        compiler_params=params(6),
     )(use_x.reshape(1), *args)
 
 
@@ -311,11 +311,12 @@
     beside_w = shift(projector, "c", 1)
     across_w = shift(near_w, "c", 1)
 
-    near = [got[k] for got in (got_x, got_z) for k in (0, 1, 3)]
+    first = [got[k] for got in (got_x, got_z) for k in (0, 2)]
+    then = [got[k] for got in (got_x, got_z) for k in (1, 3)]
     sums = []
     for use_x, coords, axis in ((1 - c, along, "z"), (c, beyond, "x")):
-        acc = early_sums(use_x, near, (own, coords[1], coords[3]))
-        part = late_sums(use_x, acc, coords[2], (got_x[2], got_z[2]))
+        acc = early_sums(use_x, first, (own, coords[2]))
+        part = late_sums(use_x, acc, (coords[1], coords[3]), then)
         sums.append([part[0]] + [cross(part[k], axis, k) for k in (1, 2, 3)])
     keep, give = combine(1 - jnp.bitwise_xor(c, yl), *sums)
     got = shift(give, "yl", 1)

time: 122 us -> 128 us (1.049)
  local copies, waits for them, and re-layouts: 2.56 us -> 10.2 us
  waiting for transfers between devices: 57.7 us -> 50.4 us
  starting transfers between devices: 30.4 us -> 35.2 us
    ppermute x1, waiting for transfers between devices: 14.4 us -> 2.37 us  [step(): lax.ppermute(projector, ('yl', 'yh'), [(0, 3), (3, 0), (1, 2), (2, 1)])]
    unnamed x18 -> x32, local copies, waits for them, and re-layouts: 2.56 us -> 10.2 us
    ppermute x15, waiting for transfers between devices: 27.5 us -> 34.8 us  [shift(): return lax.ppermute(a, axis, [(i, (i + k) % n) for i in range(n)])]
    ppermute x15, starting transfers between devices: 13.4 us -> 16.3 us  [shift(): return lax.ppermute(a, axis, [(i, (i + k) % n) for i in range(n)])]
    ppermute x9, waiting for transfers between devices: 15.9 us -> 13.2 us  [cross(): return lax.ppermute(a, AXES, pairs)]
    ppermute x9, starting transfers between devices: 13.8 us -> 15.7 us  [cross(): return lax.ppermute(a, AXES, pairs)]
where the time goes in v8:
time: 128 us
  waiting for transfers between devices  50.4 us (39%)
  starting transfers between devices  35.2 us (28%)
  Pallas kernels  31 us (24%)
  local copies, waits for them, and re-layouts  10.2 us (8%)
    ppermute x15, waiting for transfers between devices, shift(): return lax.ppermute(a, axis, [(i, (i + k) % n) for i in range(n)])  34.8 us
    ppermute x15, starting transfers between devices, shift(): return lax.ppermute(a, axis, [(i, (i + k) % n) for i in range(n)])  16.3 us
    ppermute x9, starting transfers between devices, cross(): return lax.ppermute(a, AXES, pairs)  15.7 us
    ppermute x9, waiting for transfers between devices, cross(): return lax.ppermute(a, AXES, pairs)  13.2 us
    unnamed x32, local copies, waits for them, and re-layouts  10.2 us
    pallas_call x1, Pallas kernels, front(): pl.pallas_call(front_kernel, grid_spec=pltpu.PrefetchScalarGridSpec(num_s...  8.99 us
    pallas_call x2, Pallas kernels, early_sums(): pl.pallas_call(early_kernel, in_specs=[SMEM] + [HBM] * 4 + [VMEM] * 2, ou...  6.95 us
    pallas_call x1, Pallas kernels, last_stage(): pl.pallas_call(last_kernel, in_specs=[SMEM] + [VMEM] * 7 + [HBM], out_spe...  6.65 us
  transfers between devices with their start and end apart: 25, of which 10 were waited for; matrix products, arithmetic and copies ran while one was open for 0% of the time, Pallas kernels for 19%

profile of v8, /device:TPU:0, one launch (start us, length us, event | category | flops | bytes accessed | tf_op | source)
XLA Modules:
  0.0 127.9 jit_solution(2448070152711337474)
XLA Ops:
  0.6 3.2 %collective-permute-start.23 = (bf16[2048,512]{1,0:T(8,128)(2,1)}, bf16[2048,512]{1,0:T(8,128)(2,1)}, u32[]{:S(2)}, u32[]{:S(2)}) collective-permute-start(bf16[2048,512]{1,0:T(8,128)(2,1)} %a.1), channel_id=1, source_target_pairs={{0,6},{6,0},{2,4},{4,2},{1,7},{7,1},{3,5},{5,3},{8,14},{14,8},{10,... | collective-permute-start | bytes 6291464 | tf_op jit(solution)/shard_map/ppermute | solution.py:310
  3.9 9.0 %front.1 = (f32[384,256]{1,0:T(8,128)S(1)}, f32[384,256]{1,0:T(8,128)S(1)}, bf16[4,224,384]{2,1,0:T(8,128)(2,1)S(1)}, bf16[4,224,384]{2,1,0:T(8,128)(2,1)S(1)}, ...) custom-call(s32[4]{0:T(128)S(1)} %pad_add_fusion.s_ref, ...), custom_call_target="tpu_custom_call" | custom-call | tf_op jit(solution)/shard_map/front/pallas_call | solution.py:77
  13.0 3.1 %collective-permute-start = (bf16[4,224,384]{2,1,0:T(8,128)(2,1)S(1)}, bf16[4,224,384]{2,1,0:T(8,128)(2,1)S(1)}, u32[]{:S(2)}, u32[]{:S(2)}) collective-permute-start(bf16[4,224,384]{2,1,0:T(8,128)(2,1)S(1)} %get-tuple-element.26), channel_id=1, source_target_pairs={{0,64},{32,96},{64,0},{96,32},{1,65},{33,97},{65,1},{97,33},{2,66}... | collective-permute-start | bytes 2064392 | tf_op jit(solution)/shard_map/ppermute | solution.py:24
  16.1 3.9 %collective-permute-start.1 = (bf16[4,224,384]{2,1,0:T(8,128)(2,1)S(1)}, bf16[4,224,384]{2,1,0:T(8,128)(2,1)S(1)}, u32[]{:S(2)}, u32[]{:S(2)}) collective-permute-start(bf16[4,224,384]{2,1,0:T(8,128)(2,1)S(1)} %get-tuple-element.28), channel_id=1, source_target_pairs={{0,16},{8,24},{16,0},{24,8},{1,17},{9,25},{17,1},{25,9},{2,18},{10... | collective-permute-start | bytes 2064392 | tf_op jit(solution)/shard_map/ppermute | solution.py:24
  21.8 7.4 %collective-permute-done.3 = bf16[384,256]{1,0:T(8,128)(2,1)S(1)} collective-permute-done((bf16[384,256]{1,0:T(8,128)(2,1)S(1)}, bf16[384,256]{1,0:T(8,128)(2,1)S(1)}, u32[]{:S(2)}, u32[]{:S(2)}) %collective-permute-start.3) | collective-permute-done | bytes 196640 | tf_op jit(solution)/shard_map/ppermute | solution.py:24
  29.3 3.1 %collective-permute-done.x2 = bf16[4,224,384]{2,1,0:T(8,128)(2,1)S(1)} collective-permute-done((bf16[4,224,384]{2,1,0:T(8,128)(2,1)S(1)}, bf16[4,224,384]{2,1,0:T(8,128)(2,1)S(1)}, u32[]{:S(2)}, u32[]{:S(2)}) %collective-permute-start) | collective-permute-done | bytes 688160 | tf_op jit(solution)/shard_map/ppermute | solution.py:24
  33.2 4.0 %collective-permute-start.11 = (bf16[4,224,384]{2,1,0:T(8,128)(2,1)S(1)}, bf16[4,224,384]{2,1,0:T(8,128)(2,1)S(1)}, u32[]{:S(2)}, u32[]{:S(2)}) collective-permute-start(bf16[4,224,384]{2,1,0:T(8,128)(2,1)S(1)} %get-tuple-element.34), channel_id=1, source_target_pairs={{0,24},{8,0},{16,8},{24,16},{1,25},{9,1},{17,9},{25,17},{2,26},{10... | collective-permute-start | bytes 2064392 | tf_op jit(solution)/shard_map/ppermute | solution.py:24
  39.6 10.8 %collective-permute-done.10.z1 = bf16[4,224,384]{2,1,0:T(8,128)(2,1)S(1)} collective-permute-done((bf16[4,224,384]{2,1,0:T(8,128)(2,1)S(1)}, bf16[4,224,384]{2,1,0:T(8,128)(2,1)S(1)}, u32[]{:S(2)}, u32[]{:S(2)}) %collective-permute-start.10) | collective-permute-done | bytes 688160 | tf_op jit(solution)/shard_map/ppermute | solution.py:24
  51.6 2.4 %collective-permute-done.23.w3 = bf16[2048,512]{1,0:T(8,128)(2,1)} collective-permute-done((bf16[2048,512]{1,0:T(8,128)(2,1)}, bf16[2048,512]{1,0:T(8,128)(2,1)}, u32[]{:S(2)}, u32[]{:S(2)}) %collective-permute-start.23) | collective-permute-done | bytes 2097184 | tf_op jit(solution)/shard_map/ppermute | solution.py:310
  54.6 3.1 %collective-permute-start.5 = (bf16[384,512]{1,0:T(8,128)(2,1)S(1)}, bf16[384,512]{1,0:T(8,128)(2,1)}, u32[]{:S(2)}, u32[]{:S(2)}) collective-permute-start(bf16[384,512]{1,0:T(8,128)(2,1)S(1)} %join.1.c0), channel_id=1, source_target_pairs={{0,64},{1,17},{2,66},{3,19},{4,68},{5,21},{6,70},{7,23},{8,72},{9,... | collective-permute-start | bytes 1179656 | tf_op jit(solution)/shard_map/ppermute | solution.py:36
  58.3 9.7 %collective-permute-done.9.x3 = bf16[4,224,384]{2,1,0:T(8,128)(2,1)S(1)} collective-permute-done((bf16[4,224,384]{2,1,0:T(8,128)(2,1)S(1)}, bf16[4,224,384]{2,1,0:T(8,128)(2,1)S(1)}, u32[]{:S(2)}, u32[]{:S(2)}) %collective-permute-start.9) | collective-permute-done | bytes 688160 | tf_op jit(solution)/shard_map/ppermute | solution.py:24
  67.9 2.4 %collective-permute-start.7 = (bf16[384,512]{1,0:T(8,128)(2,1)S(1)}, bf16[384,512]{1,0:T(8,128)(2,1)}, u32[]{:S(2)}, u32[]{:S(2)}) collective-permute-start(bf16[384,512]{1,0:T(8,128)(2,1)S(1)} %join.1.c0), channel_id=1, source_target_pairs={{0,96},{1,25},{2,98},{3,27},{4,100},{5,29},{6,102},{7,31},{8,104},... | collective-permute-start | bytes 1179656 | tf_op jit(solution)/shard_map/ppermute | solution.py:36
  70.8 7.8 %collective-permute-done.7.c3 = bf16[384,512]{1,0:T(8,128)(2,1)} collective-permute-done((bf16[384,512]{1,0:T(8,128)(2,1)S(1)}, bf16[384,512]{1,0:T(8,128)(2,1)}, u32[]{:S(2)}, u32[]{:S(2)}) %collective-permute-start.7) | collective-permute-done | bytes 393248 | tf_op jit(solution)/shard_map/ppermute | solution.py:36
  78.6 3.5 %shard_map.85.acc = f32[4,224,512]{2,1,0:T(8,128)S(1)} custom-call(s32[1]{0:T(128)} %bitcast.5.s_ref, bf16[4,224,384]{2,1,0:T(8,128)(2,1)} %copy-done, bf16[4,224,384]{2,1,0:T(8,128)(2,1)} %copy-done.14, bf16[4,224,384]{2,1,0:T(8,128)(2,1)} %copy-done.1, bf16[4,224,384]{2,1,0:T(8,128)(2,1)} %copy-done.15, bf16[384,512]{1,0:T(8,128)(2,1)S(1)} %join.1.c0, ...), custom_call_target="tpu_custom_call" | custom-call | tf_op jit(solution)/shard_map/pallas_call | solution.py:170
  82.1 2.3 %shard_map.86 = (f32[224,512]{1,0:T(8,128)S(1)}, bf16[224,512]{1,0:T(8,128)(2,1)S(1)}, bf16[224,512]{1,0:T(8,128)(2,1)S(1)}, bf16[224,512]{1,0:T(8,128)(2,1)S(1)}) custom-call(s32[1]{0:T(128)} %bitcast.5.s_ref, f32[4,224,512]{2,1,0:T(8,128)S(1)} %shard_map.85.acc, bf16[384,512]{1,0:T(8,128)(2,1)} %collective-permute-done.6.c1, ...), custom_call_target="tpu_custom_call" | custom-call | tf_op jit(solution)/shard_map/pallas_call | solution.py:197
  87.6 2.5 %collective-permute-start.14 = (bf16[224,512]{1,0:T(8,128)(2,1)S(1)}, bf16[224,512]{1,0:T(8,128)(2,1)S(1)}, u32[]{:S(2)}, u32[]{:S(2)}) collective-permute-start(bf16[224,512]{1,0:T(8,128)(2,1)S(1)} %get-tuple-element.38), channel_id=1, source_target_pairs={{0,24},{1,97},{2,26},{3,99},{4,28},{5,101},{6,30},{7,103},{8,0},{9... | collective-permute-start | bytes 688136 | tf_op jit(solution)/shard_map/ppermute | solution.py:36
  90.2 3.5 %shard_map.87.acc = f32[4,224,512]{2,1,0:T(8,128)S(1)} custom-call(s32[1]{0:T(128)} %bitcast.2.s_ref, bf16[4,224,384]{2,1,0:T(8,128)(2,1)} %copy-done, bf16[4,224,384]{2,1,0:T(8,128)(2,1)} %copy-done.14, bf16[4,224,384]{2,1,0:T(8,128)(2,1)} %copy-done.1, bf16[4,224,384]{2,1,0:T(8,128)(2,1)} %copy-done.15, bf16[384,512]{1,0:T(8,128)(2,1)S(1)} %join.1.c0, ...), custom_call_target="tpu_custom_call" | custom-call | tf_op jit(solution)/shard_map/pallas_call | solution.py:170
  93.7 3.0 %shard_map.88 = (f32[224,512]{1,0:T(8,128)S(1)}, bf16[224,512]{1,0:T(8,128)(2,1)}, bf16[224,512]{1,0:T(8,128)(2,1)}, bf16[224,512]{1,0:T(8,128)(2,1)}) custom-call(s32[1]{0:T(128)} %bitcast.2.s_ref, f32[4,224,512]{2,1,0:T(8,128)S(1)} %shard_map.87.acc, bf16[384,512]{1,0:T(8,128)(2,1)S(1)} %collective-permute-done.16.c1, ...), custom_call_target="tpu_custom_call" | custom-call | tf_op jit(solution)/shard_map/pallas_call | solution.py:197
  98.1 2.0 %collective-permute-start.18 = (bf16[224,512]{1,0:T(8,128)(2,1)}, bf16[224,512]{1,0:T(8,128)(2,1)S(1)}, u32[]{:S(2)}, u32[]{:S(2)}) collective-permute-start(bf16[224,512]{1,0:T(8,128)(2,1)} %get-tuple-element.40), channel_id=1, source_target_pairs={{0,32},{1,9},{2,34},{3,11},{4,36},{5,13},{6,38},{7,15},{8,40},{9,1... | collective-permute-start | bytes 688136 | tf_op jit(solution)/shard_map/ppermute | solution.py:36
  101.7 2.5 %collective-permute-start.20 = (bf16[224,512]{1,0:T(8,128)(2,1)}, bf16[224,512]{1,0:T(8,128)(2,1)S(1)}, u32[]{:S(2)}, u32[]{:S(2)}) collective-permute-start(bf16[224,512]{1,0:T(8,128)(2,1)} %get-tuple-element.42), channel_id=1, source_target_pairs={{0,96},{1,25},{2,98},{3,27},{4,100},{5,29},{6,102},{7,31},{8,104},... | collective-permute-start | bytes 688136 | tf_op jit(solution)/shard_map/ppermute | solution.py:36
  105.6 3.0 %collective-permute-done.19.t2 = bf16[224,512]{1,0:T(8,128)(2,1)S(1)} collective-permute-done((bf16[224,512]{1,0:T(8,128)(2,1)}, bf16[224,512]{1,0:T(8,128)(2,1)S(1)}, u32[]{:S(2)}, u32[]{:S(2)}) %collective-permute-start.19) | collective-permute-done | bytes 229408 | tf_op jit(solution)/shard_map/ppermute | solution.py:36
  114.9 2.3 %keep.1 = (bf16[2048,512]{1,0:T(8,128)(2,1)S(1)}, bf16[2048,512]{1,0:T(8,128)(2,1)S(1)}) custom-call(bf16[2048,512]{1,0:T(8,128)(2,1)} %a.1, bf16[2048,512]{1,0:T(8,128)(2,1)} %collective-permute-done.22.b), custom_call_target="tpu_custom_call" | custom-call | tf_op jit(solution)/shard_map/keep/pallas_call | solution.py:129
  117.2 3.9 %collective-permute-done.21.got = bf16[224,512]{1,0:T(8,128)(2,1)S(1)} collective-permute-done((bf16[224,512]{1,0:T(8,128)(2,1)S(1)}, bf16[224,512]{1,0:T(8,128)(2,1)S(1)}, u32[]{:S(2)}, u32[]{:S(2)}) %collective-permute-start.21) | collective-permute-done | bytes 229408 | tf_op jit(solution)/shard_map/ppermute | solution.py:24
  121.1 6.6 %last.1 = (f32[224,512]{1,0:T(8,128)}, f32[224,512]{1,0:T(8,128)}, bf16[224,8192]{1,0:T(8,128)(2,1)}) custom-call(s32[4]{0:T(128)S(1)} %pad_add_fusion.s_ref, f32[224,512]{1,0:T(8,128)S(1)} %get-tuple-element.43.mine, bf16[224,512]{1,0:T(8,128)(2,1)S(1)} %collective-permute-done.21.got, f32[224,512]{1,0:T(8,128)S(1)} %copy-done.6, f32[224,512]{1,0:T(8,128)S(1)} %copy-done.7, ...), custom_call_target="tpu_custom_call" | custom-call | tf_op jit(solution)/shard_map/last/pallas_call | solution.py:277
  (70 shorter events, 22.1 us)
Async XLA Ops:
  0.6 53.4 %collective-permute-start.23 = (bf16[2048,512]{1,0:T(8,128)(2,1)}, bf16[2048,512]{1,0:T(8,128)(2,1)}, u32[]{:S(2)}, u32[]{:S(2)}) collective-permute-start(bf16[2048,512]{1,0:T(8,128)(2,1)} %a.1), channel_id=1, source_target_pairs={{0,6},{6,0},{2,4},{4,2},{1,7},{7,1},{3,5},{5,3},{8,14},{14,8},{10,... | collective-permute-start | bytes 6291464 | tf_op jit(solution)/shard_map/ppermute | solution.py:310
  12.9 8.1 %collective-permute-start.2 = (f32[384,256]{1,0:T(8,128)S(1)}, f32[384,256]{1,0:T(8,128)S(1)}, u32[]{:S(2)}, u32[]{:S(2)}) collective-permute-start(f32[384,256]{1,0:T(8,128)S(1)} %get-tuple-element.30), channel_id=1, source_target_pairs={{0,1},{1,0},{2,3},{3,2},{4,5},{5,4},{6,7},{7,6},{8,9},{9,8},{10,11... | collective-permute-start | bytes 1179656 | tf_op jit(solution)/shard_map/ppermute | solution.py:24
  13.0 19.3 %collective-permute-start = (bf16[4,224,384]{2,1,0:T(8,128)(2,1)S(1)}, bf16[4,224,384]{2,1,0:T(8,128)(2,1)S(1)}, u32[]{:S(2)}, u32[]{:S(2)}) collective-permute-start(bf16[4,224,384]{2,1,0:T(8,128)(2,1)S(1)} %get-tuple-element.26), channel_id=1, source_target_pairs={{0,64},{32,96},{64,0},{96,32},{1,65},{33,97},{65,1},{97,33},{2,66}... | collective-permute-start | bytes 2064392 | tf_op jit(solution)/shard_map/ppermute | solution.py:24
  16.1 21.1 %collective-permute-start.1 = (bf16[4,224,384]{2,1,0:T(8,128)(2,1)S(1)}, bf16[4,224,384]{2,1,0:T(8,128)(2,1)S(1)}, u32[]{:S(2)}, u32[]{:S(2)}) collective-permute-start(bf16[4,224,384]{2,1,0:T(8,128)(2,1)S(1)} %get-tuple-element.28), channel_id=1, source_target_pairs={{0,16},{8,24},{16,0},{24,8},{1,17},{9,25},{17,1},{25,9},{2,18},{10... | collective-permute-start | bytes 2064392 | tf_op jit(solution)/shard_map/ppermute | solution.py:24
  20.0 30.5 %collective-permute-start.10 = (bf16[4,224,384]{2,1,0:T(8,128)(2,1)S(1)}, bf16[4,224,384]{2,1,0:T(8,128)(2,1)S(1)}, u32[]{:S(2)}, u32[]{:S(2)}) collective-permute-start(bf16[4,224,384]{2,1,0:T(8,128)(2,1)S(1)} %get-tuple-element.33), channel_id=1, source_target_pairs={{0,8},{8,16},{16,24},{24,0},{1,9},{9,17},{17,25},{25,1},{2,10},{10... | collective-permute-start | bytes 2064392 | tf_op jit(solution)/shard_map/ppermute | solution.py:24
  21.1 8.1 %collective-permute-start.3 = (bf16[384,256]{1,0:T(8,128)(2,1)S(1)}, bf16[384,256]{1,0:T(8,128)(2,1)S(1)}, u32[]{:S(2)}, u32[]{:S(2)}) collective-permute-start(bf16[384,256]{1,0:T(8,128)(2,1)S(1)} %get-tuple-element.47), channel_id=1, source_target_pairs={{0,2},{2,0},{1,3},{3,1},{4,6},{6,4},{5,7},{7,5},{8,10},{10,8},{9,1... | collective-permute-start | bytes 589832 | tf_op jit(solution)/shard_map/ppermute | solution.py:24
  29.2 22.4 %collective-permute-start.4 = (bf16[384,256]{1,0:T(8,128)(2,1)S(1)}, bf16[384,256]{1,0:T(8,128)(2,1)S(1)}, u32[]{:S(2)}, u32[]{:S(2)}) collective-permute-start(bf16[384,256]{1,0:T(8,128)(2,1)S(1)} %add_convert_fusion.half), channel_id=1, source_target_pairs={{0,1},{1,0},{2,3},{3,2},{4,5},{5,4},{6,7},{7,6},{8,9},{9,8},{10,11... | collective-permute-start | bytes 589832 | tf_op jit(solution)/shard_map/ppermute | solution.py:24
  33.2 21.4 %collective-permute-start.11 = (bf16[4,224,384]{2,1,0:T(8,128)(2,1)S(1)}, bf16[4,224,384]{2,1,0:T(8,128)(2,1)S(1)}, u32[]{:S(2)}, u32[]{:S(2)}) collective-permute-start(bf16[4,224,384]{2,1,0:T(8,128)(2,1)S(1)} %get-tuple-element.34), channel_id=1, source_target_pairs={{0,24},{8,0},{16,8},{24,16},{1,25},{9,1},{17,9},{25,17},{2,26},{10... | collective-permute-start | bytes 2064392 | tf_op jit(solution)/shard_map/ppermute | solution.py:24
  38.2 19.5 %collective-permute-start.8 = (bf16[4,224,384]{2,1,0:T(8,128)(2,1)S(1)}, bf16[4,224,384]{2,1,0:T(8,128)(2,1)S(1)}, u32[]{:S(2)}, u32[]{:S(2)}) collective-permute-start(bf16[4,224,384]{2,1,0:T(8,128)(2,1)S(1)} %get-tuple-element.31), channel_id=1, source_target_pairs={{0,32},{32,64},{64,96},{96,0},{1,33},{33,65},{65,97},{97,1},{2,34}... | collective-permute-start | bytes 2064392 | tf_op jit(solution)/shard_map/ppermute | solution.py:24
  50.5 17.5 %collective-permute-start.9 = (bf16[4,224,384]{2,1,0:T(8,128)(2,1)S(1)}, bf16[4,224,384]{2,1,0:T(8,128)(2,1)S(1)}, u32[]{:S(2)}, u32[]{:S(2)}) collective-permute-start(bf16[4,224,384]{2,1,0:T(8,128)(2,1)S(1)} %get-tuple-element.32), channel_id=1, source_target_pairs={{0,96},{32,0},{64,32},{96,64},{1,97},{33,1},{65,33},{97,65},{2,98}... | collective-permute-start | bytes 2064392 | tf_op jit(solution)/shard_map/ppermute | solution.py:24
  51.6 63.3 %collective-permute-start.22 = (bf16[2048,512]{1,0:T(8,128)(2,1)}, bf16[2048,512]{1,0:T(8,128)(2,1)}, u32[]{:S(2)}, u32[]{:S(2)}) collective-permute-start(bf16[2048,512]{1,0:T(8,128)(2,1)} %a.1), channel_id=1, source_target_pairs={{0,1},{1,0},{2,3},{3,2},{4,5},{5,4},{6,7},{7,6},{8,9},{9,8},{10,11... | collective-permute-start | bytes 6291464 | tf_op jit(solution)/shard_map/ppermute | solution.py:24
  54.0 67.1 %collective-permute-start.24 = (bf16[2048,512]{1,0:T(8,128)(2,1)}, bf16[2048,512]{1,0:T(8,128)(2,1)}, u32[]{:S(2)}, u32[]{:S(2)}) collective-permute-start(bf16[2048,512]{1,0:T(8,128)(2,1)} %collective-permute-done.23.w3), channel_id=1, source_target_pairs={{0,1},{1,0},{2,3},{3,2},{4,5},{5,4},{6,7},{7,6},{8,9},{9,8},{10,11... | collective-permute-start | bytes 6291464 | tf_op jit(solution)/shard_map/ppermute | solution.py:24
  54.6 15.7 %collective-permute-start.5 = (bf16[384,512]{1,0:T(8,128)(2,1)S(1)}, bf16[384,512]{1,0:T(8,128)(2,1)}, u32[]{:S(2)}, u32[]{:S(2)}) collective-permute-start(bf16[384,512]{1,0:T(8,128)(2,1)S(1)} %join.1.c0), channel_id=1, source_target_pairs={{0,64},{1,17},{2,66},{3,19},{4,68},{5,21},{6,70},{7,23},{8,72},{9,... | collective-permute-start | bytes 1179656 | tf_op jit(solution)/shard_map/ppermute | solution.py:36
  57.7 12.6 %collective-permute-start.6 = (bf16[384,512]{1,0:T(8,128)(2,1)S(1)}, bf16[384,512]{1,0:T(8,128)(2,1)}, u32[]{:S(2)}, u32[]{:S(2)}) collective-permute-start(bf16[384,512]{1,0:T(8,128)(2,1)S(1)} %join.1.c0), channel_id=1, source_target_pairs={{0,32},{1,9},{2,34},{3,11},{4,36},{5,13},{6,38},{7,15},{8,40},{9,1... | collective-permute-start | bytes 1179656 | tf_op jit(solution)/shard_map/ppermute | solution.py:36
  67.9 10.7 %collective-permute-start.7 = (bf16[384,512]{1,0:T(8,128)(2,1)S(1)}, bf16[384,512]{1,0:T(8,128)(2,1)}, u32[]{:S(2)}, u32[]{:S(2)}) collective-permute-start(bf16[384,512]{1,0:T(8,128)(2,1)S(1)} %join.1.c0), channel_id=1, source_target_pairs={{0,96},{1,25},{2,98},{3,27},{4,100},{5,29},{6,102},{7,31},{8,104},... | collective-permute-start | bytes 1179656 | tf_op jit(solution)/shard_map/ppermute | solution.py:36
  70.3 14.9 %collective-permute-start.15 = (bf16[384,512]{1,0:T(8,128)(2,1)}, bf16[384,512]{1,0:T(8,128)(2,1)}, u32[]{:S(2)}, u32[]{:S(2)}) collective-permute-start(bf16[384,512]{1,0:T(8,128)(2,1)} %collective-permute-done.5.c2), channel_id=1, source_target_pairs={{0,1},{1,0},{2,3},{3,2},{4,5},{5,4},{6,7},{7,6},{8,9},{9,8},{10,11... | collective-permute-start | bytes 1179656 | tf_op jit(solution)/shard_map/ppermute | solution.py:24
  70.3 15.9 %collective-permute-start.16 = (bf16[384,512]{1,0:T(8,128)(2,1)}, bf16[384,512]{1,0:T(8,128)(2,1)S(1)}, u32[]{:S(2)}, u32[]{:S(2)}) collective-permute-start(bf16[384,512]{1,0:T(8,128)(2,1)} %collective-permute-done.6.c1), channel_id=1, source_target_pairs={{0,1},{1,0},{2,3},{3,2},{4,5},{5,4},{6,7},{7,6},{8,9},{9,8},{10,11... | collective-permute-start | bytes 1179656 | tf_op jit(solution)/shard_map/ppermute | solution.py:24
  78.6 9.0 %collective-permute-start.17 = (bf16[384,512]{1,0:T(8,128)(2,1)}, bf16[384,512]{1,0:T(8,128)(2,1)}, u32[]{:S(2)}, u32[]{:S(2)}) collective-permute-start(bf16[384,512]{1,0:T(8,128)(2,1)} %collective-permute-done.7.c3), channel_id=1, source_target_pairs={{0,1},{1,0},{2,3},{3,2},{4,5},{5,4},{6,7},{7,6},{8,9},{9,8},{10,11... | collective-permute-start | bytes 1179656 | tf_op jit(solution)/shard_map/ppermute | solution.py:24
  85.2 12.3 %collective-permute-start.12 = (bf16[224,512]{1,0:T(8,128)(2,1)S(1)}, bf16[224,512]{1,0:T(8,128)(2,1)S(1)}, u32[]{:S(2)}, u32[]{:S(2)}) collective-permute-start(bf16[224,512]{1,0:T(8,128)(2,1)S(1)} %get-tuple-element.36), channel_id=1, source_target_pairs={{0,8},{1,33},{2,10},{3,35},{4,12},{5,37},{6,14},{7,39},{8,16},{9,4... | collective-permute-start | bytes 688136 | tf_op jit(solution)/shard_map/ppermute | solution.py:36
  86.2 13.9 %collective-permute-start.13 = (bf16[224,512]{1,0:T(8,128)(2,1)S(1)}, bf16[224,512]{1,0:T(8,128)(2,1)S(1)}, u32[]{:S(2)}, u32[]{:S(2)}) collective-permute-start(bf16[224,512]{1,0:T(8,128)(2,1)S(1)} %get-tuple-element.37), channel_id=1, source_target_pairs={{0,16},{1,65},{2,18},{3,67},{4,20},{5,69},{6,22},{7,71},{8,24},{9,... | collective-permute-start | bytes 688136 | tf_op jit(solution)/shard_map/ppermute | solution.py:36
  87.6 13.4 %collective-permute-start.14 = (bf16[224,512]{1,0:T(8,128)(2,1)S(1)}, bf16[224,512]{1,0:T(8,128)(2,1)S(1)}, u32[]{:S(2)}, u32[]{:S(2)}) collective-permute-start(bf16[224,512]{1,0:T(8,128)(2,1)S(1)} %get-tuple-element.38), channel_id=1, source_target_pairs={{0,24},{1,97},{2,26},{3,99},{4,28},{5,101},{6,30},{7,103},{8,0},{9... | collective-permute-start | bytes 688136 | tf_op jit(solution)/shard_map/ppermute | solution.py:36
  98.1 7.4 %collective-permute-start.18 = (bf16[224,512]{1,0:T(8,128)(2,1)}, bf16[224,512]{1,0:T(8,128)(2,1)S(1)}, u32[]{:S(2)}, u32[]{:S(2)}) collective-permute-start(bf16[224,512]{1,0:T(8,128)(2,1)} %get-tuple-element.40), channel_id=1, source_target_pairs={{0,32},{1,9},{2,34},{3,11},{4,36},{5,13},{6,38},{7,15},{8,40},{9,1... | collective-permute-start | bytes 688136 | tf_op jit(solution)/shard_map/ppermute | solution.py:36
  100.8 7.7 %collective-permute-start.19 = (bf16[224,512]{1,0:T(8,128)(2,1)}, bf16[224,512]{1,0:T(8,128)(2,1)S(1)}, u32[]{:S(2)}, u32[]{:S(2)}) collective-permute-start(bf16[224,512]{1,0:T(8,128)(2,1)} %get-tuple-element.41), channel_id=1, source_target_pairs={{0,64},{1,17},{2,66},{3,19},{4,68},{5,21},{6,70},{7,23},{8,72},{9,... | collective-permute-start | bytes 688136 | tf_op jit(solution)/shard_map/ppermute | solution.py:36
  101.7 7.8 %collective-permute-start.20 = (bf16[224,512]{1,0:T(8,128)(2,1)}, bf16[224,512]{1,0:T(8,128)(2,1)S(1)}, u32[]{:S(2)}, u32[]{:S(2)}) collective-permute-start(bf16[224,512]{1,0:T(8,128)(2,1)} %get-tuple-element.42), channel_id=1, source_target_pairs={{0,96},{1,25},{2,98},{3,27},{4,100},{5,29},{6,102},{7,31},{8,104},... | collective-permute-start | bytes 688136 | tf_op jit(solution)/shard_map/ppermute | solution.py:36
  (17 other events, 160.7 us)

commit v9 on v8

--- a/solution.py
+++ b/solution.py
@@ -147,7 +147,12 @@
     return pltpu.make_async_copy(piece_x, dst, sem)
 
 
-def early_kernel(s_ref, x0, x2, z0, z2, c0, c2, out, lhs, rhs, sem):
+def early_kernel(s_ref, x0, x2, z0, z2, c0, c2, *rest):
+    n_more = (len(rest) - 5) // 2
+    more, (out, *kept), (lhs, rhs, sem, more_sem) = rest[:n_more], rest[n_more:-4], rest[-4:]
+    copies = [pltpu.make_async_copy(a, b, more_sem.at[k]) for k, (a, b) in enumerate(zip(more, kept))]
+    for copy in copies:
+        copy.start()
     loads = [
         [
             load(s_ref[0], a.at[j], b.at[j], lhs.at[j, :, pl.ds(n * 384, 384)], sem.at[j, n])
@@ -161,46 +166,63 @@
         for copy in loads[j]:
             copy.wait()
         out[j] = jnp.dot(lhs[j], rhs[...], preferred_element_type=F32)
-
-
-def early_sums(use_x, pieces, coords):
+    for copy in copies:
+        copy.wait()
+
+
+def early_sums(use_x, pieces, coords, more):
     t = pieces[0].shape[-1]
     args = [pltpu.with_memory_space_constraint(a, pltpu.HBM) for a in pieces]
     args += [pltpu.with_memory_space_constraint(a, pltpu.VMEM) for a in coords]
+    args += [pltpu.with_memory_space_constraint(a, pltpu.HBM) for a in more]
     return pl.pallas_call(
         early_kernel,
-        in_specs=[SMEM] + [HBM] * 4 + [VMEM] * 2,
-        out_specs=VMEM,
-        out_shape=pltpu.VMEM((4, 224, 512), F32),
+        in_specs=[SMEM] + [HBM] * 4 + [VMEM] * 2 + [HBM] * len(more),
+        out_specs=[VMEM] * (1 + len(more)),
+        out_shape=[pltpu.VMEM((4, 224, 512), F32)] + [pltpu.VMEM(a.shape, a.dtype) for a in more],
         scratch_shapes=[
             pltpu.VMEM((4, 224, 2 * t), BF16),
             pltpu.VMEM((2 * t, 512), BF16),
             pltpu.SemaphoreType.DMA((4, 2)),
+            pltpu.SemaphoreType.DMA((2,)),
         ],
         compiler_params=params(8),
     )(use_x.reshape(1), *args)
 
 
-def late_kernel(s_ref, acc, c1, c3, x1, x3, z1, z3, o0, o1, o2, o3):
-    for use, ones, threes in ((1, x1, x3), (0, z1, z3)):
+def late_kernel(s_ref, acc_m, acc_t, c1m, c3m, c1t, c3t, x1, x3, z1, z3, *rest):
+    outs_m, outs_t, (own, sem) = rest[:4], rest[4:8], rest[8:]
+    sides = ((acc_m, c1m, c3m, outs_m), (acc_t, c1t, c3t, outs_t))
+    writes = [pltpu.make_async_copy(own.at[n], side[3][0], sem.at[n]) for n, side in enumerate(sides)]
+    for use, pieces in ((1, ((x1, x3), (z1, z3))), (0, ((z1, z3), (x1, x3)))):
 
         @pl.when(s_ref[0] == use)
         def _():
-            for j, out in enumerate((o0, o1, o2, o3)):
-                part = acc[j] + jnp.dot(ones[j], c1[...], preferred_element_type=F32)
-                part += jnp.dot(threes[j], c3[...], preferred_element_type=F32)
-                out[...] = part.astype(out.dtype)
-
-
-def late_sums(use_x, acc, coords, pieces):
-    args = [pltpu.with_memory_space_constraint(a, pltpu.VMEM) for a in (acc, *coords, *pieces)]
+            for n, ((acc, c1, c3, outs), (ones, threes)) in enumerate(zip(sides, pieces)):
+                for j, out in enumerate((own.at[n], *outs[1:])):
+                    part = acc[j] + jnp.dot(ones[j], c1[...], preferred_element_type=F32)
+                    part += jnp.dot(threes[j], c3[...], preferred_element_type=F32)
+                    out[...] = part.astype(out.dtype)
+                    if j == 0:
+                        writes[n].start()
+
+    for write in writes:
+        write.wait()
+
+
+def late_sums(mine_x, accs, coords, pieces):
+    args = [pltpu.with_memory_space_constraint(a, pltpu.VMEM) for a in (*accs, *coords, *pieces)]
+    out_specs = [pl.BlockSpec(memory_space=pltpu.HBM)] + [VMEM] * 3
+    out_shape = [pltpu.HBM((224, 512), F32)] + [pltpu.VMEM((224, 512), BF16)] * 3
     return pl.pallas_call(
         late_kernel,
-        in_specs=[SMEM] + [VMEM] * 7,
-        out_specs=[VMEM] * 4,
-        out_shape=[pltpu.VMEM((224, 512), F32)] + [pltpu.VMEM((224, 512), BF16)] * 3,
+        in_specs=[SMEM] + [VMEM] * 10,
+        out_specs=out_specs * 2,
+        out_shape=out_shape * 2,
+        scratch_shapes=[pltpu.VMEM((2, 224, 512), F32), pltpu.SemaphoreType.DMA((2,))],
         compiler_params=params(6),
-    )(use_x.reshape(1), *args)
+        name="late",
+    )(mine_x.reshape(1), *args)
 
 
 def combine_kernel(s_ref, m0, m1, m2, m3, t0, t1, t2, t3, keep, give):
@@ -313,11 +335,13 @@
 
     first = [got[k] for got in (got_x, got_z) for k in (0, 2)]
     then = [got[k] for got in (got_x, got_z) for k in (1, 3)]
-    sums = []
-    for use_x, coords, axis in ((1 - c, along, "z"), (c, beyond, "x")):
-        acc = early_sums(use_x, first, (own, coords[2]))
-        part = late_sums(use_x, acc, (coords[1], coords[3]), then)
-        sums.append([part[0]] + [cross(part[k], axis, k) for k in (1, 2, 3)])
+    acc_m = early_sums(1 - c, first, (own, along[2]), ())[0]
+    acc_t, *moved = early_sums(c, first, (own, beyond[2]), (along[1], along[3]))
+    part = late_sums(1 - c, (acc_m, acc_t), (*moved, beyond[1], beyond[3]), then)
+    sums = [
+        [own_part] + [cross(sent[k - 1], axis, k) for k in (1, 2, 3)]
+        for own_part, sent, axis in ((part[0], part[1:4], "z"), (part[4], part[5:], "x"))
+    ]
     keep, give = combine(1 - jnp.bitwise_xor(c, yl), *sums)
     got = shift(give, "yl", 1)
     held = hold((projector, beside_w))

time: 128 us -> 129 us (level)
  the two profiles are of different devices: /device:TPU:0 before, /device:TPU:2 now
where the time goes in v9:
time: 129 us; the launch traced here: 128 us
  waiting for transfers between devices  58.7 us (46%)
  starting transfers between devices  32.6 us (25%)
  Pallas kernels  29.5 us (23%)
  local copies, waits for them, and re-layouts  6.35 us (5%)
    ppermute x15, waiting for transfers between devices, shift(): return lax.ppermute(a, axis, [(i, (i + k) % n) for i in range(n)])  23.4 us
    ppermute x9, waiting for transfers between devices, cross(): return lax.ppermute(a, AXES, pairs)  18.1 us
    ppermute x1, waiting for transfers between devices, step(): lax.ppermute(projector, ('yl', 'yh'), [(0, 3), (3, 0), (1, 2), (2, 1)])  17.1 us
    ppermute x9, starting transfers between devices, cross(): return lax.ppermute(a, AXES, pairs)  15.1 us
    ppermute x15, starting transfers between devices, shift(): return lax.ppermute(a, axis, [(i, (i + k) % n) for i in range(n)])  14.4 us
    pallas_call x1, Pallas kernels, front(): pl.pallas_call(front_kernel, grid_spec=pltpu.PrefetchScalarGridSpec(num_s...  9.8 us
    unnamed x32, local copies, waits for them, and re-layouts  6.35 us
    pallas_call x1, Pallas kernels, last_stage(): pl.pallas_call(last_kernel, in_specs=[SMEM] + [VMEM] * 7 + [HBM], out_spe...  6.24 us
  transfers between devices with their start and end apart: 25, of which 12 were waited for; matrix products, arithmetic and copies ran while one was open for 0% of the time, Pallas kernels for 18%

profile of v9, /device:TPU:2, one launch (start us, length us, event | category | flops | bytes accessed | tf_op | source)
XLA Modules:
  0.0 128.2 jit_solution(537390653277364858)
XLA Ops:
  0.6 3.1 %collective-permute-start.23 = (bf16[2048,512]{1,0:T(8,128)(2,1)}, bf16[2048,512]{1,0:T(8,128)(2,1)}, u32[]{:S(2)}, u32[]{:S(2)}) collective-permute-start(bf16[2048,512]{1,0:T(8,128)(2,1)} %a.1), channel_id=1, source_target_pairs={{0,6},{6,0},{2,4},{4,2},{1,7},{7,1},{3,5},{5,3},{8,14},{14,8},{10,... | collective-permute-start | bytes 6291464 | tf_op jit(solution)/shard_map/ppermute | solution.py:332
  3.8 9.8 %front.1 = (f32[384,256]{1,0:T(8,128)S(1)}, f32[384,256]{1,0:T(8,128)S(1)}, bf16[4,224,384]{2,1,0:T(8,128)(2,1)S(1)}, bf16[4,224,384]{2,1,0:T(8,128)(2,1)S(1)}, ...) custom-call(s32[4]{0:T(128)S(1)} %pad_add_fusion.s_ref, ...), custom_call_target="tpu_custom_call" | custom-call | tf_op jit(solution)/shard_map/front/pallas_call | solution.py:77
  13.6 2.2 %collective-permute-start = (bf16[4,224,384]{2,1,0:T(8,128)(2,1)S(1)}, bf16[4,224,384]{2,1,0:T(8,128)(2,1)S(1)}, u32[]{:S(2)}, u32[]{:S(2)}) collective-permute-start(bf16[4,224,384]{2,1,0:T(8,128)(2,1)S(1)} %get-tuple-element.29), channel_id=1, source_target_pairs={{0,64},{32,96},{64,0},{96,32},{1,65},{33,97},{65,1},{97,33},{2,66}... | collective-permute-start | bytes 2064392 | tf_op jit(solution)/shard_map/ppermute | solution.py:24
  15.8 3.9 %collective-permute-start.1 = (bf16[4,224,384]{2,1,0:T(8,128)(2,1)S(1)}, bf16[4,224,384]{2,1,0:T(8,128)(2,1)S(1)}, u32[]{:S(2)}, u32[]{:S(2)}) collective-permute-start(bf16[4,224,384]{2,1,0:T(8,128)(2,1)S(1)} %get-tuple-element.31), channel_id=1, source_target_pairs={{0,16},{8,24},{16,0},{24,8},{1,17},{9,25},{17,1},{25,9},{2,18},{10... | collective-permute-start | bytes 2064392 | tf_op jit(solution)/shard_map/ppermute | solution.py:24
  20.5 7.6 %collective-permute-done.3 = bf16[384,256]{1,0:T(8,128)(2,1)S(1)} collective-permute-done((bf16[384,256]{1,0:T(8,128)(2,1)S(1)}, bf16[384,256]{1,0:T(8,128)(2,1)S(1)}, u32[]{:S(2)}, u32[]{:S(2)}) %collective-permute-start.3) | collective-permute-done | bytes 196640 | tf_op jit(solution)/shard_map/ppermute | solution.py:24
  29.6 3.9 %collective-permute-done.x2 = bf16[4,224,384]{2,1,0:T(8,128)(2,1)S(1)} collective-permute-done((bf16[4,224,384]{2,1,0:T(8,128)(2,1)S(1)}, bf16[4,224,384]{2,1,0:T(8,128)(2,1)S(1)}, u32[]{:S(2)}, u32[]{:S(2)}) %collective-permute-start) | collective-permute-done | bytes 688160 | tf_op jit(solution)/shard_map/ppermute | solution.py:24
  33.6 1.9 %collective-permute-done.1.z2 = bf16[4,224,384]{2,1,0:T(8,128)(2,1)S(1)} collective-permute-done((bf16[4,224,384]{2,1,0:T(8,128)(2,1)S(1)}, bf16[4,224,384]{2,1,0:T(8,128)(2,1)S(1)}, u32[]{:S(2)}, u32[]{:S(2)}) %collective-permute-start.1) | collective-permute-done | bytes 688160 | tf_op jit(solution)/shard_map/ppermute | solution.py:24
  36.7 17.1 %collective-permute-done.23.w3 = bf16[2048,512]{1,0:T(8,128)(2,1)} collective-permute-done((bf16[2048,512]{1,0:T(8,128)(2,1)}, bf16[2048,512]{1,0:T(8,128)(2,1)}, u32[]{:S(2)}, u32[]{:S(2)}) %collective-permute-start.23) | collective-permute-done | bytes 2097184 | tf_op jit(solution)/shard_map/ppermute | solution.py:332
  54.5 2.2 %collective-permute-start.5 = (bf16[384,512]{1,0:T(8,128)(2,1)S(1)}, bf16[384,512]{1,0:T(8,128)(2,1)S(1)}, u32[]{:S(2)}, u32[]{:S(2)}) collective-permute-start(bf16[384,512]{1,0:T(8,128)(2,1)S(1)} %join.1.c0), channel_id=1, source_target_pairs={{0,64},{1,17},{2,66},{3,19},{4,68},{5,21},{6,70},{7,23},{8,72},{9,... | collective-permute-start | bytes 1179656 | tf_op jit(solution)/shard_map/ppermute | solution.py:36
  58.5 2.0 %collective-permute-start.8 = (bf16[384,512]{1,0:T(8,128)(2,1)S(1)}, bf16[384,512]{1,0:T(8,128)(2,1)}, u32[]{:S(2)}, u32[]{:S(2)}) collective-permute-start(bf16[384,512]{1,0:T(8,128)(2,1)S(1)} %join.1.c0), channel_id=1, source_target_pairs={{0,96},{1,25},{2,98},{3,27},{4,100},{5,29},{6,102},{7,31},{8,104},... | collective-permute-start | bytes 1179656 | tf_op jit(solution)/shard_map/ppermute | solution.py:36
  60.5 3.4 %collective-permute-done.5.c2 = bf16[384,512]{1,0:T(8,128)(2,1)S(1)} collective-permute-done((bf16[384,512]{1,0:T(8,128)(2,1)S(1)}, bf16[384,512]{1,0:T(8,128)(2,1)S(1)}, u32[]{:S(2)}, u32[]{:S(2)}) %collective-permute-start.5) | collective-permute-done | bytes 393248 | tf_op jit(solution)/shard_map/ppermute | solution.py:36
  64.7 3.5 %collective-permute-done.7.rest_0_ = bf16[384,512]{1,0:T(8,128)(2,1)} collective-permute-done((bf16[384,512]{1,0:T(8,128)(2,1)S(1)}, bf16[384,512]{1,0:T(8,128)(2,1)}, u32[]{:S(2)}, u32[]{:S(2)}) %collective-permute-start.7) | collective-permute-done | bytes 393248 | tf_op jit(solution)/shard_map/ppermute | solution.py:36
  68.2 4.0 %collective-permute-start.14 = (bf16[4,224,384]{2,1,0:T(8,128)(2,1)}, bf16[4,224,384]{2,1,0:T(8,128)(2,1)}, u32[]{:S(2)}, u32[]{:S(2)}) collective-permute-start(bf16[4,224,384]{2,1,0:T(8,128)(2,1)} %get-tuple-element.40), channel_id=1, source_target_pairs={{0,24},{8,0},{16,8},{24,16},{1,25},{9,1},{17,9},{25,17},{2,26},{10... | collective-permute-start | bytes 2064392 | tf_op jit(solution)/shard_map/ppermute | solution.py:24
  74.6 2.5 %shard_map.85.acc_m = f32[4,224,512]{2,1,0:T(8,128)S(1)} custom-call(s32[1]{0:T(128)} %bitcast.5.s_ref, bf16[4,224,384]{2,1,0:T(8,128)(2,1)} %copy-done, bf16[4,224,384]{2,1,0:T(8,128)(2,1)} %copy-done.14, bf16[4,224,384]{2,1,0:T(8,128)(2,1)} %copy-done.1, bf16[4,224,384]{2,1,0:T(8,128)(2,1)} %copy-done.15, bf16[384,512]{1,0:T(8,128)(2,1)S(1)} %join.1.c0, ...), custom_call_target="tpu_custom_call" | custom-call | tf_op jit(solution)/shard_map/pallas_call | solution.py:178
  77.1 2.6 %shard_map.86 = (f32[4,224,512]{2,1,0:T(8,128)S(1)}, bf16[384,512]{1,0:T(8,128)(2,1)S(1)}, bf16[384,512]{1,0:T(8,128)(2,1)S(1)}) custom-call(s32[1]{0:T(128)} %bitcast.2.s_ref, bf16[4,224,384]{2,1,0:T(8,128)(2,1)} %copy-done, bf16[4,224,384]{2,1,0:T(8,128)(2,1)} %copy-done.14, bf16[4,224,384]{2,1,0:T(8,128)(2,1)} %copy-done.1, ...), custom_call_target="tpu_custom_call" | custom-call | tf_op jit(solution)/shard_map/pallas_call | solution.py:178
  79.7 6.4 %collective-permute-done.14.z3 = bf16[4,224,384]{2,1,0:T(8,128)(2,1)} collective-permute-done((bf16[4,224,384]{2,1,0:T(8,128)(2,1)}, bf16[4,224,384]{2,1,0:T(8,128)(2,1)}, u32[]{:S(2)}, u32[]{:S(2)}) %collective-permute-start.14) | collective-permute-done | bytes 688160 | tf_op jit(solution)/shard_map/ppermute | solution.py:24
  86.2 4.4 %late.1 = (f32[224,512]{1,0:T(8,128)}, bf16[224,512]{1,0:T(8,128)(2,1)S(1)}, bf16[224,512]{1,0:T(8,128)(2,1)S(1)}, bf16[224,512]{1,0:T(8,128)(2,1)S(1)}, f32[224...) custom-call(s32[1]{0:T(128)} %bitcast.5.s_ref, ...), custom_call_target="tpu_custom_call" | custom-call | tf_op jit(solution)/shard_map/late/pallas_call | solution.py:217
  94.1 2.4 %collective-permute-start.17 = (bf16[224,512]{1,0:T(8,128)(2,1)S(1)}, bf16[224,512]{1,0:T(8,128)(2,1)S(1)}, u32[]{:S(2)}, u32[]{:S(2)}) collective-permute-start(bf16[224,512]{1,0:T(8,128)(2,1)S(1)} %get-tuple-element.44), channel_id=1, source_target_pairs={{0,24},{1,97},{2,26},{3,99},{4,28},{5,101},{6,30},{7,103},{8,0},{9... | collective-permute-start | bytes 688136 | tf_op jit(solution)/shard_map/ppermute | solution.py:36
  99.3 2.9 %collective-permute-done.16.m2 = bf16[224,512]{1,0:T(8,128)(2,1)S(1)} collective-permute-done((bf16[224,512]{1,0:T(8,128)(2,1)S(1)}, bf16[224,512]{1,0:T(8,128)(2,1)S(1)}, u32[]{:S(2)}, u32[]{:S(2)}) %collective-permute-start.16) | collective-permute-done | bytes 229408 | tf_op jit(solution)/shard_map/ppermute | solution.py:36
  105.7 4.4 %collective-permute-done.19.t2 = bf16[224,512]{1,0:T(8,128)(2,1)S(1)} collective-permute-done((bf16[224,512]{1,0:T(8,128)(2,1)}, bf16[224,512]{1,0:T(8,128)(2,1)S(1)}, u32[]{:S(2)}, u32[]{:S(2)}) %collective-permute-start.19) | collective-permute-done | bytes 229408 | tf_op jit(solution)/shard_map/ppermute | solution.py:36
  110.0 2.5 %collective-permute-done.20.t3 = bf16[224,512]{1,0:T(8,128)(2,1)} collective-permute-done((bf16[224,512]{1,0:T(8,128)(2,1)}, bf16[224,512]{1,0:T(8,128)(2,1)}, u32[]{:S(2)}, u32[]{:S(2)}) %collective-permute-start.20) | collective-permute-done | bytes 229408 | tf_op jit(solution)/shard_map/ppermute | solution.py:36
  116.1 2.2 %keep.1 = (bf16[2048,512]{1,0:T(8,128)(2,1)S(1)}, bf16[2048,512]{1,0:T(8,128)(2,1)S(1)}) custom-call(bf16[2048,512]{1,0:T(8,128)(2,1)} %a.1, bf16[2048,512]{1,0:T(8,128)(2,1)} %collective-permute-done.22.b), custom_call_target="tpu_custom_call" | custom-call | tf_op jit(solution)/shard_map/keep/pallas_call | solution.py:129
  118.3 3.5 %collective-permute-done.21.got = bf16[224,512]{1,0:T(8,128)(2,1)S(1)} collective-permute-done((bf16[224,512]{1,0:T(8,128)(2,1)S(1)}, bf16[224,512]{1,0:T(8,128)(2,1)S(1)}, u32[]{:S(2)}, u32[]{:S(2)}) %collective-permute-start.21) | collective-permute-done | bytes 229408 | tf_op jit(solution)/shard_map/ppermute | solution.py:24
  121.8 6.2 %last.1 = (f32[224,512]{1,0:T(8,128)}, f32[224,512]{1,0:T(8,128)}, bf16[224,8192]{1,0:T(8,128)(2,1)}) custom-call(s32[4]{0:T(128)S(1)} %pad_add_fusion.s_ref, f32[224,512]{1,0:T(8,128)S(1)} %get-tuple-element.49.mine, bf16[224,512]{1,0:T(8,128)(2,1)S(1)} %collective-permute-done.21.got, f32[224,512]{1,0:T(8,128)S(1)} %copy-done.8, f32[224,512]{1,0:T(8,128)S(1)} %copy-done.9, ...), custom_call_target="tpu_custom_call" | custom-call | tf_op jit(solution)/shard_map/last/pallas_call | solution.py:299
  (69 shorter events, 22.5 us)
Async XLA Ops:
  0.6 53.3 %collective-permute-start.23 = (bf16[2048,512]{1,0:T(8,128)(2,1)}, bf16[2048,512]{1,0:T(8,128)(2,1)}, u32[]{:S(2)}, u32[]{:S(2)}) collective-permute-start(bf16[2048,512]{1,0:T(8,128)(2,1)} %a.1), channel_id=1, source_target_pairs={{0,6},{6,0},{2,4},{4,2},{1,7},{7,1},{3,5},{5,3},{8,14},{14,8},{10,... | collective-permute-start | bytes 6291464 | tf_op jit(solution)/shard_map/ppermute | solution.py:332
  13.6 6.1 %collective-permute-start.2 = (f32[384,256]{1,0:T(8,128)S(1)}, f32[384,256]{1,0:T(8,128)S(1)}, u32[]{:S(2)}, u32[]{:S(2)}) collective-permute-start(f32[384,256]{1,0:T(8,128)S(1)} %get-tuple-element.33), channel_id=1, source_target_pairs={{0,1},{1,0},{2,3},{3,2},{4,5},{5,4},{6,7},{7,6},{8,9},{9,8},{10,11... | collective-permute-start | bytes 1179656 | tf_op jit(solution)/shard_map/ppermute | solution.py:24
  13.6 19.9 %collective-permute-start = (bf16[4,224,384]{2,1,0:T(8,128)(2,1)S(1)}, bf16[4,224,384]{2,1,0:T(8,128)(2,1)S(1)}, u32[]{:S(2)}, u32[]{:S(2)}) collective-permute-start(bf16[4,224,384]{2,1,0:T(8,128)(2,1)S(1)} %get-tuple-element.29), channel_id=1, source_target_pairs={{0,64},{32,96},{64,0},{96,32},{1,65},{33,97},{65,1},{97,33},{2,66}... | collective-permute-start | bytes 2064392 | tf_op jit(solution)/shard_map/ppermute | solution.py:24
  15.8 19.6 %collective-permute-start.1 = (bf16[4,224,384]{2,1,0:T(8,128)(2,1)S(1)}, bf16[4,224,384]{2,1,0:T(8,128)(2,1)S(1)}, u32[]{:S(2)}, u32[]{:S(2)}) collective-permute-start(bf16[4,224,384]{2,1,0:T(8,128)(2,1)S(1)} %get-tuple-element.31), channel_id=1, source_target_pairs={{0,16},{8,24},{16,0},{24,8},{1,17},{9,25},{17,1},{25,9},{2,18},{10... | collective-permute-start | bytes 2064392 | tf_op jit(solution)/shard_map/ppermute | solution.py:24
  19.8 8.4 %collective-permute-start.3 = (bf16[384,256]{1,0:T(8,128)(2,1)S(1)}, bf16[384,256]{1,0:T(8,128)(2,1)S(1)}, u32[]{:S(2)}, u32[]{:S(2)}) collective-permute-start(bf16[384,256]{1,0:T(8,128)(2,1)S(1)} %get-tuple-element.53), channel_id=1, source_target_pairs={{0,2},{2,0},{1,3},{3,1},{4,6},{6,4},{5,7},{7,5},{8,10},{10,8},{9,1... | collective-permute-start | bytes 589832 | tf_op jit(solution)/shard_map/ppermute | solution.py:24
  20.5 34.0 %collective-permute-start.11 = (bf16[4,224,384]{2,1,0:T(8,128)(2,1)S(1)}, bf16[4,224,384]{2,1,0:T(8,128)(2,1)S(1)}, u32[]{:S(2)}, u32[]{:S(2)}) collective-permute-start(bf16[4,224,384]{2,1,0:T(8,128)(2,1)S(1)} %get-tuple-element.37), channel_id=1, source_target_pairs={{0,32},{32,64},{64,96},{96,0},{1,33},{33,65},{65,97},{97,1},{2,34}... | collective-permute-start | bytes 2064392 | tf_op jit(solution)/shard_map/ppermute | solution.py:24
  28.1 28.6 %collective-permute-start.12 = (bf16[4,224,384]{2,1,0:T(8,128)(2,1)S(1)}, bf16[4,224,384]{2,1,0:T(8,128)(2,1)S(1)}, u32[]{:S(2)}, u32[]{:S(2)}) collective-permute-start(bf16[4,224,384]{2,1,0:T(8,128)(2,1)S(1)} %get-tuple-element.38), channel_id=1, source_target_pairs={{0,96},{32,0},{64,32},{96,64},{1,97},{33,1},{65,33},{97,65},{2,98}... | collective-permute-start | bytes 2064392 | tf_op jit(solution)/shard_map/ppermute | solution.py:24
  35.4 22.1 %collective-permute-start.13 = (bf16[4,224,384]{2,1,0:T(8,128)(2,1)S(1)}, bf16[4,224,384]{2,1,0:T(8,128)(2,1)S(1)}, u32[]{:S(2)}, u32[]{:S(2)}) collective-permute-start(bf16[4,224,384]{2,1,0:T(8,128)(2,1)S(1)} %get-tuple-element.39), channel_id=1, source_target_pairs={{0,8},{8,16},{16,24},{24,0},{1,9},{9,17},{17,25},{25,1},{2,10},{10... | collective-permute-start | bytes 2064392 | tf_op jit(solution)/shard_map/ppermute | solution.py:24
  36.7 79.4 %collective-permute-start.22 = (bf16[2048,512]{1,0:T(8,128)(2,1)}, bf16[2048,512]{1,0:T(8,128)(2,1)}, u32[]{:S(2)}, u32[]{:S(2)}) collective-permute-start(bf16[2048,512]{1,0:T(8,128)(2,1)} %a.1), channel_id=1, source_target_pairs={{0,1},{1,0},{2,3},{3,2},{4,5},{5,4},{6,7},{7,6},{8,9},{9,8},{10,11... | collective-permute-start | bytes 6291464 | tf_op jit(solution)/shard_map/ppermute | solution.py:24
  53.9 68.0 %collective-permute-start.24 = (bf16[2048,512]{1,0:T(8,128)(2,1)}, bf16[2048,512]{1,0:T(8,128)(2,1)S(1)}, u32[]{:S(2)}, u32[]{:S(2)}) collective-permute-start(bf16[2048,512]{1,0:T(8,128)(2,1)} %collective-permute-done.23.w3), channel_id=1, source_target_pairs={{0,1},{1,0},{2,3},{3,2},{4,5},{5,4},{6,7},{7,6},{8,9},{9,8},{10,11... | collective-permute-start | bytes 6291464 | tf_op jit(solution)/shard_map/ppermute | solution.py:24
  54.5 9.5 %collective-permute-start.5 = (bf16[384,512]{1,0:T(8,128)(2,1)S(1)}, bf16[384,512]{1,0:T(8,128)(2,1)S(1)}, u32[]{:S(2)}, u32[]{:S(2)}) collective-permute-start(bf16[384,512]{1,0:T(8,128)(2,1)S(1)} %join.1.c0), channel_id=1, source_target_pairs={{0,64},{1,17},{2,66},{3,19},{4,68},{5,21},{6,70},{7,23},{8,72},{9,... | collective-permute-start | bytes 1179656 | tf_op jit(solution)/shard_map/ppermute | solution.py:36
  57.6 10.7 %collective-permute-start.7 = (bf16[384,512]{1,0:T(8,128)(2,1)S(1)}, bf16[384,512]{1,0:T(8,128)(2,1)}, u32[]{:S(2)}, u32[]{:S(2)}) collective-permute-start(bf16[384,512]{1,0:T(8,128)(2,1)S(1)} %join.1.c0), channel_id=1, source_target_pairs={{0,32},{1,9},{2,34},{3,11},{4,36},{5,13},{6,38},{7,15},{8,40},{9,1... | collective-permute-start | bytes 1179656 | tf_op jit(solution)/shard_map/ppermute | solution.py:36
  58.5 13.8 %collective-permute-start.8 = (bf16[384,512]{1,0:T(8,128)(2,1)S(1)}, bf16[384,512]{1,0:T(8,128)(2,1)}, u32[]{:S(2)}, u32[]{:S(2)}) collective-permute-start(bf16[384,512]{1,0:T(8,128)(2,1)S(1)} %join.1.c0), channel_id=1, source_target_pairs={{0,96},{1,25},{2,98},{3,27},{4,100},{5,29},{6,102},{7,31},{8,104},... | collective-permute-start | bytes 1179656 | tf_op jit(solution)/shard_map/ppermute | solution.py:36
  63.9 8.4 %collective-permute-start.6 = (bf16[384,512]{1,0:T(8,128)(2,1)S(1)}, bf16[384,512]{1,0:T(8,128)(2,1)S(1)}, u32[]{:S(2)}, u32[]{:S(2)}) collective-permute-start(bf16[384,512]{1,0:T(8,128)(2,1)S(1)} %collective-permute-done.5.c2), channel_id=1, source_target_pairs={{0,1},{1,0},{2,3},{3,2},{4,5},{5,4},{6,7},{7,6},{8,9},{9,8},{10,11... | collective-permute-start | bytes 1179656 | tf_op jit(solution)/shard_map/ppermute | solution.py:24
  68.2 17.9 %collective-permute-start.14 = (bf16[4,224,384]{2,1,0:T(8,128)(2,1)}, bf16[4,224,384]{2,1,0:T(8,128)(2,1)}, u32[]{:S(2)}, u32[]{:S(2)}) collective-permute-start(bf16[4,224,384]{2,1,0:T(8,128)(2,1)} %get-tuple-element.40), channel_id=1, source_target_pairs={{0,24},{8,0},{16,8},{24,16},{1,25},{9,1},{17,9},{25,17},{2,26},{10... | collective-permute-start | bytes 2064392 | tf_op jit(solution)/shard_map/ppermute | solution.py:24
  72.3 13.9 %collective-permute-start.10 = (bf16[384,512]{1,0:T(8,128)(2,1)}, bf16[384,512]{1,0:T(8,128)(2,1)}, u32[]{:S(2)}, u32[]{:S(2)}) collective-permute-start(bf16[384,512]{1,0:T(8,128)(2,1)} %collective-permute-done.8.rest_1_), channel_id=1, source_target_pairs={{0,1},{1,0},{2,3},{3,2},{4,5},{5,4},{6,7},{7,6},{8,9},{9,8},{10,11... | collective-permute-start | bytes 1179656 | tf_op jit(solution)/shard_map/ppermute | solution.py:24
  73.1 13.1 %collective-permute-start.9 = (bf16[384,512]{1,0:T(8,128)(2,1)}, bf16[384,512]{1,0:T(8,128)(2,1)}, u32[]{:S(2)}, u32[]{:S(2)}) collective-permute-start(bf16[384,512]{1,0:T(8,128)(2,1)} %collective-permute-done.7.rest_0_), channel_id=1, source_target_pairs={{0,1},{1,0},{2,3},{3,2},{4,5},{5,4},{6,7},{7,6},{8,9},{9,8},{10,11... | collective-permute-start | bytes 1179656 | tf_op jit(solution)/shard_map/ppermute | solution.py:24
  90.5 7.3 %collective-permute-start.15 = (bf16[224,512]{1,0:T(8,128)(2,1)S(1)}, bf16[224,512]{1,0:T(8,128)(2,1)S(1)}, u32[]{:S(2)}, u32[]{:S(2)}) collective-permute-start(bf16[224,512]{1,0:T(8,128)(2,1)S(1)} %get-tuple-element.42), channel_id=1, source_target_pairs={{0,8},{1,33},{2,10},{3,35},{4,12},{5,37},{6,14},{7,39},{8,16},{9,4... | collective-permute-start | bytes 688136 | tf_op jit(solution)/shard_map/ppermute | solution.py:36
  92.4 9.8 %collective-permute-start.16 = (bf16[224,512]{1,0:T(8,128)(2,1)S(1)}, bf16[224,512]{1,0:T(8,128)(2,1)S(1)}, u32[]{:S(2)}, u32[]{:S(2)}) collective-permute-start(bf16[224,512]{1,0:T(8,128)(2,1)S(1)} %get-tuple-element.43), channel_id=1, source_target_pairs={{0,16},{1,65},{2,18},{3,67},{4,20},{5,69},{6,22},{7,71},{8,24},{9,... | collective-permute-start | bytes 688136 | tf_op jit(solution)/shard_map/ppermute | solution.py:36
  94.1 9.8 %collective-permute-start.17 = (bf16[224,512]{1,0:T(8,128)(2,1)S(1)}, bf16[224,512]{1,0:T(8,128)(2,1)S(1)}, u32[]{:S(2)}, u32[]{:S(2)}) collective-permute-start(bf16[224,512]{1,0:T(8,128)(2,1)S(1)} %get-tuple-element.44), channel_id=1, source_target_pairs={{0,24},{1,97},{2,26},{3,99},{4,28},{5,101},{6,30},{7,103},{8,0},{9... | collective-permute-start | bytes 688136 | tf_op jit(solution)/shard_map/ppermute | solution.py:36
  97.8 7.8 %collective-permute-start.18 = (bf16[224,512]{1,0:T(8,128)(2,1)}, bf16[224,512]{1,0:T(8,128)(2,1)S(1)}, u32[]{:S(2)}, u32[]{:S(2)}) collective-permute-start(bf16[224,512]{1,0:T(8,128)(2,1)} %get-tuple-element.46), channel_id=1, source_target_pairs={{0,32},{1,9},{2,34},{3,11},{4,36},{5,13},{6,38},{7,15},{8,40},{9,1... | collective-permute-start | bytes 688136 | tf_op jit(solution)/shard_map/ppermute | solution.py:36
  102.2 7.8 %collective-permute-start.19 = (bf16[224,512]{1,0:T(8,128)(2,1)}, bf16[224,512]{1,0:T(8,128)(2,1)S(1)}, u32[]{:S(2)}, u32[]{:S(2)}) collective-permute-start(bf16[224,512]{1,0:T(8,128)(2,1)} %get-tuple-element.47), channel_id=1, source_target_pairs={{0,64},{1,17},{2,66},{3,19},{4,68},{5,21},{6,70},{7,23},{8,72},{9,... | collective-permute-start | bytes 688136 | tf_op jit(solution)/shard_map/ppermute | solution.py:36
  103.9 8.6 %collective-permute-start.20 = (bf16[224,512]{1,0:T(8,128)(2,1)}, bf16[224,512]{1,0:T(8,128)(2,1)}, u32[]{:S(2)}, u32[]{:S(2)}) collective-permute-start(bf16[224,512]{1,0:T(8,128)(2,1)} %get-tuple-element.48), channel_id=1, source_target_pairs={{0,96},{1,25},{2,98},{3,27},{4,100},{5,29},{6,102},{7,31},{8,104},... | collective-permute-start | bytes 688136 | tf_op jit(solution)/shard_map/ppermute | solution.py:36
  115.7 6.1 %collective-permute-start.21 = (bf16[224,512]{1,0:T(8,128)(2,1)S(1)}, bf16[224,512]{1,0:T(8,128)(2,1)S(1)}, u32[]{:S(2)}, u32[]{:S(2)}) collective-permute-start(bf16[224,512]{1,0:T(8,128)(2,1)S(1)} %get-tuple-element.50), channel_id=1, source_target_pairs={{0,4},{4,0},{1,5},{5,1},{2,6},{6,2},{3,7},{7,3},{8,12},{12,8},{9,1... | collective-permute-start | bytes 688136 | tf_op jit(solution)/shard_map/ppermute | solution.py:24
  (17 other events, 235.3 us)

commit v10 on v8

--- a/solution.py
+++ b/solution.py
@@ -147,7 +147,12 @@
     return pltpu.make_async_copy(piece_x, dst, sem)
 
 
-def early_kernel(s_ref, x0, x2, z0, z2, c0, c2, out, lhs, rhs, sem):
+def early_kernel(s_ref, x0, x2, z0, z2, c0, c2, *rest):
+    n_more = (len(rest) - 5) // 2
+    more, (out, *kept), (lhs, rhs, sem, more_sem) = rest[:n_more], rest[n_more:-4], rest[-4:]
+    copies = [pltpu.make_async_copy(a, b, more_sem.at[k]) for k, (a, b) in enumerate(zip(more, kept))]
+    for copy in copies:
+        copy.start()
     loads = [
         [
             load(s_ref[0], a.at[j], b.at[j], lhs.at[j, :, pl.ds(n * 384, 384)], sem.at[j, n])
@@ -161,35 +166,44 @@
         for copy in loads[j]:
             copy.wait()
         out[j] = jnp.dot(lhs[j], rhs[...], preferred_element_type=F32)
-
-
-def early_sums(use_x, pieces, coords):
+    for copy in copies:
+        copy.wait()
+
+
+def early_sums(use_x, pieces, coords, more):
     t = pieces[0].shape[-1]
     args = [pltpu.with_memory_space_constraint(a, pltpu.HBM) for a in pieces]
     args += [pltpu.with_memory_space_constraint(a, pltpu.VMEM) for a in coords]
+    args += [pltpu.with_memory_space_constraint(a, pltpu.HBM) for a in more]
     return pl.pallas_call(
         early_kernel,
-        in_specs=[SMEM] + [HBM] * 4 + [VMEM] * 2,
-        out_specs=VMEM,
-        out_shape=pltpu.VMEM((4, 224, 512), F32),
+        in_specs=[SMEM] + [HBM] * 4 + [VMEM] * 2 + [HBM] * len(more),
+        out_specs=[VMEM] * (1 + len(more)),
+        out_shape=[pltpu.VMEM((4, 224, 512), F32)] + [pltpu.VMEM(a.shape, a.dtype) for a in more],
         scratch_shapes=[
             pltpu.VMEM((4, 224, 2 * t), BF16),
             pltpu.VMEM((2 * t, 512), BF16),
             pltpu.SemaphoreType.DMA((4, 2)),
+            pltpu.SemaphoreType.DMA((2,)),
         ],
         compiler_params=params(8),
     )(use_x.reshape(1), *args)
 
 
-def late_kernel(s_ref, acc, c1, c3, x1, x3, z1, z3, o0, o1, o2, o3):
+def late_kernel(s_ref, acc, c1, c3, x1, x3, z1, z3, o0, o1, o2, o3, own, sem):
+    write = pltpu.make_async_copy(own, o0, sem)
     for use, ones, threes in ((1, x1, x3), (0, z1, z3)):
 
         @pl.when(s_ref[0] == use)
         def _():
-            for j, out in enumerate((o0, o1, o2, o3)):
+            for j, out in enumerate((own, o1, o2, o3)):
                 part = acc[j] + jnp.dot(ones[j], c1[...], preferred_element_type=F32)
                 part += jnp.dot(threes[j], c3[...], preferred_element_type=F32)
                 out[...] = part.astype(out.dtype)
+                if j == 0:
+                    write.start()
+
+    write.wait()
 
 
 def late_sums(use_x, acc, coords, pieces):
@@ -197,8 +211,9 @@
     return pl.pallas_call(
         late_kernel,
         in_specs=[SMEM] + [VMEM] * 7,
-        out_specs=[VMEM] * 4,
-        out_shape=[pltpu.VMEM((224, 512), F32)] + [pltpu.VMEM((224, 512), BF16)] * 3,
+        out_specs=[pl.BlockSpec(memory_space=pltpu.HBM)] + [VMEM] * 3,
+        out_shape=[pltpu.HBM((224, 512), F32)] + [pltpu.VMEM((224, 512), BF16)] * 3,
+        scratch_shapes=[pltpu.VMEM((224, 512), F32), pltpu.SemaphoreType.DMA],
         compiler_params=params(6),
     )(use_x.reshape(1), *args)
 
@@ -313,10 +328,13 @@
 
     first = [got[k] for got in (got_x, got_z) for k in (0, 2)]
     then = [got[k] for got in (got_x, got_z) for k in (1, 3)]
+    acc_m = early_sums(1 - c, first, (own, along[2]), ())[0]
+    acc_t, *moved = early_sums(c, first, (own, beyond[2]), (along[1], along[3]))
     sums = []
-    for use_x, coords, axis in ((1 - c, along, "z"), (c, beyond, "x")):
-        acc = early_sums(use_x, first, (own, coords[2]))
-        part = late_sums(use_x, acc, (coords[1], coords[3]), then)
+    for use_x, acc, coords, axis in (
+        (1 - c, acc_m, moved, "z"), (c, acc_t, (beyond[1], beyond[3]), "x")
+    ):
+        part = late_sums(use_x, acc, coords, then)
         sums.append([part[0]] + [cross(part[k], axis, k) for k in (1, 2, 3)])
     keep, give = combine(1 - jnp.bitwise_xor(c, yl), *sums)
     got = shift(give, "yl", 1)

time: 128 us -> 126 us (0.984)
  waiting for transfers between devices: 50.4 us -> 58.9 us
  local copies, waits for them, and re-layouts: 10.2 us -> 2.3 us
  Pallas kernels: 31 us -> 29 us
    ppermute x1, waiting for transfers between devices: 2.37 us -> 14.8 us  [step(): lax.ppermute(projector, ('yl', 'yh'), [(0, 3), (3, 0), (1, 2), (2, 1)])]
    unnamed x32 -> x28, local copies, waits for them, and re-layouts: 10.2 us -> 2.3 us
    ppermute x15, waiting for transfers between devices: 34.8 us -> 30.7 us  [shift(): return lax.ppermute(a, axis, [(i, (i + k) % n) for i in range(n)])]
    pallas_call x4, Pallas kernels: 12.2 us -> 9.2 us  [the longest x2 5.03 us: early_sums(): pl.pallas_call(early_kernel, in_specs=[SMEM] + [HBM] * 4 + [VMEM] * 2 + [...]
  transfers between devices with their start and end apart: 25 -> 25, of which waited for: 10 -> 12; matrix products, arithmetic and copies ran while one was open for 0% -> 0% of each run, Pallas kernels for 19% -> 18%
where the time goes in v10:
time: 126 us
  waiting for transfers between devices  58.9 us (47%)
  starting transfers between devices  34.7 us (28%)
  Pallas kernels  29 us (23%)
  local copies, waits for them, and re-layouts  2.3 us (2%)
    ppermute x15, waiting for transfers between devices, shift(): return lax.ppermute(a, axis, [(i, (i + k) % n) for i in range(n)])  30.7 us
    ppermute x9, starting transfers between devices, cross(): return lax.ppermute(a, AXES, pairs)  16.3 us
    ppermute x15, starting transfers between devices, shift(): return lax.ppermute(a, axis, [(i, (i + k) % n) for i in range(n)])  15.2 us
    ppermute x1, waiting for transfers between devices, step(): lax.ppermute(projector, ('yl', 'yh'), [(0, 3), (3, 0), (1, 2), (2, 1)])  14.8 us
    ppermute x9, waiting for transfers between devices, cross(): return lax.ppermute(a, AXES, pairs)  13.4 us
    pallas_call x1, Pallas kernels, front(): pl.pallas_call(front_kernel, grid_spec=pltpu.PrefetchScalarGridSpec(num_s...  8.99 us
    pallas_call x1, Pallas kernels, last_stage(): pl.pallas_call(last_kernel, in_specs=[SMEM] + [VMEM] * 7 + [HBM], out_spe...  6.65 us
    pallas_call x2, Pallas kernels, early_sums(): pl.pallas_call(early_kernel, in_specs=[SMEM] + [HBM] * 4 + [VMEM] * 2 + [...  5.03 us
  transfers between devices with their start and end apart: 25, of which 12 were waited for; matrix products, arithmetic and copies ran while one was open for 0% of the time, Pallas kernels for 18%

profile of v10, /device:TPU:0, one launch (start us, length us, event | category | flops | bytes accessed | tf_op | source)
XLA Modules:
  0.0 126.1 jit_solution(15425320382518417143)
XLA Ops:
  0.6 3.2 %collective-permute-start.23 = (bf16[2048,512]{1,0:T(8,128)(2,1)}, bf16[2048,512]{1,0:T(8,128)(2,1)}, u32[]{:S(2)}, u32[]{:S(2)}) collective-permute-start(bf16[2048,512]{1,0:T(8,128)(2,1)} %a.1), channel_id=1, source_target_pairs={{0,6},{6,0},{2,4},{4,2},{1,7},{7,1},{3,5},{5,3},{8,14},{14,8},{10,... | collective-permute-start | bytes 6291464 | tf_op jit(solution)/shard_map/ppermute | solution.py:325
  3.9 9.0 %front.1 = (f32[384,256]{1,0:T(8,128)S(1)}, f32[384,256]{1,0:T(8,128)S(1)}, bf16[4,224,384]{2,1,0:T(8,128)(2,1)S(1)}, bf16[4,224,384]{2,1,0:T(8,128)(2,1)S(1)}, ...) custom-call(s32[4]{0:T(128)S(1)} %pad_add_fusion.s_ref, ...), custom_call_target="tpu_custom_call" | custom-call | tf_op jit(solution)/shard_map/front/pallas_call | solution.py:77
  13.0 3.1 %collective-permute-start = (bf16[4,224,384]{2,1,0:T(8,128)(2,1)S(1)}, bf16[4,224,384]{2,1,0:T(8,128)(2,1)S(1)}, u32[]{:S(2)}, u32[]{:S(2)}) collective-permute-start(bf16[4,224,384]{2,1,0:T(8,128)(2,1)S(1)} %get-tuple-element.29), channel_id=1, source_target_pairs={{0,64},{32,96},{64,0},{96,32},{1,65},{33,97},{65,1},{97,33},{2,66}... | collective-permute-start | bytes 2064392 | tf_op jit(solution)/shard_map/ppermute | solution.py:24
  16.1 3.9 %collective-permute-start.1 = (bf16[4,224,384]{2,1,0:T(8,128)(2,1)S(1)}, bf16[4,224,384]{2,1,0:T(8,128)(2,1)S(1)}, u32[]{:S(2)}, u32[]{:S(2)}) collective-permute-start(bf16[4,224,384]{2,1,0:T(8,128)(2,1)S(1)} %get-tuple-element.31), channel_id=1, source_target_pairs={{0,16},{8,24},{16,0},{24,8},{1,17},{9,25},{17,1},{25,9},{2,18},{10... | collective-permute-start | bytes 2064392 | tf_op jit(solution)/shard_map/ppermute | solution.py:24
  21.9 6.5 %collective-permute-done.3 = bf16[384,256]{1,0:T(8,128)(2,1)S(1)} collective-permute-done((bf16[384,256]{1,0:T(8,128)(2,1)S(1)}, bf16[384,256]{1,0:T(8,128)(2,1)S(1)}, u32[]{:S(2)}, u32[]{:S(2)}) %collective-permute-start.3) | collective-permute-done | bytes 196640 | tf_op jit(solution)/shard_map/ppermute | solution.py:24
  29.5 2.9 %collective-permute-done.x2 = bf16[4,224,384]{2,1,0:T(8,128)(2,1)S(1)} collective-permute-done((bf16[4,224,384]{2,1,0:T(8,128)(2,1)S(1)}, bf16[4,224,384]{2,1,0:T(8,128)(2,1)S(1)}, u32[]{:S(2)}, u32[]{:S(2)}) %collective-permute-start) | collective-permute-done | bytes 688160 | tf_op jit(solution)/shard_map/ppermute | solution.py:24
  32.4 4.0 %collective-permute-done.1.z2 = bf16[4,224,384]{2,1,0:T(8,128)(2,1)S(1)} collective-permute-done((bf16[4,224,384]{2,1,0:T(8,128)(2,1)S(1)}, bf16[4,224,384]{2,1,0:T(8,128)(2,1)S(1)}, u32[]{:S(2)}, u32[]{:S(2)}) %collective-permute-start.1) | collective-permute-done | bytes 688160 | tf_op jit(solution)/shard_map/ppermute | solution.py:24
  36.3 2.8 %collective-permute-start.12 = (bf16[4,224,384]{2,1,0:T(8,128)(2,1)S(1)}, bf16[4,224,384]{2,1,0:T(8,128)(2,1)S(1)}, u32[]{:S(2)}, u32[]{:S(2)}) collective-permute-start(bf16[4,224,384]{2,1,0:T(8,128)(2,1)S(1)} %get-tuple-element.39), channel_id=1, source_target_pairs={{0,24},{8,0},{16,8},{24,16},{1,25},{9,1},{17,9},{25,17},{2,26},{10... | collective-permute-start | bytes 2064392 | tf_op jit(solution)/shard_map/ppermute | solution.py:24
  39.2 14.8 %collective-permute-done.23.w3 = bf16[2048,512]{1,0:T(8,128)(2,1)} collective-permute-done((bf16[2048,512]{1,0:T(8,128)(2,1)}, bf16[2048,512]{1,0:T(8,128)(2,1)}, u32[]{:S(2)}, u32[]{:S(2)}) %collective-permute-start.23) | collective-permute-done | bytes 2097184 | tf_op jit(solution)/shard_map/ppermute | solution.py:325
  54.6 3.1 %collective-permute-start.5 = (bf16[384,512]{1,0:T(8,128)(2,1)S(1)}, bf16[384,512]{1,0:T(8,128)(2,1)S(1)}, u32[]{:S(2)}, u32[]{:S(2)}) collective-permute-start(bf16[384,512]{1,0:T(8,128)(2,1)S(1)} %join.1.c0), channel_id=1, source_target_pairs={{0,64},{1,17},{2,66},{3,19},{4,68},{5,21},{6,70},{7,23},{8,72},{9,... | collective-permute-start | bytes 1179656 | tf_op jit(solution)/shard_map/ppermute | solution.py:36
  58.3 2.6 %collective-permute-start.8 = (bf16[384,512]{1,0:T(8,128)(2,1)S(1)}, bf16[384,512]{1,0:T(8,128)(2,1)S(1)}, u32[]{:S(2)}, u32[]{:S(2)}) collective-permute-start(bf16[384,512]{1,0:T(8,128)(2,1)S(1)} %join.1.c0), channel_id=1, source_target_pairs={{0,96},{1,25},{2,98},{3,27},{4,100},{5,29},{6,102},{7,31},{8,104},... | collective-permute-start | bytes 1179656 | tf_op jit(solution)/shard_map/ppermute | solution.py:36
  60.9 3.1 %collective-permute-done.5.c2 = bf16[384,512]{1,0:T(8,128)(2,1)S(1)} collective-permute-done((bf16[384,512]{1,0:T(8,128)(2,1)S(1)}, bf16[384,512]{1,0:T(8,128)(2,1)S(1)}, u32[]{:S(2)}, u32[]{:S(2)}) %collective-permute-start.5) | collective-permute-done | bytes 393248 | tf_op jit(solution)/shard_map/ppermute | solution.py:36
  64.1 4.1 %collective-permute-done.7.rest_0_ = bf16[384,512]{1,0:T(8,128)(2,1)S(1)} collective-permute-done((bf16[384,512]{1,0:T(8,128)(2,1)S(1)}, bf16[384,512]{1,0:T(8,128)(2,1)S(1)}, u32[]{:S(2)}, u32[]{:S(2)}) %collective-permute-start.7) | collective-permute-done | bytes 393248 | tf_op jit(solution)/shard_map/ppermute | solution.py:36
  70.5 2.5 %shard_map.86 = (f32[4,224,512]{2,1,0:T(8,128)S(1)}, bf16[384,512]{1,0:T(8,128)(2,1)S(1)}, bf16[384,512]{1,0:T(8,128)(2,1)S(1)}) custom-call(s32[1]{0:T(128)} %bitcast.2.s_ref, bf16[4,224,384]{2,1,0:T(8,128)(2,1)} %copy-done, bf16[4,224,384]{2,1,0:T(8,128)(2,1)} %copy-done.10, bf16[4,224,384]{2,1,0:T(8,128)(2,1)} %copy-done.1, ...), custom_call_target="tpu_custom_call" | custom-call | tf_op jit(solution)/shard_map/pallas_call | solution.py:178
  73.0 13.8 %collective-permute-done.9.x1 = bf16[4,224,384]{2,1,0:T(8,128)(2,1)S(1)} collective-permute-done((bf16[4,224,384]{2,1,0:T(8,128)(2,1)S(1)}, bf16[4,224,384]{2,1,0:T(8,128)(2,1)S(1)}, u32[]{:S(2)}, u32[]{:S(2)}) %collective-permute-start.9) | collective-permute-done | bytes 688160 | tf_op jit(solution)/shard_map/ppermute | solution.py:24
  90.8 2.5 %collective-permute-start.20 = (bf16[224,512]{1,0:T(8,128)(2,1)}, bf16[224,512]{1,0:T(8,128)(2,1)}, u32[]{:S(2)}, u32[]{:S(2)}) collective-permute-start(bf16[224,512]{1,0:T(8,128)(2,1)} %get-tuple-element.48), channel_id=1, source_target_pairs={{0,96},{1,25},{2,98},{3,27},{4,100},{5,29},{6,102},{7,31},{8,104},... | collective-permute-start | bytes 688136 | tf_op jit(solution)/shard_map/ppermute | solution.py:36
  93.3 2.5 %shard_map.85.acc = f32[4,224,512]{2,1,0:T(8,128)S(1)} custom-call(s32[1]{0:T(128)} %bitcast.5.s_ref, bf16[4,224,384]{2,1,0:T(8,128)(2,1)} %copy-done, bf16[4,224,384]{2,1,0:T(8,128)(2,1)} %copy-done.10, bf16[4,224,384]{2,1,0:T(8,128)(2,1)} %copy-done.1, bf16[4,224,384]{2,1,0:T(8,128)(2,1)} %copy-done.11, bf16[384,512]{1,0:T(8,128)(2,1)S(1)} %join.1.c0, ...), custom_call_target="tpu_custom_call" | custom-call | tf_op jit(solution)/shard_map/pallas_call | solution.py:178
  95.9 2.1 %shard_map.87 = (f32[224,512]{1,0:T(8,128)}, bf16[224,512]{1,0:T(8,128)(2,1)}, bf16[224,512]{1,0:T(8,128)(2,1)}, bf16[224,512]{1,0:T(8,128)(2,1)S(1)}) custom-call(s32[1]{0:T(128)} %bitcast.5.s_ref, f32[4,224,512]{2,1,0:T(8,128)S(1)} %shard_map.85.acc, bf16[384,512]{1,0:T(8,128)(2,1)S(1)} %copy-done.7, bf16[384,512]{1,0:T(8,128)(2,1)S(1)} %copy-done.9, ...), custom_call_target="tpu_custom_call" | custom-call | tf_op jit(solution)/shard_map/pallas_call | solution.py:211
  99.0 2.1 %collective-permute-start.13 = (bf16[224,512]{1,0:T(8,128)(2,1)}, bf16[224,512]{1,0:T(8,128)(2,1)S(1)}, u32[]{:S(2)}, u32[]{:S(2)}) collective-permute-start(bf16[224,512]{1,0:T(8,128)(2,1)} %get-tuple-element.41), channel_id=1, source_target_pairs={{0,8},{1,33},{2,10},{3,35},{4,12},{5,37},{6,14},{7,39},{8,16},{9,4... | collective-permute-start | bytes 688136 | tf_op jit(solution)/shard_map/ppermute | solution.py:36
  102.0 2.6 %collective-permute-start.15 = (bf16[224,512]{1,0:T(8,128)(2,1)S(1)}, bf16[224,512]{1,0:T(8,128)(2,1)S(1)}, u32[]{:S(2)}, u32[]{:S(2)}) collective-permute-start(bf16[224,512]{1,0:T(8,128)(2,1)S(1)} %get-tuple-element.43), channel_id=1, source_target_pairs={{0,24},{1,97},{2,26},{3,99},{4,28},{5,101},{6,30},{7,103},{8,0},{9... | collective-permute-start | bytes 688136 | tf_op jit(solution)/shard_map/ppermute | solution.py:36
  106.5 2.4 %collective-permute-done.14.m2 = bf16[224,512]{1,0:T(8,128)(2,1)S(1)} collective-permute-done((bf16[224,512]{1,0:T(8,128)(2,1)}, bf16[224,512]{1,0:T(8,128)(2,1)S(1)}, u32[]{:S(2)}, u32[]{:S(2)}) %collective-permute-start.14) | collective-permute-done | bytes 229408 | tf_op jit(solution)/shard_map/ppermute | solution.py:36
  113.6 2.2 %keep.1 = (bf16[2048,512]{1,0:T(8,128)(2,1)S(1)}, bf16[2048,512]{1,0:T(8,128)(2,1)S(1)}) custom-call(bf16[2048,512]{1,0:T(8,128)(2,1)} %a.1, bf16[2048,512]{1,0:T(8,128)(2,1)} %collective-permute-done.22.b), custom_call_target="tpu_custom_call" | custom-call | tf_op jit(solution)/shard_map/keep/pallas_call | solution.py:129
  115.8 3.5 %collective-permute-done.21.got = bf16[224,512]{1,0:T(8,128)(2,1)S(1)} collective-permute-done((bf16[224,512]{1,0:T(8,128)(2,1)S(1)}, bf16[224,512]{1,0:T(8,128)(2,1)S(1)}, u32[]{:S(2)}, u32[]{:S(2)}) %collective-permute-start.21) | collective-permute-done | bytes 229408 | tf_op jit(solution)/shard_map/ppermute | solution.py:24
  119.3 6.6 %last.1 = (f32[224,512]{1,0:T(8,128)}, f32[224,512]{1,0:T(8,128)}, bf16[224,8192]{1,0:T(8,128)(2,1)}) custom-call(s32[4]{0:T(128)S(1)} %pad_add_fusion.s_ref, f32[224,512]{1,0:T(8,128)S(1)} %get-tuple-element.49.mine, bf16[224,512]{1,0:T(8,128)(2,1)S(1)} %collective-permute-done.21.got, f32[224,512]{1,0:T(8,128)S(1)} %copy-done.4, f32[224,512]{1,0:T(8,128)S(1)} %copy-done.5, ...), custom_call_target="tpu_custom_call" | custom-call | tf_op jit(solution)/shard_map/last/pallas_call | solution.py:292
  (66 shorter events, 19.0 us)
Async XLA Ops:
  0.6 53.4 %collective-permute-start.23 = (bf16[2048,512]{1,0:T(8,128)(2,1)}, bf16[2048,512]{1,0:T(8,128)(2,1)}, u32[]{:S(2)}, u32[]{:S(2)}) collective-permute-start(bf16[2048,512]{1,0:T(8,128)(2,1)} %a.1), channel_id=1, source_target_pairs={{0,6},{6,0},{2,4},{4,2},{1,7},{7,1},{3,5},{5,3},{8,14},{14,8},{10,... | collective-permute-start | bytes 6291464 | tf_op jit(solution)/shard_map/ppermute | solution.py:325
  12.9 7.1 %collective-permute-start.2 = (f32[384,256]{1,0:T(8,128)S(1)}, f32[384,256]{1,0:T(8,128)S(1)}, u32[]{:S(2)}, u32[]{:S(2)}) collective-permute-start(f32[384,256]{1,0:T(8,128)S(1)} %get-tuple-element.33), channel_id=1, source_target_pairs={{0,1},{1,0},{2,3},{3,2},{4,5},{5,4},{6,7},{7,6},{8,9},{9,8},{10,11... | collective-permute-start | bytes 1179656 | tf_op jit(solution)/shard_map/ppermute | solution.py:24
  13.0 19.3 %collective-permute-start = (bf16[4,224,384]{2,1,0:T(8,128)(2,1)S(1)}, bf16[4,224,384]{2,1,0:T(8,128)(2,1)S(1)}, u32[]{:S(2)}, u32[]{:S(2)}) collective-permute-start(bf16[4,224,384]{2,1,0:T(8,128)(2,1)S(1)} %get-tuple-element.29), channel_id=1, source_target_pairs={{0,64},{32,96},{64,0},{96,32},{1,65},{33,97},{65,1},{97,33},{2,66}... | collective-permute-start | bytes 2064392 | tf_op jit(solution)/shard_map/ppermute | solution.py:24
  16.1 20.2 %collective-permute-start.1 = (bf16[4,224,384]{2,1,0:T(8,128)(2,1)S(1)}, bf16[4,224,384]{2,1,0:T(8,128)(2,1)S(1)}, u32[]{:S(2)}, u32[]{:S(2)}) collective-permute-start(bf16[4,224,384]{2,1,0:T(8,128)(2,1)S(1)} %get-tuple-element.31), channel_id=1, source_target_pairs={{0,16},{8,24},{16,0},{24,8},{1,17},{9,25},{17,1},{25,9},{2,18},{10... | collective-permute-start | bytes 2064392 | tf_op jit(solution)/shard_map/ppermute | solution.py:24
  20.1 8.3 %collective-permute-start.3 = (bf16[384,256]{1,0:T(8,128)(2,1)S(1)}, bf16[384,256]{1,0:T(8,128)(2,1)S(1)}, u32[]{:S(2)}, u32[]{:S(2)}) collective-permute-start(bf16[384,256]{1,0:T(8,128)(2,1)S(1)} %get-tuple-element.53), channel_id=1, source_target_pairs={{0,2},{2,0},{1,3},{3,1},{4,6},{6,4},{5,7},{7,5},{8,10},{10,8},{9,1... | collective-permute-start | bytes 589832 | tf_op jit(solution)/shard_map/ppermute | solution.py:24
  20.8 33.8 %collective-permute-start.10 = (bf16[4,224,384]{2,1,0:T(8,128)(2,1)S(1)}, bf16[4,224,384]{2,1,0:T(8,128)(2,1)S(1)}, u32[]{:S(2)}, u32[]{:S(2)}) collective-permute-start(bf16[4,224,384]{2,1,0:T(8,128)(2,1)S(1)} %get-tuple-element.37), channel_id=1, source_target_pairs={{0,96},{32,0},{64,32},{96,64},{1,97},{33,1},{65,33},{97,65},{2,98}... | collective-permute-start | bytes 2064392 | tf_op jit(solution)/shard_map/ppermute | solution.py:24
  28.4 29.3 %collective-permute-start.11 = (bf16[4,224,384]{2,1,0:T(8,128)(2,1)S(1)}, bf16[4,224,384]{2,1,0:T(8,128)(2,1)S(1)}, u32[]{:S(2)}, u32[]{:S(2)}) collective-permute-start(bf16[4,224,384]{2,1,0:T(8,128)(2,1)S(1)} %get-tuple-element.38), channel_id=1, source_target_pairs={{0,8},{8,16},{16,24},{24,0},{1,9},{9,17},{17,25},{25,1},{2,10},{10... | collective-permute-start | bytes 2064392 | tf_op jit(solution)/shard_map/ppermute | solution.py:24
  32.4 6.8 %collective-permute-start.4 = (bf16[384,256]{1,0:T(8,128)(2,1)S(1)}, bf16[384,256]{1,0:T(8,128)(2,1)S(1)}, u32[]{:S(2)}, u32[]{:S(2)}) collective-permute-start(bf16[384,256]{1,0:T(8,128)(2,1)S(1)} %add_convert_fusion.half), channel_id=1, source_target_pairs={{0,1},{1,0},{2,3},{3,2},{4,5},{5,4},{6,7},{7,6},{8,9},{9,8},{10,11... | collective-permute-start | bytes 589832 | tf_op jit(solution)/shard_map/ppermute | solution.py:24
  36.3 22.0 %collective-permute-start.12 = (bf16[4,224,384]{2,1,0:T(8,128)(2,1)S(1)}, bf16[4,224,384]{2,1,0:T(8,128)(2,1)S(1)}, u32[]{:S(2)}, u32[]{:S(2)}) collective-permute-start(bf16[4,224,384]{2,1,0:T(8,128)(2,1)S(1)} %get-tuple-element.39), channel_id=1, source_target_pairs={{0,24},{8,0},{16,8},{24,16},{1,25},{9,1},{17,9},{25,17},{2,26},{10... | collective-permute-start | bytes 2064392 | tf_op jit(solution)/shard_map/ppermute | solution.py:24
  39.2 74.4 %collective-permute-start.22 = (bf16[2048,512]{1,0:T(8,128)(2,1)}, bf16[2048,512]{1,0:T(8,128)(2,1)}, u32[]{:S(2)}, u32[]{:S(2)}) collective-permute-start(bf16[2048,512]{1,0:T(8,128)(2,1)} %a.1), channel_id=1, source_target_pairs={{0,1},{1,0},{2,3},{3,2},{4,5},{5,4},{6,7},{7,6},{8,9},{9,8},{10,11... | collective-permute-start | bytes 6291464 | tf_op jit(solution)/shard_map/ppermute | solution.py:24
  54.0 65.3 %collective-permute-start.24 = (bf16[2048,512]{1,0:T(8,128)(2,1)}, bf16[2048,512]{1,0:T(8,128)(2,1)}, u32[]{:S(2)}, u32[]{:S(2)}) collective-permute-start(bf16[2048,512]{1,0:T(8,128)(2,1)} %collective-permute-done.23.w3), channel_id=1, source_target_pairs={{0,1},{1,0},{2,3},{3,2},{4,5},{5,4},{6,7},{7,6},{8,9},{9,8},{10,11... | collective-permute-start | bytes 6291464 | tf_op jit(solution)/shard_map/ppermute | solution.py:24
  54.6 9.5 %collective-permute-start.5 = (bf16[384,512]{1,0:T(8,128)(2,1)S(1)}, bf16[384,512]{1,0:T(8,128)(2,1)S(1)}, u32[]{:S(2)}, u32[]{:S(2)}) collective-permute-start(bf16[384,512]{1,0:T(8,128)(2,1)S(1)} %join.1.c0), channel_id=1, source_target_pairs={{0,64},{1,17},{2,66},{3,19},{4,68},{5,21},{6,70},{7,23},{8,72},{9,... | collective-permute-start | bytes 1179656 | tf_op jit(solution)/shard_map/ppermute | solution.py:36
  57.7 10.5 %collective-permute-start.7 = (bf16[384,512]{1,0:T(8,128)(2,1)S(1)}, bf16[384,512]{1,0:T(8,128)(2,1)S(1)}, u32[]{:S(2)}, u32[]{:S(2)}) collective-permute-start(bf16[384,512]{1,0:T(8,128)(2,1)S(1)} %join.1.c0), channel_id=1, source_target_pairs={{0,32},{1,9},{2,34},{3,11},{4,36},{5,13},{6,38},{7,15},{8,40},{9,1... | collective-permute-start | bytes 1179656 | tf_op jit(solution)/shard_map/ppermute | solution.py:36
  58.3 11.4 %collective-permute-start.8 = (bf16[384,512]{1,0:T(8,128)(2,1)S(1)}, bf16[384,512]{1,0:T(8,128)(2,1)S(1)}, u32[]{:S(2)}, u32[]{:S(2)}) collective-permute-start(bf16[384,512]{1,0:T(8,128)(2,1)S(1)} %join.1.c0), channel_id=1, source_target_pairs={{0,96},{1,25},{2,98},{3,27},{4,100},{5,29},{6,102},{7,31},{8,104},... | collective-permute-start | bytes 1179656 | tf_op jit(solution)/shard_map/ppermute | solution.py:36
  68.2 18.7 %collective-permute-start.9 = (bf16[4,224,384]{2,1,0:T(8,128)(2,1)S(1)}, bf16[4,224,384]{2,1,0:T(8,128)(2,1)S(1)}, u32[]{:S(2)}, u32[]{:S(2)}) collective-permute-start(bf16[4,224,384]{2,1,0:T(8,128)(2,1)S(1)} %get-tuple-element.36), channel_id=1, source_target_pairs={{0,32},{32,64},{64,96},{96,0},{1,33},{33,65},{65,97},{97,1},{2,34}... | collective-permute-start | bytes 2064392 | tf_op jit(solution)/shard_map/ppermute | solution.py:24
  69.7 17.1 %collective-permute-start.16 = (bf16[384,512]{1,0:T(8,128)(2,1)S(1)}, bf16[384,512]{1,0:T(8,128)(2,1)S(1)}, u32[]{:S(2)}, u32[]{:S(2)}) collective-permute-start(bf16[384,512]{1,0:T(8,128)(2,1)S(1)} %collective-permute-done.7.rest_0_), channel_id=1, source_target_pairs={{0,1},{1,0},{2,3},{3,2},{4,5},{5,4},{6,7},{7,6},{8,9},{9,8},{10,11... | collective-permute-start | bytes 1179656 | tf_op jit(solution)/shard_map/ppermute | solution.py:24
  69.8 17.1 %collective-permute-start.17 = (bf16[384,512]{1,0:T(8,128)(2,1)S(1)}, bf16[384,512]{1,0:T(8,128)(2,1)S(1)}, u32[]{:S(2)}, u32[]{:S(2)}) collective-permute-start(bf16[384,512]{1,0:T(8,128)(2,1)S(1)} %collective-permute-done.8.rest_1_), channel_id=1, source_target_pairs={{0,1},{1,0},{2,3},{3,2},{4,5},{5,4},{6,7},{7,6},{8,9},{9,8},{10,11... | collective-permute-start | bytes 1179656 | tf_op jit(solution)/shard_map/ppermute | solution.py:24
  88.9 10.1 %collective-permute-start.18 = (bf16[224,512]{1,0:T(8,128)(2,1)}, bf16[224,512]{1,0:T(8,128)(2,1)}, u32[]{:S(2)}, u32[]{:S(2)}) collective-permute-start(bf16[224,512]{1,0:T(8,128)(2,1)} %get-tuple-element.46), channel_id=1, source_target_pairs={{0,32},{1,9},{2,34},{3,11},{4,36},{5,13},{6,38},{7,15},{8,40},{9,1... | collective-permute-start | bytes 688136 | tf_op jit(solution)/shard_map/ppermute | solution.py:36
  89.1 11.9 %collective-permute-start.19 = (bf16[224,512]{1,0:T(8,128)(2,1)}, bf16[224,512]{1,0:T(8,128)(2,1)}, u32[]{:S(2)}, u32[]{:S(2)}) collective-permute-start(bf16[224,512]{1,0:T(8,128)(2,1)} %get-tuple-element.47), channel_id=1, source_target_pairs={{0,64},{1,17},{2,66},{3,19},{4,68},{5,21},{6,70},{7,23},{8,72},{9,... | collective-permute-start | bytes 688136 | tf_op jit(solution)/shard_map/ppermute | solution.py:36
  90.8 11.2 %collective-permute-start.20 = (bf16[224,512]{1,0:T(8,128)(2,1)}, bf16[224,512]{1,0:T(8,128)(2,1)}, u32[]{:S(2)}, u32[]{:S(2)}) collective-permute-start(bf16[224,512]{1,0:T(8,128)(2,1)} %get-tuple-element.48), channel_id=1, source_target_pairs={{0,96},{1,25},{2,98},{3,27},{4,100},{5,29},{6,102},{7,31},{8,104},... | collective-permute-start | bytes 688136 | tf_op jit(solution)/shard_map/ppermute | solution.py:36
  99.0 7.5 %collective-permute-start.13 = (bf16[224,512]{1,0:T(8,128)(2,1)}, bf16[224,512]{1,0:T(8,128)(2,1)S(1)}, u32[]{:S(2)}, u32[]{:S(2)}) collective-permute-start(bf16[224,512]{1,0:T(8,128)(2,1)} %get-tuple-element.41), channel_id=1, source_target_pairs={{0,8},{1,33},{2,10},{3,35},{4,12},{5,37},{6,14},{7,39},{8,16},{9,4... | collective-permute-start | bytes 688136 | tf_op jit(solution)/shard_map/ppermute | solution.py:36
  101.1 7.8 %collective-permute-start.14 = (bf16[224,512]{1,0:T(8,128)(2,1)}, bf16[224,512]{1,0:T(8,128)(2,1)S(1)}, u32[]{:S(2)}, u32[]{:S(2)}) collective-permute-start(bf16[224,512]{1,0:T(8,128)(2,1)} %get-tuple-element.42), channel_id=1, source_target_pairs={{0,16},{1,65},{2,18},{3,67},{4,20},{5,69},{6,22},{7,71},{8,24},{9,... | collective-permute-start | bytes 688136 | tf_op jit(solution)/shard_map/ppermute | solution.py:36
  102.0 7.8 %collective-permute-start.15 = (bf16[224,512]{1,0:T(8,128)(2,1)S(1)}, bf16[224,512]{1,0:T(8,128)(2,1)S(1)}, u32[]{:S(2)}, u32[]{:S(2)}) collective-permute-start(bf16[224,512]{1,0:T(8,128)(2,1)S(1)} %get-tuple-element.43), channel_id=1, source_target_pairs={{0,24},{1,97},{2,26},{3,99},{4,28},{5,101},{6,30},{7,103},{8,0},{9... | collective-permute-start | bytes 688136 | tf_op jit(solution)/shard_map/ppermute | solution.py:36
  113.2 6.1 %collective-permute-start.21 = (bf16[224,512]{1,0:T(8,128)(2,1)S(1)}, bf16[224,512]{1,0:T(8,128)(2,1)S(1)}, u32[]{:S(2)}, u32[]{:S(2)}) collective-permute-start(bf16[224,512]{1,0:T(8,128)(2,1)S(1)} %get-tuple-element.50), channel_id=1, source_target_pairs={{0,4},{4,0},{1,5},{5,1},{2,6},{6,2},{3,7},{7,3},{8,12},{12,8},{9,1... | collective-permute-start | bytes 688136 | tf_op jit(solution)/shard_map/ppermute | solution.py:24
  (15 other events, 246.4 us)
